TPU v7x, 32 devices: a whole 2x2x4 slice. The times are simulated.
32 devices in a mesh: pb: 32 (over z, y, x, core).
Axes of the slice: x: 2, y: 2, z: 4, core: 2. Of those that a mesh axis runs over, the one named last changes fastest.
Arguments:
- densities: bfloat16 [32, 32, 32, 1200], P(None, 'pb'), may hold values from -1.1953125 to 1.1953125
- screening: bfloat16 [32, 1200, 1200], P('pb'), may hold values from -0.1875 to 0.1875
- live: int32 [32, 32], P(None, 'pb'), may hold values 0 or 1
Outputs:
- kernel: bfloat16 [32, 32, 256], P(None, 'pb')
All inputs are finite; a program needn't handle non-finite values. No bound on the sum of `live` on one device may be relied on, other than what follows from the above.
Results may differ from a plain program's by a relative error of at most 0.0049.
Values may be sent and summed in bfloat16 or wider, within the bound.
No kernel may reach another device: no remote copies, remote signals or barrier semaphores. Data moves between devices by JAX's collectives and lax.ppermute only.
A program may use at most 128 MiB of HBM per device.

v0:
```python
import jax
import jax.numpy as jnp
from jax import lax
from jax.experimental import pallas as pl
from jax.experimental.pallas import tpu as pltpu
from jax.sharding import PartitionSpec as P


BF16, F32 = jnp.bfloat16, jnp.float32
LANES = 128
HALF = LANES // 2
COLS = 256


VM = pl.BlockSpec(memory_space=pltpu.VMEM)
SM = pl.BlockSpec(memory_space=pltpu.SMEM)
ANY = pl.BlockSpec(memory_space=pl.ANY)
HBM = pl.BlockSpec(memory_space=pltpu.HBM)


def split(devices):
    outer = 2 ** ((devices.bit_length() - 1) // 2)
    return outer, devices // outer


class Sizes:
    def __init__(self, shape, devices):
        self.q, _, both, self.ng = shape
        self.pairs = both // 2
        self.full, self.tail = divmod(self.ng, LANES)
        self.rows = self.pairs * self.full + (self.pairs // 2 if self.tail else 0)
        self.wide = LANES * (self.full + (1 if self.tail else 0))
        self.devices = devices
        self.outer, self.inner = split(devices)

    def fits(self):
        power = self.devices & (self.devices - 1) == 0
        return power and self.inner >= 4 and self.pairs == 16 and 0 < self.tail <= HALF


def call(kernel, outs, ins, specs, scratch=(), flops=0, moved=0, after=()):
    k, a = len(ins), len(after)

    def body(*refs):
        kernel(*refs[:k], *refs[k + a :])

    return pallas(body, outs, specs, a, scratch, flops, moved)(*ins, *after)


def pallas(body, outs, specs, a, scratch, flops, moved):
    return pl.pallas_call(
        body,
        out_shape=tuple(outs),
        in_specs=[*specs, *[ANY] * a],
        out_specs=tuple(pl.BlockSpec(memory_space=pltpu.VMEM) for _ in outs),
        scratch_shapes=list(scratch),
        compiler_params=pltpu.CompilerParams(vmem_limit_bytes=24 << 20),
        cost_estimate=pl.CostEstimate(flops=flops, bytes_accessed=moved, transcendentals=0),
    )


def pack(s, read, dst, b, base):
    n = s.pairs
    for j in range(s.full):
        dst[b, base + n * j : base + n * (j + 1), :] = read(LANES * j, LANES * (j + 1))
    last = read(LANES * s.full, s.wide).astype(F32)
    lane = lax.broadcasted_iota(jnp.int32, (n // 2, LANES), 1)
    folded = jnp.where(lane < HALF, last[: n // 2], pltpu.roll(last[n // 2 :], HALF, 1))
    dst[b, base + n * s.full : base + s.rows, :] = folded.astype(BF16)


def unpack(s, src, b, base, dst, row):
    n = s.pairs
    for j in range(s.full):
        dst[row : row + n, LANES * j : LANES * (j + 1)] = src[b, base + n * j : base + n * (j + 1), :]
    folded = src[b, base + n * s.full : base + s.rows, :].astype(F32)
    last = jnp.concatenate([folded, pltpu.roll(folded, HALF, 1)], axis=0).astype(BF16)
    dst[row : row + n, LANES * s.full : s.ng] = last[:, : s.tail]


def nt(x, y):
    return lax.dot_general(x, y, (((1,), (1,)), ((), ())), preferred_element_type=F32)


def screen(s, v, w_ref, out):
    for lo in range(0, s.ng, COLS):
        hi = min(lo + COLS, s.ng)
        out[:, lo:hi] = nt(v[...], w_ref[0, lo:hi, :]).astype(BF16)


def rows_of_pairs(s, me, offsets, c, sc):
    n, count = s.pairs, len(offsets) * s.pairs
    full = nt(c, sc)
    r = lax.broadcasted_iota(jnp.int32, (count, count), 0)
    k = lax.broadcasted_iota(jnp.int32, (count, count), 1)
    own = jnp.where(r // n == k // n, full, 0.0).astype(BF16)
    e = lax.broadcasted_iota(jnp.int32, (count, n * n), 0)
    f = lax.broadcasted_iota(jnp.int32, (count, n * n), 1)
    spread = jnp.where(e % n == f % n, 1.0, 0.0).astype(BF16)
    x = jnp.dot(own, spread, preferred_element_type=F32)
    x = jnp.where(f // n == e % n, x, 0.0).astype(BF16)
    i = lax.broadcasted_iota(jnp.int32, (s.devices, count), 1) // n
    at = lax.broadcasted_iota(jnp.int32, (s.devices, count), 0)
    target = jnp.zeros_like(i)
    for index, m in enumerate(offsets):
        target = jnp.where(i == index, m, target)
    place = jnp.where(at == (target ^ me), 1.0, 0.0).astype(BF16)
    return jnp.dot(place, x, preferred_element_type=F32)


def gather(s, me, dens, offsets, half, buf, sem):
    lo, n = (0, 2 * s.pairs) if half is None else (half * s.pairs, s.pairs)
    copies = [
        pltpu.make_async_copy(dens.at[me ^ m, 0, pl.ds(lo, n), :], buf.at[i], sem.at[i])
        for i, m in enumerate(offsets)
    ]
    for c in copies:
        c.start()
    return copies


def reader(s, buf, i, row, edge):
    def read(lo, hi):
        if hi <= s.ng:
            return buf[i, row : row + s.pairs, lo:hi]
        edge[i, :, : s.tail] = buf[i, row : row + s.pairs, lo : s.ng]
        return edge[i]

    return read


def fast(s, densities, weights, live):
    me_arr = lax.axis_index("pb").astype(jnp.int32).reshape(1)
    O, I, N, n = s.outer, s.inner, s.devices, s.pairs
    inner = sorted(range(I), key=lambda p: (bin(p).count("1"), p))
    back, there = inner[: I // 2], inner[I // 2 :]
    groups = [there[: len(there) // 2], there[len(there) // 2 :]]
    h = len(back)
    far = list(range(O - 1, 0, -1))
    block = n * s.ng

    def sds(*shape):
        return jax.ShapeDtypeStruct(shape, BF16)

    def hop(x, m):
        return lax.ppermute(x, "pb", [(d, d ^ m) for d in range(N)])

    densities = pltpu.with_memory_space_constraint(densities, pltpu.HBM)

    def take_v(me_ref, dens, *refs):
        outs, (buf, edge, sem) = refs[:O], refs[O:]
        me = me_ref[0]
        offs = [dz * I + p for dz in [*far, 0] for p in back]
        copies = gather(s, me, dens, offs, 1, buf, sem)
        for i, c in enumerate(copies):
            c.wait()
            dz, j = offs[i] // I, i % h
            pack(s, reader(s, buf, i, 0, edge), outs[dz], j, 0)

    vb = call(
        take_v,
        [sds(h, s.rows, LANES)] * O,
        (me_arr, densities),
        [SM, HBM],
        [pltpu.VMEM((O * h, n, s.ng), BF16), pltpu.VMEM((O * h, n, LANES), BF16), pltpu.SemaphoreType.DMA((O * h,))],
        moved=4 * O * h * block,
    )
    vz = {dz: hop(vb[dz], dz * I) for dz in far}

    def take_cv(index):
        group = groups[index]
        g = len(group)

        def kernel(me_ref, dens, *refs):
            outs, (buf, edge, edge2, sem) = refs[:g], refs[g:]
            me = me_ref[0]
            offs = [dz * I + p for p in group for dz in range(O)]
            copies = gather(s, me, dens, offs, None, buf, sem)
            for i, c in enumerate(copies):
                c.wait()
                pack(s, reader(s, buf, i, 0, edge), outs[i // O], i % O, 0)
                pack(s, reader(s, buf, i, n, edge2), outs[i // O], i % O, s.rows)

        k = O * g
        return call(
            kernel,
            [sds(O, 2 * s.rows, LANES)] * g,
            (me_arr, densities),
            [SM, HBM],
            [
                pltpu.VMEM((k, 2 * n, s.ng), BF16),
                pltpu.VMEM((k, n, LANES), BF16),
                pltpu.VMEM((k, n, LANES), BF16),
                pltpu.SemaphoreType.DMA((k,)),
            ],
            moved=8 * k * block,
            after=(vb[0],),
        )

    def regroup(picks, count, parts, ins, after=()):
        def kernel(*refs):
            src, outs = refs[: len(ins)], refs[len(ins) :]
            for o, pick in zip(outs, picks):
                for i, (a, b) in enumerate(pick):
                    o[i] = src[a][b]

        return call(
            kernel,
            [sds(count, parts * s.rows, LANES)] * len(picks),
            ins,
            [VM] * len(ins),
            moved=4 * len(picks) * count * parts * block,
            after=after,
        )

    early, late = [0, *range(1, O // 2)], list(range(O - 1, O // 2 - 1, -1))

    def take_c(me_ref, dens, *refs):
        outs, sems = refs[:2], refs[2]
        copies = []
        for t, zs in enumerate((early, late)):
            offs = [dz * I + p for dz in zs for p in back]
            copies += gather(s, me_ref[0], dens, offs, 0, outs[t], sems.at[t])
        for c in copies:
            c.wait()

    def onward(index, after):
        near, group = nears[index], groups[index]
        g = len(group)
        parts = regroup([[(j, dz) for j in range(g)] for dz in [0, *far]], g, 2, near, after)
        return [(0, parts[0])] + [(dz, hop(x, dz * I)) for dz, x in zip(far, parts[1:])]

    sents = [take_cv(index) for index in range(2)]
    nears = [[hop(x, p) for x, p in zip(sent, group)] for sent, group in zip(sents, groups)]
    own_c = call(
        take_c,
        [sds(O // 2 * h, n, s.ng)] * 2,
        (me_arr, densities),
        [SM, HBM],
        [pltpu.SemaphoreType.DMA((2, O // 2 * h))],
        moved=4 * O * h * block,
        after=(sents[1][0],),
    )
    arrived = [onward(0, (own_c[0],))]

    zs = [vb[0]] + [vz[dz] for dz in far]
    order = [0, *far]
    pieces = regroup([[(a, j) for a in range(O)] for j in range(h)], O, 1, zs, (arrived[0][0][1],))
    arrived.append(onward(1, (pieces[0],)))
    own_v, send_v = pieces[0], pieces[1:]
    vin = [own_v] + [hop(x, p) for x, p in zip(send_v, back[1:])]

    def screen_back(*refs):
        src, w_ref, outs, (v, sc) = refs[:h], refs[h], refs[h + 1 : 2 * h + 1], refs[2 * h + 1 :]
        for j in range(h):
            for a in range(O):
                unpack(s, src[j], a, 0, v, n * (j * O + a))
        screen(s, v, w_ref, sc)
        for j in range(h):
            for a in range(O):
                row = n * (j * O + a)
                pack(s, lambda lo, hi, row=row: sc[row : row + n, lo:hi], outs[j], a, 0)

    m_rows = n * h * O
    sb = call(
        screen_back,
        [sds(O, s.rows, LANES)] * h,
        (*vin, weights),
        [VM] * (h + 1),
        [pltpu.VMEM((m_rows, s.ng), BF16), pltpu.VMEM((m_rows, s.wide), BF16)],
        flops=2 * m_rows * s.ng * s.ng,
        moved=2 * s.ng * s.ng,
        after=(arrived[1][0][1],),
    )
    sin = [sb[0]] + [hop(x, p) for x, p in zip(sb[1:], back[1:])]
    out_z = regroup([[(j, a) for j in range(h)] for a in range(O)], h, 1, sin)
    sz = [out_z[0]] + [hop(x, dz * I) for dz, x in zip(far, out_z[1:])]

    def blocks_at_owner(group, index, prior):
        g = len(group)
        got = arrived[index]
        offs = [dz * I + p for dz, _ in got for p in group]
        count = len(offs)
        last = prior is not None

        def kernel(me_ref, *refs):
            src, w_ref = refs[:O], refs[O]
            rest = refs[O + 1 :]
            if last:
                before, rest = rest[0], rest[1:]
            out, c, v, sc = rest
            for a in range(O):
                for j in range(g):
                    unpack(s, src[a], j, 0, c, n * (a * g + j))
                    unpack(s, src[a], j, s.rows, v, n * (a * g + j))
            screen(s, v, w_ref, sc)
            r = rows_of_pairs(s, me_ref[0], offs, c[...], sc[:, : s.ng])
            if last:
                r = r + before[...]
                for t in range(n * n // LANES):
                    out[:, t, :] = r[:, LANES * t : LANES * (t + 1)].astype(BF16)
            else:
                out[...] = r

        shape = (N, n * n // LANES, LANES) if last else (N, n * n)
        return call(
            kernel,
            [jax.ShapeDtypeStruct(shape, BF16 if last else F32)],
            (me_arr, *[x for _, x in got], weights) + ((prior,) if last else ()),
            [SM] + [VM] * (O + 1 + (1 if last else 0)),
            [
                pltpu.VMEM((n * count, s.ng), BF16),
                pltpu.VMEM((n * count, s.ng), BF16),
                pltpu.VMEM((n * count, s.wide), BF16),
            ],
            flops=2 * n * count * s.ng * s.ng,
            moved=2 * s.ng * s.ng,
            after=(out_z[0],),
        )[0]

    sums = None
    for index, group in enumerate(groups):
        sums = blocks_at_owner(group, index, sums)
    returned = lax.all_to_all(sums, "pb", split_axis=0, concat_axis=0, tiled=True)

    def finish(part, zs, first):
        count = len(zs) * h
        offs = [dz * I + p for dz in zs for p in back]

        def kernel(me_ref, c_ref, *refs):
            src, (before, live_ref, out, c, sc) = refs[: len(zs)], refs[len(zs) :]
            for a in range(len(zs)):
                for j in range(h):
                    row = n * (a * h + j)
                    c[row : row + n, :] = c_ref[a * h + j]
                    unpack(s, src[a], j, 0, sc, row)
            r = rows_of_pairs(s, me_ref[0], offs, c[...], sc[...])
            if part == 0:
                r = r + jnp.concatenate([before[:, t, :].astype(F32) for t in range(n * n // LANES)], axis=1)
                out[...] = r
            else:
                out[...] = ((r + before[...]) * live_ref[...].astype(F32)).astype(BF16)

        return call(
            kernel,
            [jax.ShapeDtypeStruct((N, n * n), F32 if part == 0 else BF16)],
            (me_arr, own_c[part], *[sz[order.index(dz)] for dz in zs], first, live),
            [SM] + [VM] * (3 + len(zs)),
            [pltpu.VMEM((n * count, s.ng), BF16), pltpu.VMEM((n * count, s.ng), BF16)],
            flops=2 * n * count * s.ng * n,
            moved=4 * n * count * s.ng,
        )[0]

    return finish(1, late, finish(0, early, returned))[:, None, :]


def plain(densities, screening, live):
    pairs = densities.shape[2] // 2
    arrived = lax.all_to_all(densities, "pb", split_axis=0, concat_axis=0, tiled=True)
    screened = jnp.einsum(
        "nkbh,gh->nkbg", arrived[:, :, pairs:, :], screening[0], preferred_element_type=F32
    ).astype(BF16)
    blocks = jnp.einsum("nkag,nkbg->nkab", arrived[:, :, :pairs, :], screened, preferred_element_type=F32)
    blocks = blocks.reshape(blocks.shape[0], blocks.shape[1], -1).astype(BF16)
    result = lax.all_to_all(blocks, "pb", split_axis=0, concat_axis=0, tiled=True)
    return result * live.astype(BF16)[:, :, None]


def solution(mesh):
    devices = mesh.shape["pb"]

    def on_device(densities, screening, live):
        s = Sizes(densities.shape, devices)
        if s.q == devices and s.fits():
            return fast(s, densities, screening, live)
        return plain(densities, screening, live)

    in_specs = (P(None, "pb", None, None), P("pb", None, None), P(None, "pb"))
    return jax.shard_map(
        on_device, mesh=mesh, in_specs=in_specs, out_specs=P(None, "pb", None), check_vma=False
    )
```

profile of v0, /device:TPU:0, one launch (start us, length us, event | category | flops | bytes accessed | tf_op | source)
XLA Modules:
  0.0 80.1 jit_solution(10817455273345747097)
XLA Ops:
  0.0 2.3 %shard_map.37 = (bf16[4,152,128]{2,1,0:T(8,128)(2,1)S(1)}, bf16[4,152,128]{2,1,0:T(8,128)(2,1)S(1)}, bf16[4,152,128]{2,1,0:T(8,128)(2,1)S(1)}, bf16[4,152,128]{2,1,0:T(8,128)(2,1)S(1)}) custom-call(s32[1]{0:T(128)} %bitcast.refs_0_, bf16[32,1,32,1200]{3,2,1,0:T(8,128)(2,1)} %refs_1_.7), custom_call_target="tpu_custom_call" | custom-call | bytes 1228800 | tf_op jit(solution)/shard_map/pallas_call | solution.py:47
  2.3 1.7 %shard_map.40 = (bf16[4,304,128]{2,1,0:T(8,128)(2,1)S(1)}, bf16[4,304,128]{2,1,0:T(8,128)(2,1)S(1)}) custom-call(s32[1]{0:T(128)} %bitcast.refs_0_, bf16[32,1,32,1200]{3,2,1,0:T(8,128)(2,1)} %refs_1_.7, bf16[4,152,128]{2,1,0:T(8,128)(2,1)S(1)} %get-tuple-element.35.refs_2_.refs_0_), custom_call_target="tpu_custom_call" | custom-call | bytes 1228800 | tf_op jit(solution)/shard_map/pallas_call | solution.py:47
  4.0 2.5 %collective-permute-start.3 = (bf16[4,304,128]{2,1,0:T(8,128)(2,1)S(1)}, bf16[4,304,128]{2,1,0:T(8,128)(2,1)S(1)}, u32[]{:S(2)}, u32[]{:S(2)}) collective-permute-start(bf16[4,304,128]{2,1,0:T(8,128)(2,1)S(1)} %get-tuple-element.41), channel_id=1, source_target_pairs={{0,3},{1,2},{2,1},{3,0},{4,7},{5,6},{6,5},{7,4},{8,11},{9,10},{10,... | collective-permute-start | bytes 933896 | tf_op jit(solution)/shard_map/ppermute | solution.py:146
  6.5 1.8 %collective-permute-start.4 = (bf16[4,304,128]{2,1,0:T(8,128)(2,1)S(1)}, bf16[4,304,128]{2,1,0:T(8,128)(2,1)S(1)}, u32[]{:S(2)}, u32[]{:S(2)}) collective-permute-start(bf16[4,304,128]{2,1,0:T(8,128)(2,1)S(1)} %get-tuple-element.42), channel_id=1, source_target_pairs={{0,5},{1,4},{2,7},{3,6},{4,1},{5,0},{6,3},{7,2},{8,13},{9,12},{10,... | collective-permute-start | bytes 933896 | tf_op jit(solution)/shard_map/ppermute | solution.py:146
  8.3 3.6 %collective-permute-start = (bf16[4,152,128]{2,1,0:T(8,128)(2,1)S(1)}, bf16[4,152,128]{2,1,0:T(8,128)(2,1)S(1)}, u32[]{:S(2)}, u32[]{:S(2)}) collective-permute-start(bf16[4,152,128]{2,1,0:T(8,128)(2,1)S(1)} %get-tuple-element.38), channel_id=1, source_target_pairs={{0,24},{1,25},{2,26},{3,27},{4,28},{5,29},{6,30},{7,31},{8,16},{9,... | collective-permute-start | bytes 466952 | tf_op jit(solution)/shard_map/ppermute | solution.py:146
  11.9 0.8 collective-permute-start.2
  12.7 1.7 %shard_map.38 = (bf16[4,304,128]{2,1,0:T(8,128)(2,1)S(1)}, bf16[4,304,128]{2,1,0:T(8,128)(2,1)S(1)}) custom-call(s32[1]{0:T(128)} %bitcast.refs_0_, bf16[32,1,32,1200]{3,2,1,0:T(8,128)(2,1)} %refs_1_.7, bf16[4,152,128]{2,1,0:T(8,128)(2,1)S(1)} %get-tuple-element.35.refs_2_.refs_0_), custom_call_target="tpu_custom_call" | custom-call | bytes 1228800 | tf_op jit(solution)/shard_map/pallas_call | solution.py:47
  14.4 0.0 copy-start
  14.4 0.0 collective-permute-done.3.refs_0_
  14.4 3.2 %collective-permute-start.8 = (bf16[4,304,128]{2,1,0:T(8,128)(2,1)S(1)}, bf16[4,304,128]{2,1,0:T(8,128)(2,1)S(1)}, u32[]{:S(2)}, u32[]{:S(2)}) collective-permute-start(bf16[4,304,128]{2,1,0:T(8,128)(2,1)S(1)} %get-tuple-element.36.refs_2_), channel_id=1, source_target_pairs={{0,6},{1,7},{2,4},{3,5},{4,2},{5,3},{6,0},{7,1},{8,14},{9,15},{10,... | collective-permute-start | bytes 933896 | tf_op jit(solution)/shard_map/ppermute | solution.py:146
  17.6 0.0 collective-permute-done.4.refs_1_
  17.6 1.2 %shard_map.39 = (bf16[8,16,1200]{2,1,0:T(8,128)(2,1)S(1)}, bf16[8,16,1200]{2,1,0:T(8,128)(2,1)S(1)}) custom-call(s32[1]{0:T(128)} %bitcast.refs_0_, bf16[32,1,32,1200]{3,2,1,0:T(8,128)(2,1)} %refs_1_.7, bf16[4,304,128]{2,1,0:T(8,128)(2,1)S(1)} %get-tuple-element.36.refs_2_), custom_call_target="tpu_custom_call" | custom-call | bytes 1228800 | tf_op jit(solution)/shard_map/pallas_call | solution.py:47
  18.9 6.1 %collective-permute-done.1.refs_2_ = bf16[4,152,128]{2,1,0:T(8,128)(2,1)S(1)} collective-permute-done((bf16[4,152,128]{2,1,0:T(8,128)(2,1)S(1)}, bf16[4,152,128]{2,1,0:T(8,128)(2,1)S(1)}, u32[]{:S(2)}, u32[]{:S(2)}) %collective-permute-start.1) | collective-permute-done | bytes 155680 | tf_op jit(solution)/shard_map/ppermute | solution.py:146
  25.1 0.0 collective-permute-done.2.refs_3_
  25.1 0.1 collective-permute-start.5
  25.2 0.7 collective-permute-start.6
  25.9 0.5 collective-permute-start.7
  26.4 0.0 collective-permute-done.8.refs_0_
  26.4 5.7 %collective-permute-done.9.refs_1_ = bf16[4,304,128]{2,1,0:T(8,128)(2,1)S(1)} collective-permute-done((bf16[4,304,128]{2,1,0:T(8,128)(2,1)S(1)}, bf16[4,304,128]{2,1,0:T(8,128)(2,1)S(1)}, u32[]{:S(2)}, u32[]{:S(2)}) %collective-permute-start.9) | collective-permute-done | bytes 311328 | tf_op jit(solution)/shard_map/ppermute | solution.py:146
  32.1 3.7 %collective-permute-start.16 = (bf16[2,304,128]{2,1,0:T(8,128)(2,1)S(1)}, bf16[2,304,128]{2,1,0:T(8,128)(2,1)S(1)}, u32[]{:S(2)}, u32[]{:S(2)}) collective-permute-start(bf16[2,304,128]{2,1,0:T(8,128)(2,1)S(1)} %get-tuple-element.59), channel_id=1, source_target_pairs={{0,24},{1,25},{2,26},{3,27},{4,28},{5,29},{6,30},{7,31},{8,16},{9,... | collective-permute-start | bytes 466952 | tf_op jit(solution)/shard_map/ppermute | solution.py:146
  35.8 1.3 %shard_map.44 = (bf16[4,152,128]{2,1,0:T(8,128)(2,1)S(1)}, bf16[4,152,128]{2,1,0:T(8,128)(2,1)S(1)}, bf16[4,152,128]{2,1,0:T(8,128)(2,1)S(1)}, bf16[4,152,128]{2,1,0:T(8,128)(2,1)S(1)}) custom-call(bf16[4,152,128]{2,1,0:T(8,128)(2,1)S(1)} %get-tuple-element.45.refs_2_.refs_0_, bf16[4,152,128]{2,1,0:T(8,128)(2,1)S(1)} %collective-permute-done.5.refs_1_, ...), custom_call_target="tpu_custom_call" | custom-call | flops 737280000 | bytes 2880000 | tf_op jit(solution)/shard_map/pallas_call | solution.py:47
  37.1 0.5 collective-permute-start.10
  37.6 1.5 %collective-permute-start.11 = (bf16[4,152,128]{2,1,0:T(8,128)(2,1)S(1)}, bf16[4,152,128]{2,1,0:T(8,128)(2,1)S(1)}, u32[]{:S(2)}, u32[]{:S(2)}) collective-permute-start(bf16[4,152,128]{2,1,0:T(8,128)(2,1)S(1)} %get-tuple-element.53), channel_id=1, source_target_pairs={{0,2},{1,3},{2,0},{3,1},{4,6},{5,7},{6,4},{7,5},{8,10},{9,11},{10,... | collective-permute-start | bytes 466952 | tf_op jit(solution)/shard_map/ppermute | solution.py:146
  39.1 1.5 %collective-permute-start.12 = (bf16[4,152,128]{2,1,0:T(8,128)(2,1)S(1)}, bf16[4,152,128]{2,1,0:T(8,128)(2,1)S(1)}, u32[]{:S(2)}, u32[]{:S(2)}) collective-permute-start(bf16[4,152,128]{2,1,0:T(8,128)(2,1)S(1)} %get-tuple-element.54), channel_id=1, source_target_pairs={{0,4},{1,5},{2,6},{3,7},{4,0},{5,1},{6,2},{7,3},{8,12},{9,13},{10,... | collective-permute-start | bytes 466952 | tf_op jit(solution)/shard_map/ppermute | solution.py:146
  40.7 2.9 %collective-permute-start.19 = (bf16[2,304,128]{2,1,0:T(8,128)(2,1)S(1)}, bf16[2,304,128]{2,1,0:T(8,128)(2,1)S(1)}, u32[]{:S(2)}, u32[]{:S(2)}) collective-permute-start(bf16[2,304,128]{2,1,0:T(8,128)(2,1)S(1)} %get-tuple-element.62), channel_id=1, source_target_pairs={{0,24},{1,25},{2,26},{3,27},{4,28},{5,29},{6,30},{7,31},{8,16},{9,... | collective-permute-start | bytes 466952 | tf_op jit(solution)/shard_map/ppermute | solution.py:146
  43.5 0.0 collective-permute-done.16.refs_2_
  43.5 1.3 %collective-permute-start.20 = (bf16[2,304,128]{2,1,0:T(8,128)(2,1)S(1)}, bf16[2,304,128]{2,1,0:T(8,128)(2,1)S(1)}, u32[]{:S(2)}, u32[]{:S(2)}) collective-permute-start(bf16[2,304,128]{2,1,0:T(8,128)(2,1)S(1)} %get-tuple-element.63), channel_id=1, source_target_pairs={{0,16},{1,17},{2,18},{3,19},{4,20},{5,21},{6,22},{7,23},{8,24},{9,... | collective-permute-start | bytes 466952 | tf_op jit(solution)/shard_map/ppermute | solution.py:146
  44.8 0.0 collective-permute-done.10.refs_1_
  44.8 0.3 collective-permute-start.21
  45.0 0.0 collective-permute-done.11.refs_2_
  45.0 1.6 %collective-permute-start.17 = (bf16[2,304,128]{2,1,0:T(8,128)(2,1)S(1)}, bf16[2,304,128]{2,1,0:T(8,128)(2,1)S(1)}, u32[]{:S(2)}, u32[]{:S(2)}) collective-permute-start(bf16[2,304,128]{2,1,0:T(8,128)(2,1)S(1)} %get-tuple-element.60), channel_id=1, source_target_pairs={{0,16},{1,17},{2,18},{3,19},{4,20},{5,21},{6,22},{7,23},{8,24},{9,... | collective-permute-start | bytes 466952 | tf_op jit(solution)/shard_map/ppermute | solution.py:146
  46.7 1.8 %collective-permute-start.18 = (bf16[2,304,128]{2,1,0:T(8,128)(2,1)S(1)}, bf16[2,304,128]{2,1,0:T(8,128)(2,1)S(1)}, u32[]{:S(2)}, u32[]{:S(2)}) collective-permute-start(bf16[2,304,128]{2,1,0:T(8,128)(2,1)S(1)} %get-tuple-element.61), channel_id=1, source_target_pairs={{0,8},{1,9},{2,10},{3,11},{4,12},{5,13},{6,14},{7,15},{8,0},{9,1},... | collective-permute-start | bytes 466952 | tf_op jit(solution)/shard_map/ppermute | solution.py:146
  48.5 0.9 %collective-permute-done.19.refs_2_ = bf16[2,304,128]{2,1,0:T(8,128)(2,1)S(1)} collective-permute-done((bf16[2,304,128]{2,1,0:T(8,128)(2,1)S(1)}, bf16[2,304,128]{2,1,0:T(8,128)(2,1)S(1)}, u32[]{:S(2)}, u32[]{:S(2)}) %collective-permute-start.19) | collective-permute-done | bytes 155680 | tf_op jit(solution)/shard_map/ppermute | solution.py:146
  49.4 6.9 %collective-permute-start.15 = (bf16[4,152,128]{2,1,0:T(8,128)(2,1)S(1)}, bf16[4,152,128]{2,1,0:T(8,128)(2,1)S(1)}, u32[]{:S(2)}, u32[]{:S(2)}) collective-permute-start(bf16[4,152,128]{2,1,0:T(8,128)(2,1)S(1)} %get-tuple-element.58), channel_id=1, source_target_pairs={{0,8},{1,9},{2,10},{3,11},{4,12},{5,13},{6,14},{7,15},{8,0},{9,1},... | collective-permute-start | bytes 466952 | tf_op jit(solution)/shard_map/ppermute | solution.py:146
  56.3 4.9 %collective-permute-done.20.refs_3_ = bf16[2,304,128]{2,1,0:T(8,128)(2,1)S(1)} collective-permute-done((bf16[2,304,128]{2,1,0:T(8,128)(2,1)S(1)}, bf16[2,304,128]{2,1,0:T(8,128)(2,1)S(1)}, u32[]{:S(2)}, u32[]{:S(2)}) %collective-permute-start.20) | collective-permute-done | bytes 155680 | tf_op jit(solution)/shard_map/ppermute | solution.py:146
  61.3 2.5 %collective-permute-start.13 = (bf16[4,152,128]{2,1,0:T(8,128)(2,1)S(1)}, bf16[4,152,128]{2,1,0:T(8,128)(2,1)S(1)}, u32[]{:S(2)}, u32[]{:S(2)}) collective-permute-start(bf16[4,152,128]{2,1,0:T(8,128)(2,1)S(1)} %get-tuple-element.55), channel_id=1, source_target_pairs={{0,24},{1,25},{2,26},{3,27},{4,28},{5,29},{6,30},{7,31},{8,16},{9,... | collective-permute-start | bytes 466952 | tf_op jit(solution)/shard_map/ppermute | solution.py:146
  63.7 0.0 collective-permute-done.21.refs_4_
  63.7 0.0 collective-permute-start.14
  63.7 1.7 %shard_map.46.refs_6_ = f32[32,256]{1,0:T(8,128)S(1)} custom-call(s32[1]{0:T(128)} %bitcast.refs_0_, bf16[2,304,128]{2,1,0:T(8,128)(2,1)S(1)} %get-tuple-element.44.refs_4_.refs_1_, bf16[2,304,128]{2,1,0:T(8,128)(2,1)S(1)} %collective-permute-done.19.refs_2_, bf16[2,304,128]{2,1,0:T(8,128)(2,1)S(1)} %collective-permute-done.20.refs_3_, ...), custom_call_target="tpu_custom_call" | custom-call | flops 368640000 | bytes 2880000 | tf_op jit(solution)/shard_map/pallas_call | solution.py:47
  65.4 0.4 collective-permute-done.17.refs_3_
  65.8 0.0 collective-permute-done.18.refs_4_
  65.9 2.3 %shard_map.47 = bf16[32,2,128]{2,1,0:T(2,128)(2,1)} custom-call(s32[1]{0:T(128)} %bitcast.refs_0_, bf16[2,304,128]{2,1,0:T(8,128)(2,1)S(1)} %get-tuple-element.50.refs_5_.refs_1_, bf16[2,304,128]{2,1,0:T(8,128)(2,1)S(1)} %collective-permute-done.16.refs_2_, bf16[2,304,128]{2,1,0:T(8,128)(2,1)S(1)} %collective-permute-done.17.refs_3_, ...), custom_call_target="tpu_custom_call" | custom-call | flops 368640000 | bytes 2880000 | tf_op jit(solution)/shard_map/pallas_call | solution.py:47
  68.2 2.9 %all-to-all-start = ((bf16[32,2,128]{2,1,0:T(2,128)(2,1)}), bf16[32,2,128]{2,1,0:T(2,128)(2,1)S(1)}, u32[]{:S(2)}, u32[]{:S(2)}) async-start(bf16[32,2,128]{2,1,0:T(2,128)(2,1)} %shard_map.47), calls=%async_computation | async-start | bytes 32768 | tf_op jit(solution)/shard_map/all_to_all | solution.py:324
  71.1 0.1 copy.4.refs_5_
  71.2 7.2 %all-to-all-done.refs_4_ = bf16[32,2,128]{2,1,0:T(2,128)(2,1)S(1)} async-done(((bf16[32,2,128]{2,1,0:T(2,128)(2,1)}), bf16[32,2,128]{2,1,0:T(2,128)(2,1)S(1)}, u32[]{:S(2)}, u32[]{:S(2)}) %all-to-all-start) | async-done | bytes 16416 | tf_op jit(solution)/shard_map/all_to_all | solution.py:324
  78.3 0.0 collective-permute-done.15.refs_3_
  78.3 0.6 shard_map.48.refs_4_
  78.9 1.2 %shard_map.49 = bf16[32,256]{1,0:T(8,128)(2,1)} custom-call(s32[1]{0:T(128)} %bitcast.refs_0_, bf16[8,16,1200]{2,1,0:T(8,128)(2,1)S(1)} %get-tuple-element.37.refs_1_, bf16[4,152,128]{2,1,0:T(8,128)(2,1)S(1)} %collective-permute-done.13.refs_2_, bf16[4,152,128]{2,1,0:T(8,128)(2,1)S(1)} %collective-permute-done.14.refs_3_, f32[32,256]{1,0:T(8,128)S(1)} %shard_map.48.refs_4_, ...), custom_call_target="tpu_custom_call" | custom-call | flops 4915200 | bytes 614400 | tf_op jit(solution)/shard_map/pallas_call | solution.py:47
  (16 shorter events, 0.2 us)
Async XLA Ops:
  4.0 10.4 %collective-permute-start.3 = (bf16[4,304,128]{2,1,0:T(8,128)(2,1)S(1)}, bf16[4,304,128]{2,1,0:T(8,128)(2,1)S(1)}, u32[]{:S(2)}, u32[]{:S(2)}) collective-permute-start(bf16[4,304,128]{2,1,0:T(8,128)(2,1)S(1)} %get-tuple-element.41), channel_id=1, source_target_pairs={{0,3},{1,2},{2,1},{3,0},{4,7},{5,6},{6,5},{7,4},{8,11},{9,10},{10,... | collective-permute-start | bytes 933896 | tf_op jit(solution)/shard_map/ppermute | solution.py:146
  6.5 11.2 %collective-permute-start.4 = (bf16[4,304,128]{2,1,0:T(8,128)(2,1)S(1)}, bf16[4,304,128]{2,1,0:T(8,128)(2,1)S(1)}, u32[]{:S(2)}, u32[]{:S(2)}) collective-permute-start(bf16[4,304,128]{2,1,0:T(8,128)(2,1)S(1)} %get-tuple-element.42), channel_id=1, source_target_pairs={{0,5},{1,4},{2,7},{3,6},{4,1},{5,0},{6,3},{7,2},{8,13},{9,12},{10,... | collective-permute-start | bytes 933896 | tf_op jit(solution)/shard_map/ppermute | solution.py:146
  8.3 10.6 %collective-permute-start = (bf16[4,152,128]{2,1,0:T(8,128)(2,1)S(1)}, bf16[4,152,128]{2,1,0:T(8,128)(2,1)S(1)}, u32[]{:S(2)}, u32[]{:S(2)}) collective-permute-start(bf16[4,152,128]{2,1,0:T(8,128)(2,1)S(1)} %get-tuple-element.38), channel_id=1, source_target_pairs={{0,24},{1,25},{2,26},{3,27},{4,28},{5,29},{6,30},{7,31},{8,16},{9,... | collective-permute-start | bytes 466952 | tf_op jit(solution)/shard_map/ppermute | solution.py:146
  11.9 13.2 %collective-permute-start.1 = (bf16[4,152,128]{2,1,0:T(8,128)(2,1)S(1)}, bf16[4,152,128]{2,1,0:T(8,128)(2,1)S(1)}, u32[]{:S(2)}, u32[]{:S(2)}) collective-permute-start(bf16[4,152,128]{2,1,0:T(8,128)(2,1)S(1)} %get-tuple-element.39), channel_id=1, source_target_pairs={{0,16},{1,17},{2,18},{3,19},{4,20},{5,21},{6,22},{7,23},{8,24},{9,... | collective-permute-start | bytes 466952 | tf_op jit(solution)/shard_map/ppermute | solution.py:146
  11.9 13.2 %collective-permute-start.2 = (bf16[4,152,128]{2,1,0:T(8,128)(2,1)S(1)}, bf16[4,152,128]{2,1,0:T(8,128)(2,1)S(1)}, u32[]{:S(2)}, u32[]{:S(2)}) collective-permute-start(bf16[4,152,128]{2,1,0:T(8,128)(2,1)S(1)} %get-tuple-element.40), channel_id=1, source_target_pairs={{0,8},{1,9},{2,10},{3,11},{4,12},{5,13},{6,14},{7,15},{8,0},{9,1},... | collective-permute-start | bytes 466952 | tf_op jit(solution)/shard_map/ppermute | solution.py:146
  14.4 21.4 %copy-start = (bf16[1,1200,1200]{2,1,0:T(8,128)(2,1)S(1)}, bf16[1,1200,1200]{2,1,0:T(8,128)(2,1)}, u32[]{:S(2)}) copy-start(bf16[1,1200,1200]{2,1,0:T(8,128)(2,1)} %refs_5_.5) | copy-start | bytes 8640004
  14.4 12.0 %collective-permute-start.8 = (bf16[4,304,128]{2,1,0:T(8,128)(2,1)S(1)}, bf16[4,304,128]{2,1,0:T(8,128)(2,1)S(1)}, u32[]{:S(2)}, u32[]{:S(2)}) collective-permute-start(bf16[4,304,128]{2,1,0:T(8,128)(2,1)S(1)} %get-tuple-element.36.refs_2_), channel_id=1, source_target_pairs={{0,6},{1,7},{2,4},{3,5},{4,2},{5,3},{6,0},{7,1},{8,14},{9,15},{10,... | collective-permute-start | bytes 933896 | tf_op jit(solution)/shard_map/ppermute | solution.py:146
  17.6 14.5 %collective-permute-start.9 = (bf16[4,304,128]{2,1,0:T(8,128)(2,1)S(1)}, bf16[4,304,128]{2,1,0:T(8,128)(2,1)S(1)}, u32[]{:S(2)}, u32[]{:S(2)}) collective-permute-start(bf16[4,304,128]{2,1,0:T(8,128)(2,1)S(1)} %get-tuple-element.49), channel_id=1, source_target_pairs={{0,7},{1,6},{2,5},{3,4},{4,3},{5,2},{6,1},{7,0},{8,15},{9,14},{10,... | collective-permute-start | bytes 933896 | tf_op jit(solution)/shard_map/ppermute | solution.py:146
  25.1 10.7 %collective-permute-start.5 = (bf16[4,152,128]{2,1,0:T(8,128)(2,1)S(1)}, bf16[4,152,128]{2,1,0:T(8,128)(2,1)S(1)}, u32[]{:S(2)}, u32[]{:S(2)}) collective-permute-start(bf16[4,152,128]{2,1,0:T(8,128)(2,1)S(1)} %get-tuple-element.46), channel_id=1, source_target_pairs={{0,1},{1,0},{2,3},{3,2},{4,5},{5,4},{6,7},{7,6},{8,9},{9,8},{10,11... | collective-permute-start | bytes 466952 | tf_op jit(solution)/shard_map/ppermute | solution.py:146
  25.2 10.6 %collective-permute-start.6 = (bf16[4,152,128]{2,1,0:T(8,128)(2,1)S(1)}, bf16[4,152,128]{2,1,0:T(8,128)(2,1)S(1)}, u32[]{:S(2)}, u32[]{:S(2)}) collective-permute-start(bf16[4,152,128]{2,1,0:T(8,128)(2,1)S(1)} %get-tuple-element.47), channel_id=1, source_target_pairs={{0,2},{1,3},{2,0},{3,1},{4,6},{5,7},{6,4},{7,5},{8,10},{9,11},{10,... | collective-permute-start | bytes 466952 | tf_op jit(solution)/shard_map/ppermute | solution.py:146
  25.9 9.9 %collective-permute-start.7 = (bf16[4,152,128]{2,1,0:T(8,128)(2,1)S(1)}, bf16[4,152,128]{2,1,0:T(8,128)(2,1)S(1)}, u32[]{:S(2)}, u32[]{:S(2)}) collective-permute-start(bf16[4,152,128]{2,1,0:T(8,128)(2,1)S(1)} %get-tuple-element.48), channel_id=1, source_target_pairs={{0,4},{1,5},{2,6},{3,7},{4,0},{5,1},{6,2},{7,3},{8,12},{9,13},{10,... | collective-permute-start | bytes 466952 | tf_op jit(solution)/shard_map/ppermute | solution.py:146
  32.1 11.4 %collective-permute-start.16 = (bf16[2,304,128]{2,1,0:T(8,128)(2,1)S(1)}, bf16[2,304,128]{2,1,0:T(8,128)(2,1)S(1)}, u32[]{:S(2)}, u32[]{:S(2)}) collective-permute-start(bf16[2,304,128]{2,1,0:T(8,128)(2,1)S(1)} %get-tuple-element.59), channel_id=1, source_target_pairs={{0,24},{1,25},{2,26},{3,27},{4,28},{5,29},{6,30},{7,31},{8,16},{9,... | collective-permute-start | bytes 466952 | tf_op jit(solution)/shard_map/ppermute | solution.py:146
  37.1 7.7 %collective-permute-start.10 = (bf16[4,152,128]{2,1,0:T(8,128)(2,1)S(1)}, bf16[4,152,128]{2,1,0:T(8,128)(2,1)S(1)}, u32[]{:S(2)}, u32[]{:S(2)}) collective-permute-start(bf16[4,152,128]{2,1,0:T(8,128)(2,1)S(1)} %get-tuple-element.52), channel_id=1, source_target_pairs={{0,1},{1,0},{2,3},{3,2},{4,5},{5,4},{6,7},{7,6},{8,9},{9,8},{10,11... | collective-permute-start | bytes 466952 | tf_op jit(solution)/shard_map/ppermute | solution.py:146
  37.6 7.4 %collective-permute-start.11 = (bf16[4,152,128]{2,1,0:T(8,128)(2,1)S(1)}, bf16[4,152,128]{2,1,0:T(8,128)(2,1)S(1)}, u32[]{:S(2)}, u32[]{:S(2)}) collective-permute-start(bf16[4,152,128]{2,1,0:T(8,128)(2,1)S(1)} %get-tuple-element.53), channel_id=1, source_target_pairs={{0,2},{1,3},{2,0},{3,1},{4,6},{5,7},{6,4},{7,5},{8,10},{9,11},{10,... | collective-permute-start | bytes 466952 | tf_op jit(solution)/shard_map/ppermute | solution.py:146
  39.1 7.6 %collective-permute-start.12 = (bf16[4,152,128]{2,1,0:T(8,128)(2,1)S(1)}, bf16[4,152,128]{2,1,0:T(8,128)(2,1)S(1)}, u32[]{:S(2)}, u32[]{:S(2)}) collective-permute-start(bf16[4,152,128]{2,1,0:T(8,128)(2,1)S(1)} %get-tuple-element.54), channel_id=1, source_target_pairs={{0,4},{1,5},{2,6},{3,7},{4,0},{5,1},{6,2},{7,3},{8,12},{9,13},{10,... | collective-permute-start | bytes 466952 | tf_op jit(solution)/shard_map/ppermute | solution.py:146
  40.7 8.7 %collective-permute-start.19 = (bf16[2,304,128]{2,1,0:T(8,128)(2,1)S(1)}, bf16[2,304,128]{2,1,0:T(8,128)(2,1)S(1)}, u32[]{:S(2)}, u32[]{:S(2)}) collective-permute-start(bf16[2,304,128]{2,1,0:T(8,128)(2,1)S(1)} %get-tuple-element.62), channel_id=1, source_target_pairs={{0,24},{1,25},{2,26},{3,27},{4,28},{5,29},{6,30},{7,31},{8,16},{9,... | collective-permute-start | bytes 466952 | tf_op jit(solution)/shard_map/ppermute | solution.py:146
  43.5 17.7 %collective-permute-start.20 = (bf16[2,304,128]{2,1,0:T(8,128)(2,1)S(1)}, bf16[2,304,128]{2,1,0:T(8,128)(2,1)S(1)}, u32[]{:S(2)}, u32[]{:S(2)}) collective-permute-start(bf16[2,304,128]{2,1,0:T(8,128)(2,1)S(1)} %get-tuple-element.63), channel_id=1, source_target_pairs={{0,16},{1,17},{2,18},{3,19},{4,20},{5,21},{6,22},{7,23},{8,24},{9,... | collective-permute-start | bytes 466952 | tf_op jit(solution)/shard_map/ppermute | solution.py:146
  44.8 19.0 %collective-permute-start.21 = (bf16[2,304,128]{2,1,0:T(8,128)(2,1)S(1)}, bf16[2,304,128]{2,1,0:T(8,128)(2,1)S(1)}, u32[]{:S(2)}, u32[]{:S(2)}) collective-permute-start(bf16[2,304,128]{2,1,0:T(8,128)(2,1)S(1)} %get-tuple-element.64), channel_id=1, source_target_pairs={{0,8},{1,9},{2,10},{3,11},{4,12},{5,13},{6,14},{7,15},{8,0},{9,1},... | collective-permute-start | bytes 466952 | tf_op jit(solution)/shard_map/ppermute | solution.py:146
  45.0 20.8 %collective-permute-start.17 = (bf16[2,304,128]{2,1,0:T(8,128)(2,1)S(1)}, bf16[2,304,128]{2,1,0:T(8,128)(2,1)S(1)}, u32[]{:S(2)}, u32[]{:S(2)}) collective-permute-start(bf16[2,304,128]{2,1,0:T(8,128)(2,1)S(1)} %get-tuple-element.60), channel_id=1, source_target_pairs={{0,16},{1,17},{2,18},{3,19},{4,20},{5,21},{6,22},{7,23},{8,24},{9,... | collective-permute-start | bytes 466952 | tf_op jit(solution)/shard_map/ppermute | solution.py:146
  46.7 19.2 %collective-permute-start.18 = (bf16[2,304,128]{2,1,0:T(8,128)(2,1)S(1)}, bf16[2,304,128]{2,1,0:T(8,128)(2,1)S(1)}, u32[]{:S(2)}, u32[]{:S(2)}) collective-permute-start(bf16[2,304,128]{2,1,0:T(8,128)(2,1)S(1)} %get-tuple-element.61), channel_id=1, source_target_pairs={{0,8},{1,9},{2,10},{3,11},{4,12},{5,13},{6,14},{7,15},{8,0},{9,1},... | collective-permute-start | bytes 466952 | tf_op jit(solution)/shard_map/ppermute | solution.py:146
  49.4 28.9 %collective-permute-start.15 = (bf16[4,152,128]{2,1,0:T(8,128)(2,1)S(1)}, bf16[4,152,128]{2,1,0:T(8,128)(2,1)S(1)}, u32[]{:S(2)}, u32[]{:S(2)}) collective-permute-start(bf16[4,152,128]{2,1,0:T(8,128)(2,1)S(1)} %get-tuple-element.58), channel_id=1, source_target_pairs={{0,8},{1,9},{2,10},{3,11},{4,12},{5,13},{6,14},{7,15},{8,0},{9,1},... | collective-permute-start | bytes 466952 | tf_op jit(solution)/shard_map/ppermute | solution.py:146
  61.3 17.6 %collective-permute-start.13 = (bf16[4,152,128]{2,1,0:T(8,128)(2,1)S(1)}, bf16[4,152,128]{2,1,0:T(8,128)(2,1)S(1)}, u32[]{:S(2)}, u32[]{:S(2)}) collective-permute-start(bf16[4,152,128]{2,1,0:T(8,128)(2,1)S(1)} %get-tuple-element.55), channel_id=1, source_target_pairs={{0,24},{1,25},{2,26},{3,27},{4,28},{5,29},{6,30},{7,31},{8,16},{9,... | collective-permute-start | bytes 466952 | tf_op jit(solution)/shard_map/ppermute | solution.py:146
  63.7 15.1 %collective-permute-start.14 = (bf16[4,152,128]{2,1,0:T(8,128)(2,1)S(1)}, bf16[4,152,128]{2,1,0:T(8,128)(2,1)S(1)}, u32[]{:S(2)}, u32[]{:S(2)}) collective-permute-start(bf16[4,152,128]{2,1,0:T(8,128)(2,1)S(1)} %get-tuple-element.56), channel_id=1, source_target_pairs={{0,16},{1,17},{2,18},{3,19},{4,20},{5,21},{6,22},{7,23},{8,24},{9,... | collective-permute-start | bytes 466952 | tf_op jit(solution)/shard_map/ppermute | solution.py:146
  63.7 7.3 %copy-start.1 = (s32[32,1]{0,1:T(1,128)S(1)}, s32[32,1]{0,1:T(1,128)}, u32[]{:S(2)}) copy-start(s32[32,1]{0,1:T(1,128)} %param.5) | copy-start | bytes 388
  68.2 10.2 %all-to-all-start = ((bf16[32,2,128]{2,1,0:T(2,128)(2,1)}), bf16[32,2,128]{2,1,0:T(2,128)(2,1)S(1)}, u32[]{:S(2)}, u32[]{:S(2)}) async-start(bf16[32,2,128]{2,1,0:T(2,128)(2,1)} %shard_map.47), calls=%async_computation | async-start | bytes 32768 | tf_op jit(solution)/shard_map/all_to_all | solution.py:324
where the time goes:
time: 80.4 us; the launch traced here: 80.1 us
  starting transfers between devices  40.5 us (50%)
  waiting for transfers between devices  25.3 us (31%)
  Pallas kernels  14 us (17%)
    ppermute x22, starting transfers between devices, hop(): return lax.ppermute(x, 'pb', [(d, d ^ m) for d in range(N)])  37.6 us
    ppermute x22, waiting for transfers between devices, hop(): return lax.ppermute(x, 'pb', [(d, d ^ m) for d in range(N)])  18.1 us
    pallas_call x13, Pallas kernels, call(): return pallas(body, outs, specs, a, scratch, flops, moved)(*ins, *after)  14 us
    all_to_all x1, waiting for transfers between devices, fast(): lax.all_to_all(sums, 'pb', split_axis=0, concat_axis=0, tiled=True)  7.15 us
    all_to_all x1, starting transfers between devices, fast(): lax.all_to_all(sums, 'pb', split_axis=0, concat_axis=0, tiled=True)  2.89 us
  transfers between devices with their start and end apart: 23, of which 6 were waited for; matrix products, arithmetic and copies ran while one was open for 0% of the time, Pallas kernels for 11%

commit v1 on v0

v1 whole, which is shorter than its diff:
```python
import jax
import jax.numpy as jnp
from jax import lax
from jax.experimental import pallas as pl
from jax.experimental.pallas import tpu as pltpu
from jax.sharding import PartitionSpec as P


BF16, F32 = jnp.bfloat16, jnp.float32
LANES = 128
HALF = LANES // 2
COLS = 256


VM = pl.BlockSpec(memory_space=pltpu.VMEM)
SM = pl.BlockSpec(memory_space=pltpu.SMEM)
ANY = pl.BlockSpec(memory_space=pl.ANY)
HBM = pl.BlockSpec(memory_space=pltpu.HBM)


def split(devices):
    outer = 2 ** ((devices.bit_length() - 1) // 2)
    return outer, devices // outer


class Sizes:
    def __init__(self, shape, devices):
        self.q, _, both, self.ng = shape
        self.pairs = both // 2
        self.full, self.tail = divmod(self.ng, LANES)
        self.rows = self.pairs * self.full + (self.pairs // 2 if self.tail else 0)
        self.wide = LANES * (self.full + (1 if self.tail else 0))
        self.devices = devices
        self.outer, self.inner = split(devices)

    def fits(self):
        power = self.devices & (self.devices - 1) == 0
        return power and self.inner >= 4 and self.pairs == 16 and 0 < self.tail <= HALF


def call(kernel, outs, ins, specs, scratch=(), flops=0, moved=0, after=()):
    k, a = len(ins), len(after)

    def body(*refs):
        kernel(*refs[:k], *refs[k + a :])

    return pallas(body, outs, specs, a, scratch, flops, moved)(*ins, *after)


def pallas(body, outs, specs, a, scratch, flops, moved):
    return pl.pallas_call(
        body,
        out_shape=tuple(outs),
        in_specs=[*specs, *[ANY] * a],
        out_specs=tuple(pl.BlockSpec(memory_space=pltpu.VMEM) for _ in outs),
        scratch_shapes=list(scratch),
        compiler_params=pltpu.CompilerParams(vmem_limit_bytes=24 << 20),
        cost_estimate=pl.CostEstimate(flops=flops, bytes_accessed=moved, transcendentals=0),
    )


def pack(s, read, dst, b, base):
    n = s.pairs
    for j in range(s.full):
        dst[b, base + n * j : base + n * (j + 1), :] = read(LANES * j, LANES * (j + 1))
    last = read(LANES * s.full, s.wide).astype(F32)
    lane = lax.broadcasted_iota(jnp.int32, (n // 2, LANES), 1)
    folded = jnp.where(lane < HALF, last[: n // 2], pltpu.roll(last[n // 2 :], HALF, 1))
    dst[b, base + n * s.full : base + s.rows, :] = folded.astype(BF16)


def unpack(s, src, b, base, dst, row):
    n = s.pairs
    src = src if b is None else src.at[b]
    for j in range(s.full):
        dst[row : row + n, LANES * j : LANES * (j + 1)] = src[base + n * j : base + n * (j + 1), :]
    folded = src[base + n * s.full : base + s.rows, :].astype(F32)
    last = jnp.concatenate([folded, pltpu.roll(folded, HALF, 1)], axis=0).astype(BF16)
    dst[row : row + n, LANES * s.full : s.ng] = last[:, : s.tail]


def nt(x, y):
    return lax.dot_general(x, y, (((1,), (1,)), ((), ())), preferred_element_type=F32)


def screen(s, v, w_ref, out):
    for lo in range(0, s.ng, COLS):
        hi = min(lo + COLS, s.ng)
        out[:, lo:hi] = nt(v[...], w_ref[0, lo:hi, :]).astype(BF16)


def spread(s, c, sc):
    n, count = s.pairs, c.shape[0]
    full = nt(c, sc)
    r = lax.broadcasted_iota(jnp.int32, (count, count), 0)
    k = lax.broadcasted_iota(jnp.int32, (count, count), 1)
    own = jnp.where(r // n == k // n, full, 0.0).astype(BF16)
    e = lax.broadcasted_iota(jnp.int32, (count, n * n), 0)
    f = lax.broadcasted_iota(jnp.int32, (count, n * n), 1)
    copies = jnp.where(e % n == f % n, 1.0, 0.0).astype(BF16)
    x = jnp.dot(own, copies, preferred_element_type=F32)
    return jnp.where(f // n == e % n, x, 0.0).astype(BF16)


def pick(shape, wanted):
    row = lax.broadcasted_iota(jnp.int32, shape, 0)
    column = lax.broadcasted_iota(jnp.int32, shape, 1)
    return jnp.where(wanted(row, column), 1.0, 0.0).astype(BF16)


def table(index, values):
    out = jnp.zeros_like(index)
    for i, value in enumerate(values):
        out = jnp.where(index == i, value, out)
    return out


def rows_of_pairs(s, me, offsets, c, sc):
    x = spread(s, c, sc)
    place = pick((s.devices, x.shape[0]), lambda q, r: q == (table(r // s.pairs, offsets) ^ me))
    return jnp.dot(place, x, preferred_element_type=F32)


def gather(s, me, dens, offsets, half, buf, sem):
    lo, n = (0, 2 * s.pairs) if half is None else (half * s.pairs, s.pairs)
    copies = [
        pltpu.make_async_copy(dens.at[me ^ m, 0, pl.ds(lo, n), :], buf.at[i], sem.at[i])
        for i, m in enumerate(offsets)
    ]
    for c in copies:
        c.start()
    return copies


def reader(s, buf, i, row, edge):
    def read(lo, hi):
        if hi <= s.ng:
            return buf[i, row : row + s.pairs, lo:hi]
        edge[i, :, : s.tail] = buf[i, row : row + s.pairs, lo : s.ng]
        return edge[i]

    return read


def parts_of(devices):
    outer, count = split(devices)
    inner = sorted(range(count), key=lambda p: (bin(p).count("1"), p))
    back, there = inner[: count // 2], inner[count // 2 :]
    half = len(there) // 2
    return [back[:half], back[half:]], [there[:half], there[half:]], list(range(outer - 1, 0, -1))


def fast(s, densities, weights, live):
    me_arr = lax.axis_index("pb").astype(jnp.int32).reshape(1)
    O, I, N, n = s.outer, s.inner, s.devices, s.pairs
    backs, groups, far = parts_of(N)
    order = [0, *far]
    back, there = backs[0] + backs[1], groups[0] + groups[1]
    h, g = len(back), len(groups[0])
    T = n * n // LANES
    block = n * s.ng

    def sds(*shape):
        return jax.ShapeDtypeStruct(shape, BF16)

    def hop(x, m):
        return lax.ppermute(x, "pb", [(d, d ^ m) for d in range(N)])

    densities = pltpu.with_memory_space_constraint(densities, pltpu.HBM)

    def take_v(zs, after):
        def kernel(me_ref, dens, *refs):
            outs, (buf, edge, sem) = refs[: len(zs)], refs[len(zs) :]
            offs = [dz * I + p for dz in zs for p in back]
            for i, c in enumerate(gather(s, me_ref[0], dens, offs, 1, buf, sem)):
                c.wait()
                pack(s, reader(s, buf, i, 0, edge), outs[i // h], i % h, 0)

        k = len(zs) * h
        return call(
            kernel,
            [sds(h, s.rows, LANES)] * len(zs),
            (me_arr, densities),
            [SM, HBM],
            [pltpu.VMEM((k, n, s.ng), BF16), pltpu.VMEM((k, n, LANES), BF16), pltpu.SemaphoreType.DMA((k,))],
            moved=4 * k * block,
            after=after,
        )

    first = take_v(far[:1], ())
    rest = take_v([*far[1:], 0], (first[0],))
    vb = dict(zip([*far, 0], [*first, *rest]))
    vz = {dz: hop(vb[dz], dz * I) for dz in far}

    def take_cv(index, after):
        group = groups[index]

        def kernel(me_ref, dens, *refs):
            outs, (buf, edge, edge2, sem) = refs[:g], refs[g:]
            offs = [dz * I + p for p in group for dz in order]
            for i, c in enumerate(gather(s, me_ref[0], dens, offs, None, buf, sem)):
                c.wait()
                pack(s, reader(s, buf, i, 0, edge), outs[i // O], i % O, 0)
                pack(s, reader(s, buf, i, n, edge2), outs[i // O], i % O, s.rows)

        k = O * g
        return call(
            kernel,
            [sds(O, 2 * s.rows, LANES)] * g,
            (me_arr, densities),
            [SM, HBM],
            [
                pltpu.VMEM((k, 2 * n, s.ng), BF16),
                pltpu.VMEM((k, n, LANES), BF16),
                pltpu.VMEM((k, n, LANES), BF16),
                pltpu.SemaphoreType.DMA((k,)),
            ],
            moved=8 * k * block,
            after=after,
        )

    def regroup(picks, count, parts, ins, after=()):
        def kernel(*refs):
            src, outs = refs[: len(ins)], refs[len(ins) :]
            for o, chosen in zip(outs, picks):
                for i, (a, b) in enumerate(chosen):
                    o[i] = src[a][b]

        return call(
            kernel,
            [sds(count, parts * s.rows, LANES)] * len(picks),
            ins,
            [VM] * len(ins),
            moved=4 * len(picks) * count * parts * block,
            after=after,
        )

    sent0 = take_cv(0, (rest[0],))
    near0 = [hop(x, p) for x, p in zip(sent0, groups[0])]
    sent1 = take_cv(1, (sent0[0],))
    near1 = [hop(x, p) for x, p in zip(sent1, groups[1])]

    def take_c(me_ref, dens, *refs):
        outs, sems = refs[:2], refs[2]
        copies = []
        for t, ps in enumerate(backs):
            copies += gather(s, me_ref[0], dens, [dz * I + p for dz in order for p in ps], 0, outs[t], sems.at[t])
        for c in copies:
            c.wait()

    own_c = call(
        take_c,
        [sds(O * len(ps), n, s.ng) for ps in backs],
        (me_arr, densities),
        [SM, HBM],
        [pltpu.SemaphoreType.DMA((2, O * h // 2))],
        moved=4 * O * h * block,
        after=(sent1[0],),
    )

    def onward(near, after):
        parts = regroup([[(j, zi) for j in range(g)] for zi in range(O)], g, 2, near, after)
        return [parts[0]] + [hop(x, dz * I) for dz, x in zip(far, parts[1:])]

    arrived = [onward(near0, (own_c[0],))]

    zs = [vb[0]] + [vz[dz] for dz in far]
    pieces = regroup([[(zi, j) for zi in range(O)] for j in range(h)], O, 1, zs, (arrived[0][0],))
    arrived.append(onward(near1, (pieces[0],)))
    vin = [pieces[0]] + [hop(x, p) for x, p in zip(pieces[1:], back[1:])]

    def screen_back(*refs):
        src, w_ref, outs, (v, sc) = refs[:h], refs[h], refs[h + 1 : 2 * h + 1], refs[2 * h + 1 :]
        for j in range(h):
            for a in range(O):
                unpack(s, src[j], a, 0, v, n * (j * O + a))
        screen(s, v, w_ref, sc)
        for j in range(h):
            for a in range(O):
                row = n * (j * O + a)
                pack(s, lambda lo, hi, row=row: sc[row : row + n, lo:hi], outs[j], a, 0)

    m_rows = n * h * O
    sb = call(
        screen_back,
        [sds(O, s.rows, LANES)] * h,
        (*vin, weights),
        [VM] * (h + 1),
        [pltpu.VMEM((m_rows, s.ng), BF16), pltpu.VMEM((m_rows, s.wide), BF16)],
        flops=2 * m_rows * s.ng * s.ng,
        moved=2 * s.ng * s.ng,
        after=(arrived[1][0],),
    )
    sin = [sb[0]] + [hop(x, p) for x, p in zip(sb[1:], back[1:])]
    half = len(backs[0])
    out0 = regroup([[(j, zi) for j in range(half)] for zi in range(O)], half, 1, sin[:half])
    sz0 = [out0[0]] + [hop(x, dz * I) for dz, x in zip(far, out0[1:])]

    def blocks_at_owner(index, after):
        count = O * g

        def kernel(*refs):
            src, w_ref, outs, (c, v, sc) = refs[:O], refs[O], refs[O + 1 : O + 1 + g], refs[O + 1 + g :]
            for zi in range(O):
                for j in range(g):
                    unpack(s, src[zi], j, 0, c, n * (zi * g + j))
                    unpack(s, src[zi], j, s.rows, v, n * (zi * g + j))
            screen(s, v, w_ref, sc)
            x = spread(s, c[...], sc[:, : s.ng])
            for j in range(g):
                total = 0.0
                for t in range(T):
                    sums = pick(
                        (O * T, count * n),
                        lambda r, k, j=j, t=t: (k // n == r // T * g + j) & (r % T == t),
                    )
                    total = total + jnp.dot(
                        sums, x[:, LANES * t : LANES * (t + 1)], preferred_element_type=F32
                    )
                outs[j][...] = total

        return call(
            kernel,
            [jax.ShapeDtypeStruct((O * T, LANES), F32)] * g,
            (*arrived[index], weights),
            [VM] * (O + 1),
            [
                pltpu.VMEM((n * count, s.ng), BF16),
                pltpu.VMEM((n * count, s.ng), BF16),
                pltpu.VMEM((n * count, s.wide), BF16),
            ],
            flops=2 * n * count * s.ng * s.ng,
            moved=2 * s.ng * s.ng,
            after=after,
        )

    done0 = blocks_at_owner(0, (out0[0],))
    done1 = blocks_at_owner(1, (done0[0],))
    returned = [hop(x, p) for x, p in zip([*done0, *done1], there)]

    rows2 = len(backs[1]) * s.rows
    extra = len(there) * T

    def outward1(*refs):
        src, small, outs = refs[: h - half], refs[h - half : h - half + 2 * g], refs[h - half + 2 * g :]
        blocks = jnp.concatenate([x[...] for x in small], axis=0).astype(BF16)
        turn = pick(
            (O * extra, O * extra),
            lambda r, k: (r % T == k % T) & (r // extra == k % (O * T) // T) & (r % extra // T == k // (O * T)),
        )
        turned = jnp.dot(turn, blocks, preferred_element_type=F32)
        for zi, o in enumerate(outs):
            for j in range(h - half):
                o[s.rows * j : s.rows * (j + 1), :] = src[j][zi]
            o[rows2 : rows2 + extra, :] = turned[extra * zi : extra * (zi + 1), :].astype(BF16)

    out1 = call(
        outward1,
        [sds(rows2 + extra, LANES)] * O,
        (*sin[half:], *returned),
        [VM] * (h - half + 2 * g),
        moved=4 * O * rows2 * LANES,
    )
    sz1 = [out1[0]] + [hop(x, dz * I) for dz, x in zip(far, out1[1:])]

    def finish0(me_ref, c_ref, *refs):
        src, (out, c, sc) = refs[:O], refs[O:]
        for zi in range(O):
            for j in range(half):
                row = n * (zi * half + j)
                c[row : row + n, :] = c_ref[zi * half + j]
                unpack(s, src[zi], j, 0, sc, row)
        out[...] = rows_of_pairs(s, me_ref[0], [dz * I + p for dz in order for p in backs[0]], c[...], sc[...])

    def finish1(me_ref, c_ref, *refs):
        src, (before, live_ref, out, c, sc) = refs[:O], refs[O:]
        me, k = me_ref[0], h - half
        for zi in range(O):
            for j in range(k):
                row = n * (zi * k + j)
                c[row : row + n, :] = c_ref[zi * k + j]
                unpack(s, src[zi], None, s.rows * j, sc, row)
        r = rows_of_pairs(s, me, [dz * I + p for dz in order for p in backs[1]], c[...], sc[...])
        small = jnp.concatenate([x[rows2 : rows2 + extra, :].astype(F32) for x in src], axis=0).astype(BF16)
        offs = [dz * I + p for dz in order for p in there]
        placed = [
            jnp.dot(
                pick((N, O * extra), lambda q, x, t=t: (q == (table(x // T, offs) ^ me)) & (x % T == t)),
                small,
                preferred_element_type=F32,
            )
            for t in range(T)
        ]
        r = r + before[...] + jnp.concatenate(placed, axis=1)
        out[...] = (r * live_ref[...].astype(F32)).astype(BF16)

    def scratch(ps):
        return [pltpu.VMEM((n * O * len(ps), s.ng), BF16)] * 2

    partial = call(
        finish0,
        [jax.ShapeDtypeStruct((N, n * n), F32)],
        (me_arr, own_c[0], *sz0),
        [SM] + [VM] * (1 + O),
        scratch(backs[0]),
        flops=2 * m_rows * s.ng * n,
        moved=4 * m_rows * s.ng,
        after=(out1[0],),
    )[0]
    return call(
        finish1,
        [sds(N, n * n)],
        (me_arr, own_c[1], *sz1, partial, live),
        [SM] + [VM] * (3 + O),
        scratch(backs[1]),
        flops=2 * m_rows * s.ng * n,
        moved=4 * m_rows * s.ng,
    )[0][:, None, :]


def plain(densities, screening, live):
    pairs = densities.shape[2] // 2
    arrived = lax.all_to_all(densities, "pb", split_axis=0, concat_axis=0, tiled=True)
    screened = jnp.einsum(
        "nkbh,gh->nkbg", arrived[:, :, pairs:, :], screening[0], preferred_element_type=F32
    ).astype(BF16)
    blocks = jnp.einsum("nkag,nkbg->nkab", arrived[:, :, :pairs, :], screened, preferred_element_type=F32)
    blocks = blocks.reshape(blocks.shape[0], blocks.shape[1], -1).astype(BF16)
    result = lax.all_to_all(blocks, "pb", split_axis=0, concat_axis=0, tiled=True)
    return result * live.astype(BF16)[:, :, None]


def solution(mesh):
    devices = mesh.shape["pb"]

    def on_device(densities, screening, live):
        s = Sizes(densities.shape, devices)
        if s.q == devices and s.fits():
            return fast(s, densities, screening, live)
        return plain(densities, screening, live)

    in_specs = (P(None, "pb", None, None), P("pb", None, None), P(None, "pb"))
    return jax.shard_map(
        on_device, mesh=mesh, in_specs=in_specs, out_specs=P(None, "pb", None), check_vma=False
    )
```

time: 80.4 us -> 95 us (1.18)
  waiting for transfers between devices: 25.3 us -> 34.7 us
  starting transfers between devices: 40.5 us -> 45.3 us
    ppermute x22 -> x29, waiting for transfers between devices: 18.1 us -> 34.7 us  [hop(): return lax.ppermute(x, 'pb', [(d, d ^ m) for d in range(N)])]
    ppermute x22 -> x29, starting transfers between devices: 37.6 us -> 45.3 us  [hop(): return lax.ppermute(x, 'pb', [(d, d ^ m) for d in range(N)])]
    all_to_all x1 -> x0, waiting for transfers between devices: 7.15 us -> none  [fast(): lax.all_to_all(sums, 'pb', split_axis=0, concat_axis=0, tiled=True)]
    all_to_all x1 -> x0, starting transfers between devices: 2.89 us -> none  [fast(): lax.all_to_all(sums, 'pb', split_axis=0, concat_axis=0, tiled=True)]
    pallas_call x13 -> x15, Pallas kernels: 14 us -> 14.2 us  [call(): return pallas(body, outs, specs, a, scratch, flops, moved)(*ins, *after)]
  transfers between devices with their start and end apart: 23 -> 29, of which waited for: 6 -> 9; matrix products, arithmetic and copies ran while one was open for 0% -> 0% of each run, Pallas kernels for 11% -> 9%
where the time goes in v1:
time: 95 us; the launch traced here: 94.6 us
  starting transfers between devices  45.3 us (48%)
  waiting for transfers between devices  34.7 us (37%)
  Pallas kernels  14.2 us (15%)
    ppermute x29, starting transfers between devices, hop(): return lax.ppermute(x, 'pb', [(d, d ^ m) for d in range(N)])  45.3 us
    ppermute x29, waiting for transfers between devices, hop(): return lax.ppermute(x, 'pb', [(d, d ^ m) for d in range(N)])  34.7 us
    pallas_call x15, Pallas kernels, call(): return pallas(body, outs, specs, a, scratch, flops, moved)(*ins, *after)  14.2 us
  transfers between devices with their start and end apart: 29, of which 9 were waited for; matrix products, arithmetic and copies ran while one was open for 0% of the time, Pallas kernels for 9%

profile of v1, /device:TPU:0, one launch (start us, length us, event | category | flops | bytes accessed | tf_op | source)
XLA Modules:
  0.0 94.6 jit_solution(7511381847700258074)
XLA Ops:
  0.0 1.1 %shard_map.37.refs_2_ = bf16[4,152,128]{2,1,0:T(8,128)(2,1)S(1)} custom-call(s32[1]{0:T(128)} %bitcast.refs_0_, bf16[32,1,32,1200]{3,2,1,0:T(8,128)(2,1)} %refs_1_.9), custom_call_target="tpu_custom_call" | custom-call | bytes 307200 | tf_op jit(solution)/shard_map/pallas_call | solution.py:47
  1.2 1.9 %shard_map.38 = (bf16[4,152,128]{2,1,0:T(8,128)(2,1)S(1)}, bf16[4,152,128]{2,1,0:T(8,128)(2,1)S(1)}, bf16[4,152,128]{2,1,0:T(8,128)(2,1)S(1)}) custom-call(s32[1]{0:T(128)} %bitcast.refs_0_, bf16[32,1,32,1200]{3,2,1,0:T(8,128)(2,1)} %refs_1_.9, bf16[4,152,128]{2,1,0:T(8,128)(2,1)S(1)} %shard_map.37.refs_2_), custom_call_target="tpu_custom_call" | custom-call | bytes 921600 | tf_op jit(solution)/shard_map/pallas_call | solution.py:47
  3.1 1.7 %shard_map.39 = (bf16[4,304,128]{2,1,0:T(8,128)(2,1)S(1)}, bf16[4,304,128]{2,1,0:T(8,128)(2,1)S(1)}) custom-call(s32[1]{0:T(128)} %bitcast.refs_0_, bf16[32,1,32,1200]{3,2,1,0:T(8,128)(2,1)} %refs_1_.9, bf16[4,152,128]{2,1,0:T(8,128)(2,1)S(1)} %get-tuple-element.42.refs_2_), custom_call_target="tpu_custom_call" | custom-call | bytes 1228800 | tf_op jit(solution)/shard_map/pallas_call | solution.py:47
  4.8 2.5 %collective-permute-start.3 = (bf16[4,304,128]{2,1,0:T(8,128)(2,1)S(1)}, bf16[4,304,128]{2,1,0:T(8,128)(2,1)S(1)}, u32[]{:S(2)}, u32[]{:S(2)}) collective-permute-start(bf16[4,304,128]{2,1,0:T(8,128)(2,1)S(1)} %get-tuple-element.43.refs_2_), channel_id=1, source_target_pairs={{0,3},{1,2},{2,1},{3,0},{4,7},{5,6},{6,5},{7,4},{8,11},{9,10},{10,... | collective-permute-start | bytes 933896 | tf_op jit(solution)/shard_map/ppermute | solution.py:167
  7.3 1.8 %collective-permute-start.4 = (bf16[4,304,128]{2,1,0:T(8,128)(2,1)S(1)}, bf16[4,304,128]{2,1,0:T(8,128)(2,1)S(1)}, u32[]{:S(2)}, u32[]{:S(2)}) collective-permute-start(bf16[4,304,128]{2,1,0:T(8,128)(2,1)S(1)} %get-tuple-element.48), channel_id=1, source_target_pairs={{0,5},{1,4},{2,7},{3,6},{4,1},{5,0},{6,3},{7,2},{8,13},{9,12},{10,... | collective-permute-start | bytes 933896 | tf_op jit(solution)/shard_map/ppermute | solution.py:167
  9.1 3.6 %collective-permute-start = (bf16[4,152,128]{2,1,0:T(8,128)(2,1)S(1)}, bf16[4,152,128]{2,1,0:T(8,128)(2,1)S(1)}, u32[]{:S(2)}, u32[]{:S(2)}) collective-permute-start(bf16[4,152,128]{2,1,0:T(8,128)(2,1)S(1)} %shard_map.37.refs_2_), channel_id=1, source_target_pairs={{0,24},{1,25},{2,26},{3,27},{4,28},{5,29},{6,30},{7,31},{8,16},{9,... | collective-permute-start | bytes 466952 | tf_op jit(solution)/shard_map/ppermute | solution.py:167
  12.7 0.0 collective-permute-start.1
  12.7 1.7 %shard_map.40 = (bf16[4,304,128]{2,1,0:T(8,128)(2,1)S(1)}, bf16[4,304,128]{2,1,0:T(8,128)(2,1)S(1)}) custom-call(s32[1]{0:T(128)} %bitcast.refs_0_, bf16[32,1,32,1200]{3,2,1,0:T(8,128)(2,1)} %refs_1_.9, bf16[4,304,128]{2,1,0:T(8,128)(2,1)S(1)} %get-tuple-element.43.refs_2_), custom_call_target="tpu_custom_call" | custom-call | bytes 1228800 | tf_op jit(solution)/shard_map/pallas_call | solution.py:47
  14.4 0.0 copy-start
  14.4 0.5 collective-permute-start.8
  14.9 0.1 collective-permute-done.3.refs_0_
  15.0 3.1 %collective-permute-start.9 = (bf16[4,304,128]{2,1,0:T(8,128)(2,1)S(1)}, bf16[4,304,128]{2,1,0:T(8,128)(2,1)S(1)}, u32[]{:S(2)}, u32[]{:S(2)}) collective-permute-start(bf16[4,304,128]{2,1,0:T(8,128)(2,1)S(1)} %get-tuple-element.55), channel_id=1, source_target_pairs={{0,7},{1,6},{2,5},{3,4},{4,3},{5,2},{6,1},{7,0},{8,15},{9,14},{10,... | collective-permute-start | bytes 933896 | tf_op jit(solution)/shard_map/ppermute | solution.py:167
  18.1 11.2 %collective-permute-done.4.refs_1_ = bf16[4,304,128]{2,1,0:T(8,128)(2,1)S(1)} collective-permute-done((bf16[4,304,128]{2,1,0:T(8,128)(2,1)S(1)}, bf16[4,304,128]{2,1,0:T(8,128)(2,1)S(1)}, u32[]{:S(2)}, u32[]{:S(2)}) %collective-permute-start.4) | collective-permute-done | bytes 311328 | tf_op jit(solution)/shard_map/ppermute | solution.py:167
  29.3 1.5 %collective-permute-start.2 = (bf16[4,152,128]{2,1,0:T(8,128)(2,1)S(1)}, bf16[4,152,128]{2,1,0:T(8,128)(2,1)S(1)}, u32[]{:S(2)}, u32[]{:S(2)}) collective-permute-start(bf16[4,152,128]{2,1,0:T(8,128)(2,1)S(1)} %get-tuple-element.47), channel_id=1, source_target_pairs={{0,8},{1,9},{2,10},{3,11},{4,12},{5,13},{6,14},{7,15},{8,0},{9,1},... | collective-permute-start | bytes 466952 | tf_op jit(solution)/shard_map/ppermute | solution.py:167
  30.9 1.2 %shard_map.41 = (bf16[8,16,1200]{2,1,0:T(8,128)(2,1)S(1)}, bf16[8,16,1200]{2,1,0:T(8,128)(2,1)S(1)}) custom-call(s32[1]{0:T(128)} %bitcast.refs_0_, bf16[32,1,32,1200]{3,2,1,0:T(8,128)(2,1)} %refs_1_.9, bf16[4,304,128]{2,1,0:T(8,128)(2,1)S(1)} %get-tuple-element.44.refs_2_), custom_call_target="tpu_custom_call" | custom-call | bytes 1228800 | tf_op jit(solution)/shard_map/pallas_call | solution.py:47
  32.1 0.0 collective-permute-done.1.refs_2_
  32.2 2.4 %collective-permute-done.2.refs_3_ = bf16[4,152,128]{2,1,0:T(8,128)(2,1)S(1)} collective-permute-done((bf16[4,152,128]{2,1,0:T(8,128)(2,1)S(1)}, bf16[4,152,128]{2,1,0:T(8,128)(2,1)S(1)}, u32[]{:S(2)}, u32[]{:S(2)}) %collective-permute-start.2) | collective-permute-done | bytes 155680 | tf_op jit(solution)/shard_map/ppermute | solution.py:167
  34.6 0.1 collective-permute-start.5
  34.7 0.1 collective-permute-start.6
  34.8 2.7 %collective-permute-start.7 = (bf16[4,152,128]{2,1,0:T(8,128)(2,1)S(1)}, bf16[4,152,128]{2,1,0:T(8,128)(2,1)S(1)}, u32[]{:S(2)}, u32[]{:S(2)}) collective-permute-start(bf16[4,152,128]{2,1,0:T(8,128)(2,1)S(1)} %get-tuple-element.54), channel_id=1, source_target_pairs={{0,4},{1,5},{2,6},{3,7},{4,0},{5,1},{6,2},{7,3},{8,12},{9,13},{10,... | collective-permute-start | bytes 466952 | tf_op jit(solution)/shard_map/ppermute | solution.py:167
  37.5 3.9 %collective-permute-start.12 = (bf16[2,304,128]{2,1,0:T(8,128)(2,1)S(1)}, bf16[2,304,128]{2,1,0:T(8,128)(2,1)S(1)}, u32[]{:S(2)}, u32[]{:S(2)}) collective-permute-start(bf16[2,304,128]{2,1,0:T(8,128)(2,1)S(1)} %get-tuple-element.59), channel_id=1, source_target_pairs={{0,24},{1,25},{2,26},{3,27},{4,28},{5,29},{6,30},{7,31},{8,16},{9,... | collective-permute-start | bytes 466952 | tf_op jit(solution)/shard_map/ppermute | solution.py:167
  41.5 0.7 collective-permute-start.14
  42.2 1.3 %shard_map.45 = (bf16[4,152,128]{2,1,0:T(8,128)(2,1)S(1)}, bf16[4,152,128]{2,1,0:T(8,128)(2,1)S(1)}, bf16[4,152,128]{2,1,0:T(8,128)(2,1)S(1)}, bf16[4,152,128]{2,1,0:T(8,128)(2,1)S(1)}) custom-call(bf16[4,152,128]{2,1,0:T(8,128)(2,1)S(1)} %get-tuple-element.51.refs_2_.refs_0_, bf16[4,152,128]{2,1,0:T(8,128)(2,1)S(1)} %collective-permute-done.5.refs_1_, ...), custom_call_target="tpu_custom_call" | custom-call | flops 737280000 | bytes 2880000 | tf_op jit(solution)/shard_map/pallas_call | solution.py:47
  43.5 0.1 collective-permute-start.15
  43.5 3.8 %collective-permute-start.18 = (bf16[2,304,128]{2,1,0:T(8,128)(2,1)S(1)}, bf16[2,304,128]{2,1,0:T(8,128)(2,1)S(1)}, u32[]{:S(2)}, u32[]{:S(2)}) collective-permute-start(bf16[2,304,128]{2,1,0:T(8,128)(2,1)S(1)} %get-tuple-element.67), channel_id=1, source_target_pairs={{0,24},{1,25},{2,26},{3,27},{4,28},{5,29},{6,30},{7,31},{8,16},{9,... | collective-permute-start | bytes 466952 | tf_op jit(solution)/shard_map/ppermute | solution.py:167
  47.4 6.3 %collective-permute-start.19 = (bf16[2,304,128]{2,1,0:T(8,128)(2,1)S(1)}, bf16[2,304,128]{2,1,0:T(8,128)(2,1)S(1)}, u32[]{:S(2)}, u32[]{:S(2)}) collective-permute-start(bf16[2,304,128]{2,1,0:T(8,128)(2,1)S(1)} %get-tuple-element.68), channel_id=1, source_target_pairs={{0,16},{1,17},{2,18},{3,19},{4,20},{5,21},{6,22},{7,23},{8,24},{9,... | collective-permute-start | bytes 466952 | tf_op jit(solution)/shard_map/ppermute | solution.py:167
  53.7 8.7 %collective-permute-done.13.refs_2_ = bf16[2,304,128]{2,1,0:T(8,128)(2,1)S(1)} collective-permute-done((bf16[2,304,128]{2,1,0:T(8,128)(2,1)S(1)}, bf16[2,304,128]{2,1,0:T(8,128)(2,1)S(1)}, u32[]{:S(2)}, u32[]{:S(2)}) %collective-permute-start.13) | collective-permute-done | bytes 155680 | tf_op jit(solution)/shard_map/ppermute | solution.py:167
  62.4 1.8 %collective-permute-start.10 = (bf16[4,152,128]{2,1,0:T(8,128)(2,1)S(1)}, bf16[4,152,128]{2,1,0:T(8,128)(2,1)S(1)}, u32[]{:S(2)}, u32[]{:S(2)}) collective-permute-start(bf16[4,152,128]{2,1,0:T(8,128)(2,1)S(1)} %get-tuple-element.57), channel_id=1, source_target_pairs={{0,2},{1,3},{2,0},{3,1},{4,6},{5,7},{6,4},{7,5},{8,10},{9,11},{10,... | collective-permute-start | bytes 466952 | tf_op jit(solution)/shard_map/ppermute | solution.py:167
  64.2 0.2 collective-permute-start.11
  64.4 2.3 %collective-permute-start.26 = (bf16[2,152,128]{2,1,0:T(8,128)(2,1)S(1)}, bf16[2,152,128]{2,1,0:T(8,128)(2,1)S(1)}, u32[]{:S(2)}, u32[]{:S(2)}) collective-permute-start(bf16[2,152,128]{2,1,0:T(8,128)(2,1)S(1)} %get-tuple-element.76), channel_id=1, source_target_pairs={{0,24},{1,25},{2,26},{3,27},{4,28},{5,29},{6,30},{7,31},{8,16},{9,... | collective-permute-start | bytes 233480 | tf_op jit(solution)/shard_map/ppermute | solution.py:167
  66.7 1.6 %shard_map.47 = (f32[8,128]{1,0:T(8,128)S(1)}, f32[8,128]{1,0:T(8,128)S(1)}) custom-call(bf16[2,304,128]{2,1,0:T(8,128)(2,1)S(1)} %get-tuple-element.50.refs_4_.refs_0_, bf16[2,304,128]{2,1,0:T(8,128)(2,1)S(1)} %collective-permute-done.12.refs_1_, bf16[2,304,128]{2,1,0:T(8,128)(2,1)S(1)} %collective-permute-done.13.refs_2_, ...), custom_call_target="tpu_custom_call" | custom-call | flops 368640000 | bytes 2880000 | tf_op jit(solution)/shard_map/pallas_call | solution.py:47
  68.3 1.6 %collective-permute-done.19.refs_2_ = bf16[2,304,128]{2,1,0:T(8,128)(2,1)S(1)} collective-permute-done((bf16[2,304,128]{2,1,0:T(8,128)(2,1)S(1)}, bf16[2,304,128]{2,1,0:T(8,128)(2,1)S(1)}, u32[]{:S(2)}, u32[]{:S(2)}) %collective-permute-start.19) | collective-permute-done | bytes 155680 | tf_op jit(solution)/shard_map/ppermute | solution.py:167
  69.9 1.8 %collective-permute-done.20.refs_3_ = bf16[2,304,128]{2,1,0:T(8,128)(2,1)S(1)} collective-permute-done((bf16[2,304,128]{2,1,0:T(8,128)(2,1)S(1)}, bf16[2,304,128]{2,1,0:T(8,128)(2,1)S(1)}, u32[]{:S(2)}, u32[]{:S(2)}) %collective-permute-start.20) | collective-permute-done | bytes 155680 | tf_op jit(solution)/shard_map/ppermute | solution.py:167
  71.7 1.6 %shard_map.48 = (f32[8,128]{1,0:T(8,128)S(1)}, f32[8,128]{1,0:T(8,128)S(1)}) custom-call(bf16[2,304,128]{2,1,0:T(8,128)(2,1)S(1)} %get-tuple-element.56.refs_5_.refs_0_, bf16[2,304,128]{2,1,0:T(8,128)(2,1)S(1)} %collective-permute-done.18.refs_1_, bf16[2,304,128]{2,1,0:T(8,128)(2,1)S(1)} %collective-permute-done.19.refs_2_, ...), custom_call_target="tpu_custom_call" | custom-call | flops 368640000 | bytes 2880000 | tf_op jit(solution)/shard_map/pallas_call | solution.py:47
  73.3 1.6 %collective-permute-start.21 = (f32[8,128]{1,0:T(8,128)S(1)}, f32[8,128]{1,0:T(8,128)S(1)}, u32[]{:S(2)}, u32[]{:S(2)}) collective-permute-start(f32[8,128]{1,0:T(8,128)S(1)} %get-tuple-element.70), channel_id=1, source_target_pairs={{0,6},{1,7},{2,4},{3,5},{4,2},{5,3},{6,0},{7,1},{8,14},{9,15},{10,... | collective-permute-start | bytes 12296 | tf_op jit(solution)/shard_map/ppermute | solution.py:167
  74.9 1.6 %collective-permute-start.22 = (f32[8,128]{1,0:T(8,128)S(1)}, f32[8,128]{1,0:T(8,128)S(1)}, u32[]{:S(2)}, u32[]{:S(2)}) collective-permute-start(f32[8,128]{1,0:T(8,128)S(1)} %get-tuple-element.71), channel_id=1, source_target_pairs={{0,7},{1,6},{2,5},{3,4},{4,3},{5,2},{6,1},{7,0},{8,15},{9,14},{10,... | collective-permute-start | bytes 12296 | tf_op jit(solution)/shard_map/ppermute | solution.py:167
  76.5 1.4 %collective-permute-done.21.refs_4_ = f32[8,128]{1,0:T(8,128)S(1)} collective-permute-done((f32[8,128]{1,0:T(8,128)S(1)}, f32[8,128]{1,0:T(8,128)S(1)}, u32[]{:S(2)}, u32[]{:S(2)}) %collective-permute-start.21) | collective-permute-done | bytes 4128 | tf_op jit(solution)/shard_map/ppermute | solution.py:167
  77.9 1.0 %collective-permute-done.22.refs_5_ = f32[8,128]{1,0:T(8,128)S(1)} collective-permute-done((f32[8,128]{1,0:T(8,128)S(1)}, f32[8,128]{1,0:T(8,128)S(1)}, u32[]{:S(2)}, u32[]{:S(2)}) %collective-permute-start.22) | collective-permute-done | bytes 4128 | tf_op jit(solution)/shard_map/ppermute | solution.py:167
  78.9 0.1 shard_map.49
  79.0 2.1 %collective-permute-start.23 = (bf16[312,128]{1,0:T(8,128)(2,1)S(1)}, bf16[312,128]{1,0:T(8,128)(2,1)S(1)}, u32[]{:S(2)}, u32[]{:S(2)}) collective-permute-start(bf16[312,128]{1,0:T(8,128)(2,1)S(1)} %get-tuple-element.73), channel_id=1, source_target_pairs={{0,24},{1,25},{2,26},{3,27},{4,28},{5,29},{6,30},{7,31},{8,16},{9,... | collective-permute-start | bytes 239624 | tf_op jit(solution)/shard_map/ppermute | solution.py:167
  81.1 2.2 %collective-permute-start.25 = (bf16[312,128]{1,0:T(8,128)(2,1)S(1)}, bf16[312,128]{1,0:T(8,128)(2,1)S(1)}, u32[]{:S(2)}, u32[]{:S(2)}) collective-permute-start(bf16[312,128]{1,0:T(8,128)(2,1)S(1)} %get-tuple-element.75), channel_id=1, source_target_pairs={{0,8},{1,9},{2,10},{3,11},{4,12},{5,13},{6,14},{7,15},{8,0},{9,1},... | collective-permute-start | bytes 239624 | tf_op jit(solution)/shard_map/ppermute | solution.py:167
  83.4 0.7 collective-permute-start.27
  84.1 2.0 %collective-permute-start.28 = (bf16[2,152,128]{2,1,0:T(8,128)(2,1)S(1)}, bf16[2,152,128]{2,1,0:T(8,128)(2,1)S(1)}, u32[]{:S(2)}, u32[]{:S(2)}) collective-permute-start(bf16[2,152,128]{2,1,0:T(8,128)(2,1)S(1)} %get-tuple-element.78), channel_id=1, source_target_pairs={{0,8},{1,9},{2,10},{3,11},{4,12},{5,13},{6,14},{7,15},{8,0},{9,1},... | collective-permute-start | bytes 233480 | tf_op jit(solution)/shard_map/ppermute | solution.py:167
  86.1 0.1 copy.4.refs_7_
  86.2 6.6 %collective-permute-done.27.refs_4_ = bf16[2,152,128]{2,1,0:T(8,128)(2,1)S(1)} collective-permute-done((bf16[2,152,128]{2,1,0:T(8,128)(2,1)S(1)}, bf16[2,152,128]{2,1,0:T(8,128)(2,1)S(1)}, u32[]{:S(2)}, u32[]{:S(2)}) %collective-permute-start.27) | collective-permute-done | bytes 77856 | tf_op jit(solution)/shard_map/ppermute | solution.py:167
  92.8 0.5 shard_map.50.refs_6_
  93.4 0.0 collective-permute-done.24.refs_4_
  93.4 1.2 %shard_map.51 = bf16[32,256]{1,0:T(8,128)(2,1)} custom-call(s32[1]{0:T(128)} %bitcast.refs_0_, bf16[8,16,1200]{2,1,0:T(8,128)(2,1)S(1)} %get-tuple-element.45.refs_1_, bf16[312,128]{1,0:T(8,128)(2,1)S(1)} %get-tuple-element.72.refs_6_.refs_2_, bf16[312,128]{1,0:T(8,128)(2,1)S(1)} %collective-permute-done.23.refs_3_, ...), custom_call_target="tpu_custom_call" | custom-call | flops 9830400 | bytes 1228800 | tf_op jit(solution)/shard_map/pallas_call | solution.py:47
  (30 shorter events, 0.2 us)
Async XLA Ops:
  4.8 10.2 %collective-permute-start.3 = (bf16[4,304,128]{2,1,0:T(8,128)(2,1)S(1)}, bf16[4,304,128]{2,1,0:T(8,128)(2,1)S(1)}, u32[]{:S(2)}, u32[]{:S(2)}) collective-permute-start(bf16[4,304,128]{2,1,0:T(8,128)(2,1)S(1)} %get-tuple-element.43.refs_2_), channel_id=1, source_target_pairs={{0,3},{1,2},{2,1},{3,0},{4,7},{5,6},{6,5},{7,4},{8,11},{9,10},{10,... | collective-permute-start | bytes 933896 | tf_op jit(solution)/shard_map/ppermute | solution.py:167
  7.3 22.1 %collective-permute-start.4 = (bf16[4,304,128]{2,1,0:T(8,128)(2,1)S(1)}, bf16[4,304,128]{2,1,0:T(8,128)(2,1)S(1)}, u32[]{:S(2)}, u32[]{:S(2)}) collective-permute-start(bf16[4,304,128]{2,1,0:T(8,128)(2,1)S(1)} %get-tuple-element.48), channel_id=1, source_target_pairs={{0,5},{1,4},{2,7},{3,6},{4,1},{5,0},{6,3},{7,2},{8,13},{9,12},{10,... | collective-permute-start | bytes 933896 | tf_op jit(solution)/shard_map/ppermute | solution.py:167
  9.1 23.1 %collective-permute-start = (bf16[4,152,128]{2,1,0:T(8,128)(2,1)S(1)}, bf16[4,152,128]{2,1,0:T(8,128)(2,1)S(1)}, u32[]{:S(2)}, u32[]{:S(2)}) collective-permute-start(bf16[4,152,128]{2,1,0:T(8,128)(2,1)S(1)} %shard_map.37.refs_2_), channel_id=1, source_target_pairs={{0,24},{1,25},{2,26},{3,27},{4,28},{5,29},{6,30},{7,31},{8,16},{9,... | collective-permute-start | bytes 466952 | tf_op jit(solution)/shard_map/ppermute | solution.py:167
  12.7 19.5 %collective-permute-start.1 = (bf16[4,152,128]{2,1,0:T(8,128)(2,1)S(1)}, bf16[4,152,128]{2,1,0:T(8,128)(2,1)S(1)}, u32[]{:S(2)}, u32[]{:S(2)}) collective-permute-start(bf16[4,152,128]{2,1,0:T(8,128)(2,1)S(1)} %get-tuple-element.42.refs_2_), channel_id=1, source_target_pairs={{0,16},{1,17},{2,18},{3,19},{4,20},{5,21},{6,22},{7,23},{8,24},{9,... | collective-permute-start | bytes 466952 | tf_op jit(solution)/shard_map/ppermute | solution.py:167
  14.4 27.8 %copy-start = (bf16[1,1200,1200]{2,1,0:T(8,128)(2,1)S(1)}, bf16[1,1200,1200]{2,1,0:T(8,128)(2,1)}, u32[]{:S(2)}) copy-start(bf16[1,1200,1200]{2,1,0:T(8,128)(2,1)} %refs_4_.5) | copy-start | bytes 8640004
  14.4 23.1 %collective-permute-start.8 = (bf16[4,304,128]{2,1,0:T(8,128)(2,1)S(1)}, bf16[4,304,128]{2,1,0:T(8,128)(2,1)S(1)}, u32[]{:S(2)}, u32[]{:S(2)}) collective-permute-start(bf16[4,304,128]{2,1,0:T(8,128)(2,1)S(1)} %get-tuple-element.44.refs_2_), channel_id=1, source_target_pairs={{0,6},{1,7},{2,4},{3,5},{4,2},{5,3},{6,0},{7,1},{8,14},{9,15},{10,... | collective-permute-start | bytes 933896 | tf_op jit(solution)/shard_map/ppermute | solution.py:167
  15.0 26.4 %collective-permute-start.9 = (bf16[4,304,128]{2,1,0:T(8,128)(2,1)S(1)}, bf16[4,304,128]{2,1,0:T(8,128)(2,1)S(1)}, u32[]{:S(2)}, u32[]{:S(2)}) collective-permute-start(bf16[4,304,128]{2,1,0:T(8,128)(2,1)S(1)} %get-tuple-element.55), channel_id=1, source_target_pairs={{0,7},{1,6},{2,5},{3,4},{4,3},{5,2},{6,1},{7,0},{8,15},{9,14},{10,... | collective-permute-start | bytes 933896 | tf_op jit(solution)/shard_map/ppermute | solution.py:167
  29.3 5.2 %collective-permute-start.2 = (bf16[4,152,128]{2,1,0:T(8,128)(2,1)S(1)}, bf16[4,152,128]{2,1,0:T(8,128)(2,1)S(1)}, u32[]{:S(2)}, u32[]{:S(2)}) collective-permute-start(bf16[4,152,128]{2,1,0:T(8,128)(2,1)S(1)} %get-tuple-element.47), channel_id=1, source_target_pairs={{0,8},{1,9},{2,10},{3,11},{4,12},{5,13},{6,14},{7,15},{8,0},{9,1},... | collective-permute-start | bytes 466952 | tf_op jit(solution)/shard_map/ppermute | solution.py:167
  34.6 6.9 %collective-permute-start.5 = (bf16[4,152,128]{2,1,0:T(8,128)(2,1)S(1)}, bf16[4,152,128]{2,1,0:T(8,128)(2,1)S(1)}, u32[]{:S(2)}, u32[]{:S(2)}) collective-permute-start(bf16[4,152,128]{2,1,0:T(8,128)(2,1)S(1)} %get-tuple-element.52), channel_id=1, source_target_pairs={{0,1},{1,0},{2,3},{3,2},{4,5},{5,4},{6,7},{7,6},{8,9},{9,8},{10,11... | collective-permute-start | bytes 466952 | tf_op jit(solution)/shard_map/ppermute | solution.py:167
  34.7 7.5 %collective-permute-start.6 = (bf16[4,152,128]{2,1,0:T(8,128)(2,1)S(1)}, bf16[4,152,128]{2,1,0:T(8,128)(2,1)S(1)}, u32[]{:S(2)}, u32[]{:S(2)}) collective-permute-start(bf16[4,152,128]{2,1,0:T(8,128)(2,1)S(1)} %get-tuple-element.53), channel_id=1, source_target_pairs={{0,2},{1,3},{2,0},{3,1},{4,6},{5,7},{6,4},{7,5},{8,10},{9,11},{10,... | collective-permute-start | bytes 466952 | tf_op jit(solution)/shard_map/ppermute | solution.py:167
  34.8 7.4 %collective-permute-start.7 = (bf16[4,152,128]{2,1,0:T(8,128)(2,1)S(1)}, bf16[4,152,128]{2,1,0:T(8,128)(2,1)S(1)}, u32[]{:S(2)}, u32[]{:S(2)}) collective-permute-start(bf16[4,152,128]{2,1,0:T(8,128)(2,1)S(1)} %get-tuple-element.54), channel_id=1, source_target_pairs={{0,4},{1,5},{2,6},{3,7},{4,0},{5,1},{6,2},{7,3},{8,12},{9,13},{10,... | collective-permute-start | bytes 466952 | tf_op jit(solution)/shard_map/ppermute | solution.py:167
  37.5 9.9 %collective-permute-start.12 = (bf16[2,304,128]{2,1,0:T(8,128)(2,1)S(1)}, bf16[2,304,128]{2,1,0:T(8,128)(2,1)S(1)}, u32[]{:S(2)}, u32[]{:S(2)}) collective-permute-start(bf16[2,304,128]{2,1,0:T(8,128)(2,1)S(1)} %get-tuple-element.59), channel_id=1, source_target_pairs={{0,24},{1,25},{2,26},{3,27},{4,28},{5,29},{6,30},{7,31},{8,16},{9,... | collective-permute-start | bytes 466952 | tf_op jit(solution)/shard_map/ppermute | solution.py:167
  41.4 21.0 %collective-permute-start.13 = (bf16[2,304,128]{2,1,0:T(8,128)(2,1)S(1)}, bf16[2,304,128]{2,1,0:T(8,128)(2,1)S(1)}, u32[]{:S(2)}, u32[]{:S(2)}) collective-permute-start(bf16[2,304,128]{2,1,0:T(8,128)(2,1)S(1)} %get-tuple-element.60), channel_id=1, source_target_pairs={{0,16},{1,17},{2,18},{3,19},{4,20},{5,21},{6,22},{7,23},{8,24},{9,... | collective-permute-start | bytes 466952 | tf_op jit(solution)/shard_map/ppermute | solution.py:167
  41.5 20.9 %collective-permute-start.14 = (bf16[2,304,128]{2,1,0:T(8,128)(2,1)S(1)}, bf16[2,304,128]{2,1,0:T(8,128)(2,1)S(1)}, u32[]{:S(2)}, u32[]{:S(2)}) collective-permute-start(bf16[2,304,128]{2,1,0:T(8,128)(2,1)S(1)} %get-tuple-element.61), channel_id=1, source_target_pairs={{0,8},{1,9},{2,10},{3,11},{4,12},{5,13},{6,14},{7,15},{8,0},{9,1},... | collective-permute-start | bytes 466952 | tf_op jit(solution)/shard_map/ppermute | solution.py:167
  43.5 20.7 %collective-permute-start.15 = (bf16[4,152,128]{2,1,0:T(8,128)(2,1)S(1)}, bf16[4,152,128]{2,1,0:T(8,128)(2,1)S(1)}, u32[]{:S(2)}, u32[]{:S(2)}) collective-permute-start(bf16[4,152,128]{2,1,0:T(8,128)(2,1)S(1)} %get-tuple-element.63), channel_id=1, source_target_pairs={{0,1},{1,0},{2,3},{3,2},{4,5},{5,4},{6,7},{7,6},{8,9},{9,8},{10,11... | collective-permute-start | bytes 466952 | tf_op jit(solution)/shard_map/ppermute | solution.py:167
  43.5 20.9 %collective-permute-start.18 = (bf16[2,304,128]{2,1,0:T(8,128)(2,1)S(1)}, bf16[2,304,128]{2,1,0:T(8,128)(2,1)S(1)}, u32[]{:S(2)}, u32[]{:S(2)}) collective-permute-start(bf16[2,304,128]{2,1,0:T(8,128)(2,1)S(1)} %get-tuple-element.67), channel_id=1, source_target_pairs={{0,24},{1,25},{2,26},{3,27},{4,28},{5,29},{6,30},{7,31},{8,16},{9,... | collective-permute-start | bytes 466952 | tf_op jit(solution)/shard_map/ppermute | solution.py:167
  47.4 22.5 %collective-permute-start.19 = (bf16[2,304,128]{2,1,0:T(8,128)(2,1)S(1)}, bf16[2,304,128]{2,1,0:T(8,128)(2,1)S(1)}, u32[]{:S(2)}, u32[]{:S(2)}) collective-permute-start(bf16[2,304,128]{2,1,0:T(8,128)(2,1)S(1)} %get-tuple-element.68), channel_id=1, source_target_pairs={{0,16},{1,17},{2,18},{3,19},{4,20},{5,21},{6,22},{7,23},{8,24},{9,... | collective-permute-start | bytes 466952 | tf_op jit(solution)/shard_map/ppermute | solution.py:167
  62.4 9.3 %collective-permute-start.20 = (bf16[2,304,128]{2,1,0:T(8,128)(2,1)S(1)}, bf16[2,304,128]{2,1,0:T(8,128)(2,1)S(1)}, u32[]{:S(2)}, u32[]{:S(2)}) collective-permute-start(bf16[2,304,128]{2,1,0:T(8,128)(2,1)S(1)} %get-tuple-element.69), channel_id=1, source_target_pairs={{0,8},{1,9},{2,10},{3,11},{4,12},{5,13},{6,14},{7,15},{8,0},{9,1},... | collective-permute-start | bytes 466952 | tf_op jit(solution)/shard_map/ppermute | solution.py:167
  62.4 10.9 %collective-permute-start.10 = (bf16[4,152,128]{2,1,0:T(8,128)(2,1)S(1)}, bf16[4,152,128]{2,1,0:T(8,128)(2,1)S(1)}, u32[]{:S(2)}, u32[]{:S(2)}) collective-permute-start(bf16[4,152,128]{2,1,0:T(8,128)(2,1)S(1)} %get-tuple-element.57), channel_id=1, source_target_pairs={{0,2},{1,3},{2,0},{3,1},{4,6},{5,7},{6,4},{7,5},{8,10},{9,11},{10,... | collective-permute-start | bytes 466952 | tf_op jit(solution)/shard_map/ppermute | solution.py:167
  64.2 10.7 %collective-permute-start.11 = (bf16[4,152,128]{2,1,0:T(8,128)(2,1)S(1)}, bf16[4,152,128]{2,1,0:T(8,128)(2,1)S(1)}, u32[]{:S(2)}, u32[]{:S(2)}) collective-permute-start(bf16[4,152,128]{2,1,0:T(8,128)(2,1)S(1)} %get-tuple-element.58), channel_id=1, source_target_pairs={{0,4},{1,5},{2,6},{3,7},{4,0},{5,1},{6,2},{7,3},{8,12},{9,13},{10,... | collective-permute-start | bytes 466952 | tf_op jit(solution)/shard_map/ppermute | solution.py:167
  64.4 19.7 %collective-permute-start.26 = (bf16[2,152,128]{2,1,0:T(8,128)(2,1)S(1)}, bf16[2,152,128]{2,1,0:T(8,128)(2,1)S(1)}, u32[]{:S(2)}, u32[]{:S(2)}) collective-permute-start(bf16[2,152,128]{2,1,0:T(8,128)(2,1)S(1)} %get-tuple-element.76), channel_id=1, source_target_pairs={{0,24},{1,25},{2,26},{3,27},{4,28},{5,29},{6,30},{7,31},{8,16},{9,... | collective-permute-start | bytes 233480 | tf_op jit(solution)/shard_map/ppermute | solution.py:167
  66.7 19.4 %copy-start.1 = (s32[32,1]{0,1:T(1,128)S(1)}, s32[32,1]{0,1:T(1,128)}, u32[]{:S(2)}) copy-start(s32[32,1]{0,1:T(1,128)} %param.5) | copy-start | bytes 388
  69.9 6.6 %collective-permute-start.16 = (f32[8,128]{1,0:T(8,128)S(1)}, f32[8,128]{1,0:T(8,128)S(1)}, u32[]{:S(2)}, u32[]{:S(2)}) collective-permute-start(f32[8,128]{1,0:T(8,128)S(1)} %get-tuple-element.65.refs_5_), channel_id=1, source_target_pairs={{0,3},{1,2},{2,1},{3,0},{4,7},{5,6},{6,5},{7,4},{8,11},{9,10},{10,... | collective-permute-start | bytes 12296 | tf_op jit(solution)/shard_map/ppermute | solution.py:167
  71.7 4.9 %collective-permute-start.17 = (f32[8,128]{1,0:T(8,128)S(1)}, f32[8,128]{1,0:T(8,128)S(1)}, u32[]{:S(2)}, u32[]{:S(2)}) collective-permute-start(f32[8,128]{1,0:T(8,128)S(1)} %get-tuple-element.66), channel_id=1, source_target_pairs={{0,5},{1,4},{2,7},{3,6},{4,1},{5,0},{6,3},{7,2},{8,13},{9,12},{10,... | collective-permute-start | bytes 12296 | tf_op jit(solution)/shard_map/ppermute | solution.py:167
  73.3 4.6 %collective-permute-start.21 = (f32[8,128]{1,0:T(8,128)S(1)}, f32[8,128]{1,0:T(8,128)S(1)}, u32[]{:S(2)}, u32[]{:S(2)}) collective-permute-start(f32[8,128]{1,0:T(8,128)S(1)} %get-tuple-element.70), channel_id=1, source_target_pairs={{0,6},{1,7},{2,4},{3,5},{4,2},{5,3},{6,0},{7,1},{8,14},{9,15},{10,... | collective-permute-start | bytes 12296 | tf_op jit(solution)/shard_map/ppermute | solution.py:167
  74.9 3.9 %collective-permute-start.22 = (f32[8,128]{1,0:T(8,128)S(1)}, f32[8,128]{1,0:T(8,128)S(1)}, u32[]{:S(2)}, u32[]{:S(2)}) collective-permute-start(f32[8,128]{1,0:T(8,128)S(1)} %get-tuple-element.71), channel_id=1, source_target_pairs={{0,7},{1,6},{2,5},{3,4},{4,3},{5,2},{6,1},{7,0},{8,15},{9,14},{10,... | collective-permute-start | bytes 12296 | tf_op jit(solution)/shard_map/ppermute | solution.py:167
  79.0 14.4 %collective-permute-start.23 = (bf16[312,128]{1,0:T(8,128)(2,1)S(1)}, bf16[312,128]{1,0:T(8,128)(2,1)S(1)}, u32[]{:S(2)}, u32[]{:S(2)}) collective-permute-start(bf16[312,128]{1,0:T(8,128)(2,1)S(1)} %get-tuple-element.73), channel_id=1, source_target_pairs={{0,24},{1,25},{2,26},{3,27},{4,28},{5,29},{6,30},{7,31},{8,16},{9,... | collective-permute-start | bytes 239624 | tf_op jit(solution)/shard_map/ppermute | solution.py:167
  81.1 12.2 %collective-permute-start.24 = (bf16[312,128]{1,0:T(8,128)(2,1)S(1)}, bf16[312,128]{1,0:T(8,128)(2,1)S(1)}, u32[]{:S(2)}, u32[]{:S(2)}) collective-permute-start(bf16[312,128]{1,0:T(8,128)(2,1)S(1)} %get-tuple-element.74), channel_id=1, source_target_pairs={{0,16},{1,17},{2,18},{3,19},{4,20},{5,21},{6,22},{7,23},{8,24},{9,... | collective-permute-start | bytes 239624 | tf_op jit(solution)/shard_map/ppermute | solution.py:167
  81.1 12.3 %collective-permute-start.25 = (bf16[312,128]{1,0:T(8,128)(2,1)S(1)}, bf16[312,128]{1,0:T(8,128)(2,1)S(1)}, u32[]{:S(2)}, u32[]{:S(2)}) collective-permute-start(bf16[312,128]{1,0:T(8,128)(2,1)S(1)} %get-tuple-element.75), channel_id=1, source_target_pairs={{0,8},{1,9},{2,10},{3,11},{4,12},{5,13},{6,14},{7,15},{8,0},{9,1},... | collective-permute-start | bytes 239624 | tf_op jit(solution)/shard_map/ppermute | solution.py:167
  83.4 9.4 %collective-permute-start.27 = (bf16[2,152,128]{2,1,0:T(8,128)(2,1)S(1)}, bf16[2,152,128]{2,1,0:T(8,128)(2,1)S(1)}, u32[]{:S(2)}, u32[]{:S(2)}) collective-permute-start(bf16[2,152,128]{2,1,0:T(8,128)(2,1)S(1)} %get-tuple-element.77), channel_id=1, source_target_pairs={{0,16},{1,17},{2,18},{3,19},{4,20},{5,21},{6,22},{7,23},{8,24},{9,... | collective-permute-start | bytes 233480 | tf_op jit(solution)/shard_map/ppermute | solution.py:167
  84.1 8.8 %collective-permute-start.28 = (bf16[2,152,128]{2,1,0:T(8,128)(2,1)S(1)}, bf16[2,152,128]{2,1,0:T(8,128)(2,1)S(1)}, u32[]{:S(2)}, u32[]{:S(2)}) collective-permute-start(bf16[2,152,128]{2,1,0:T(8,128)(2,1)S(1)} %get-tuple-element.78), channel_id=1, source_target_pairs={{0,8},{1,9},{2,10},{3,11},{4,12},{5,13},{6,14},{7,15},{8,0},{9,1},... | collective-permute-start | bytes 233480 | tf_op jit(solution)/shard_map/ppermute | solution.py:167

commit v2 on v1

--- a/solution.py
+++ b/solution.py
@@ -146,17 +146,17 @@
     outer, count = split(devices)
     inner = sorted(range(count), key=lambda p: (bin(p).count("1"), p))
     back, there = inner[: count // 2], inner[count // 2 :]
-    half = len(there) // 2
-    return [back[:half], back[half:]], [there[:half], there[half:]], list(range(outer - 1, 0, -1))
+    half, most = len(there) // 2, len(back) * 3 // 4
+    return [back[:most], back[most:]], [there[:half], there[half:]], list(range(outer - 1, 0, -1))
 
 
 def fast(s, densities, weights, live):
     me_arr = lax.axis_index("pb").astype(jnp.int32).reshape(1)
     O, I, N, n = s.outer, s.inner, s.devices, s.pairs
-    backs, groups, far = parts_of(N)
+    backs, (later, sooner), far = parts_of(N)
     order = [0, *far]
-    back, there = backs[0] + backs[1], groups[0] + groups[1]
-    h, g = len(back), len(groups[0])
+    back, there = backs[0] + backs[1], later + sooner
+    h, g = len(back), len(later)
     T = n * n // LANES
     block = n * s.ng
 
@@ -192,21 +192,19 @@
     vb = dict(zip([*far, 0], [*first, *rest]))
     vz = {dz: hop(vb[dz], dz * I) for dz in far}
 
-    def take_cv(index, after):
-        group = groups[index]
-
+    def take_cv(picks, count, after):
         def kernel(me_ref, dens, *refs):
-            outs, (buf, edge, edge2, sem) = refs[:g], refs[g:]
-            offs = [dz * I + p for p in group for dz in order]
+            outs, (buf, edge, edge2, sem) = refs[: len(picks)], refs[len(picks) :]
+            offs = [m for chosen in picks for m in chosen]
             for i, c in enumerate(gather(s, me_ref[0], dens, offs, None, buf, sem)):
                 c.wait()
-                pack(s, reader(s, buf, i, 0, edge), outs[i // O], i % O, 0)
-                pack(s, reader(s, buf, i, n, edge2), outs[i // O], i % O, s.rows)
-
-        k = O * g
+                pack(s, reader(s, buf, i, 0, edge), outs[i // count], i % count, 0)
+                pack(s, reader(s, buf, i, n, edge2), outs[i // count], i % count, s.rows)
+
+        k = len(picks) * count
         return call(
             kernel,
-            [sds(O, 2 * s.rows, LANES)] * g,
+            [sds(count, 2 * s.rows, LANES)] * len(picks),
             (me_arr, densities),
             [SM, HBM],
             [
@@ -235,10 +233,10 @@
             after=after,
         )
 
-    sent0 = take_cv(0, (rest[0],))
-    near0 = [hop(x, p) for x, p in zip(sent0, groups[0])]
-    sent1 = take_cv(1, (sent0[0],))
-    near1 = [hop(x, p) for x, p in zip(sent1, groups[1])]
+    sent = take_cv([[dz * I + p for dz in order] for p in sooner], O, (rest[0],))
+    near = [hop(x, p) for x, p in zip(sent, sooner)]
+    whole = take_cv([[dz * I + p for p in later] for dz in order], g, (sent[0],))
+    azf = [whole[0]] + [hop(x, dz * I) for dz, x in zip(far, whole[1:])]
 
     def take_c(me_ref, dens, *refs):
         outs, sems = refs[:2], refs[2]
@@ -253,21 +251,17 @@
         [sds(O * len(ps), n, s.ng) for ps in backs],
         (me_arr, densities),
         [SM, HBM],
-        [pltpu.SemaphoreType.DMA((2, O * h // 2))],
+        [pltpu.SemaphoreType.DMA((2, O * h))],
         moved=4 * O * h * block,
-        after=(sent1[0],),
+        after=(whole[0],),
     )
 
-    def onward(near, after):
-        parts = regroup([[(j, zi) for j in range(g)] for zi in range(O)], g, 2, near, after)
-        return [parts[0]] + [hop(x, dz * I) for dz, x in zip(far, parts[1:])]
-
-    arrived = [onward(near0, (own_c[0],))]
-
     zs = [vb[0]] + [vz[dz] for dz in far]
-    pieces = regroup([[(zi, j) for zi in range(O)] for j in range(h)], O, 1, zs, (arrived[0][0],))
-    arrived.append(onward(near1, (pieces[0],)))
+    pieces = regroup([[(zi, j) for zi in range(O)] for j in range(h)], O, 1, zs, (own_c[0],))
     vin = [pieces[0]] + [hop(x, p) for x, p in zip(pieces[1:], back[1:])]
+
+    parts = regroup([[(j, zi) for j in range(g)] for zi in range(O)], g, 2, near, (pieces[0],))
+    azn = [parts[0]] + [hop(x, dz * I) for dz, x in zip(far, parts[1:])]
 
     def screen_back(*refs):
         src, w_ref, outs, (v, sc) = refs[:h], refs[h], refs[h + 1 : 2 * h + 1], refs[2 * h + 1 :]
@@ -289,22 +283,25 @@
         [pltpu.VMEM((m_rows, s.ng), BF16), pltpu.VMEM((m_rows, s.wide), BF16)],
         flops=2 * m_rows * s.ng * s.ng,
         moved=2 * s.ng * s.ng,
-        after=(arrived[1][0],),
+        after=(parts[0],),
     )
     sin = [sb[0]] + [hop(x, p) for x, p in zip(sb[1:], back[1:])]
     half = len(backs[0])
-    out0 = regroup([[(j, zi) for j in range(half)] for zi in range(O)], half, 1, sin[:half])
+    mine = regroup([[(zi, j) for zi in range(O)] for j in range(g)], O, 2, azf, (sb[0],))
+    fin = [hop(x, p) for x, p in zip(mine, later)]
+    out0 = regroup([[(j, zi) for j in range(half)] for zi in range(O)], half, 1, sin[:half], (mine[0],))
     sz0 = [out0[0]] + [hop(x, dz * I) for dz, x in zip(far, out0[1:])]
 
-    def blocks_at_owner(index, after):
-        count = O * g
+    def blocks_at_owner(arrived, by_outer, after):
+        count, k = O * g, len(arrived)
 
         def kernel(*refs):
-            src, w_ref, outs, (c, v, sc) = refs[:O], refs[O], refs[O + 1 : O + 1 + g], refs[O + 1 + g :]
+            src, w_ref, outs, (c, v, sc) = refs[:k], refs[k], refs[k + 1 : k + 1 + g], refs[k + 1 + g :]
             for zi in range(O):
                 for j in range(g):
-                    unpack(s, src[zi], j, 0, c, n * (zi * g + j))
-                    unpack(s, src[zi], j, s.rows, v, n * (zi * g + j))
+                    a, b = (zi, j) if by_outer else (j, zi)
+                    unpack(s, src[a], b, 0, c, n * (zi * g + j))
+                    unpack(s, src[a], b, s.rows, v, n * (zi * g + j))
             screen(s, v, w_ref, sc)
             x = spread(s, c[...], sc[:, : s.ng])
             for j in range(g):
@@ -322,8 +319,8 @@
         return call(
             kernel,
             [jax.ShapeDtypeStruct((O * T, LANES), F32)] * g,
-            (*arrived[index], weights),
-            [VM] * (O + 1),
+            (*arrived, weights),
+            [VM] * (k + 1),
             [
                 pltpu.VMEM((n * count, s.ng), BF16),
                 pltpu.VMEM((n * count, s.ng), BF16),
@@ -334,8 +331,8 @@
             after=after,
         )
 
-    done0 = blocks_at_owner(0, (out0[0],))
-    done1 = blocks_at_owner(1, (done0[0],))
+    done0 = blocks_at_owner(fin, False, (out0[0],))
+    done1 = blocks_at_owner(azn, True, (done0[0],))
     returned = [hop(x, p) for x, p in zip([*done0, *done1], there)]
 
     rows2 = len(backs[1]) * s.rows

time: 95 us -> 84.1 us (0.89)
  starting transfers between devices: 45.3 us -> 35 us
    ppermute x29, starting transfers between devices: 45.3 us -> 35 us  [hop(): return lax.ppermute(x, 'pb', [(d, d ^ m) for d in range(N)])]
  transfers between devices with their start and end apart: 29 -> 29, of which waited for: 9 -> 14; matrix products, arithmetic and copies ran while one was open for 0% -> 0% of each run, Pallas kernels for 9% -> 12%
where the time goes in v2:
time: 84.1 us; the launch traced here: 83.8 us
  starting transfers between devices  35 us (42%)
  waiting for transfers between devices  34 us (40%)
  Pallas kernels  14.6 us (17%)
    ppermute x29, starting transfers between devices, hop(): return lax.ppermute(x, 'pb', [(d, d ^ m) for d in range(N)])  35 us
    ppermute x29, waiting for transfers between devices, hop(): return lax.ppermute(x, 'pb', [(d, d ^ m) for d in range(N)])  34 us
    pallas_call x15, Pallas kernels, call(): return pallas(body, outs, specs, a, scratch, flops, moved)(*ins, *after)  14.6 us
  transfers between devices with their start and end apart: 29, of which 14 were waited for; matrix products, arithmetic and copies ran while one was open for 0% of the time, Pallas kernels for 12%

profile of v2, /device:TPU:0, one launch (start us, length us, event | category | flops | bytes accessed | tf_op | source)
XLA Modules:
  0.0 83.8 jit_solution(347894633697159142)
XLA Ops:
  0.0 1.1 %shard_map.37.refs_2_ = bf16[4,152,128]{2,1,0:T(8,128)(2,1)S(1)} custom-call(s32[1]{0:T(128)} %bitcast.refs_0_, bf16[32,1,32,1200]{3,2,1,0:T(8,128)(2,1)} %refs_1_.9), custom_call_target="tpu_custom_call" | custom-call | bytes 307200 | tf_op jit(solution)/shard_map/pallas_call | solution.py:47
  1.2 1.9 %shard_map.38 = (bf16[4,152,128]{2,1,0:T(8,128)(2,1)S(1)}, bf16[4,152,128]{2,1,0:T(8,128)(2,1)S(1)}, bf16[4,152,128]{2,1,0:T(8,128)(2,1)S(1)}) custom-call(s32[1]{0:T(128)} %bitcast.refs_0_, bf16[32,1,32,1200]{3,2,1,0:T(8,128)(2,1)} %refs_1_.9, bf16[4,152,128]{2,1,0:T(8,128)(2,1)S(1)} %shard_map.37.refs_2_), custom_call_target="tpu_custom_call" | custom-call | bytes 921600 | tf_op jit(solution)/shard_map/pallas_call | solution.py:47
  3.1 4.1 %collective-permute-start.1 = (bf16[4,152,128]{2,1,0:T(8,128)(2,1)S(1)}, bf16[4,152,128]{2,1,0:T(8,128)(2,1)S(1)}, u32[]{:S(2)}, u32[]{:S(2)}) collective-permute-start(bf16[4,152,128]{2,1,0:T(8,128)(2,1)S(1)} %get-tuple-element.42.refs_2_), channel_id=1, source_target_pairs={{0,16},{1,17},{2,18},{3,19},{4,20},{5,21},{6,22},{7,23},{8,24},{9,... | collective-permute-start | bytes 466952 | tf_op jit(solution)/shard_map/ppermute | solution.py:167
  7.2 1.6 %collective-permute-start.2 = (bf16[4,152,128]{2,1,0:T(8,128)(2,1)S(1)}, bf16[4,152,128]{2,1,0:T(8,128)(2,1)S(1)}, u32[]{:S(2)}, u32[]{:S(2)}) collective-permute-start(bf16[4,152,128]{2,1,0:T(8,128)(2,1)S(1)} %get-tuple-element.47), channel_id=1, source_target_pairs={{0,8},{1,9},{2,10},{3,11},{4,12},{5,13},{6,14},{7,15},{8,0},{9,1},... | collective-permute-start | bytes 466952 | tf_op jit(solution)/shard_map/ppermute | solution.py:167
  8.8 1.7 %shard_map.39 = (bf16[4,304,128]{2,1,0:T(8,128)(2,1)S(1)}, bf16[4,304,128]{2,1,0:T(8,128)(2,1)S(1)}) custom-call(s32[1]{0:T(128)} %bitcast.refs_0_, bf16[32,1,32,1200]{3,2,1,0:T(8,128)(2,1)} %refs_1_.9, bf16[4,152,128]{2,1,0:T(8,128)(2,1)S(1)} %get-tuple-element.42.refs_2_), custom_call_target="tpu_custom_call" | custom-call | bytes 1228800 | tf_op jit(solution)/shard_map/pallas_call | solution.py:47
  10.5 2.5 %collective-permute-start.6 = (bf16[4,304,128]{2,1,0:T(8,128)(2,1)S(1)}, bf16[4,304,128]{2,1,0:T(8,128)(2,1)S(1)}, u32[]{:S(2)}, u32[]{:S(2)}) collective-permute-start(bf16[4,304,128]{2,1,0:T(8,128)(2,1)S(1)} %get-tuple-element.43.refs_2_), channel_id=1, source_target_pairs={{0,6},{1,7},{2,4},{3,5},{4,2},{5,3},{6,0},{7,1},{8,14},{9,15},{10,... | collective-permute-start | bytes 933896 | tf_op jit(solution)/shard_map/ppermute | solution.py:167
  13.0 0.2 collective-permute-start
  13.2 1.7 %shard_map.40 = (bf16[2,304,128]{2,1,0:T(8,128)(2,1)S(1)}, bf16[2,304,128]{2,1,0:T(8,128)(2,1)S(1)}, bf16[2,304,128]{2,1,0:T(8,128)(2,1)S(1)}, bf16[2,304,128]{2,1,0:T(8,128)(2,1)S(1)}) custom-call(s32[1]{0:T(128)} %bitcast.refs_0_, bf16[32,1,32,1200]{3,2,1,0:T(8,128)(2,1)} %refs_1_.9, bf16[4,304,128]{2,1,0:T(8,128)(2,1)S(1)} %get-tuple-element.43.refs_2_), custom_call_target="tpu_custom_call" | custom-call | bytes 1228800 | tf_op jit(solution)/shard_map/pallas_call | solution.py:47
  14.9 1.5 %shard_map.41 = (bf16[12,16,1200]{2,1,0:T(8,128)(2,1)S(1)}, bf16[4,16,1200]{2,1,0:T(8,128)(2,1)S(1)}) custom-call(s32[1]{0:T(128)} %bitcast.refs_0_, bf16[32,1,32,1200]{3,2,1,0:T(8,128)(2,1)} %refs_1_.9, bf16[2,304,128]{2,1,0:T(8,128)(2,1)S(1)} %get-tuple-element.44.refs_2_.refs_0_), custom_call_target="tpu_custom_call" | custom-call | bytes 1228800 | tf_op jit(solution)/shard_map/pallas_call | solution.py:47
  16.5 3.6 %collective-permute-done.refs_1_ = bf16[4,152,128]{2,1,0:T(8,128)(2,1)S(1)} collective-permute-done((bf16[4,152,128]{2,1,0:T(8,128)(2,1)S(1)}, bf16[4,152,128]{2,1,0:T(8,128)(2,1)S(1)}, u32[]{:S(2)}, u32[]{:S(2)}) %collective-permute-start) | collective-permute-done | bytes 155680 | tf_op jit(solution)/shard_map/ppermute | solution.py:167
  20.2 0.6 collective-permute-start.4
  20.8 1.5 %collective-permute-start.5 = (bf16[4,152,128]{2,1,0:T(8,128)(2,1)S(1)}, bf16[4,152,128]{2,1,0:T(8,128)(2,1)S(1)}, u32[]{:S(2)}, u32[]{:S(2)}) collective-permute-start(bf16[4,152,128]{2,1,0:T(8,128)(2,1)S(1)} %get-tuple-element.52), channel_id=1, source_target_pairs={{0,4},{1,5},{2,6},{3,7},{4,0},{5,1},{6,2},{7,3},{8,12},{9,13},{10,... | collective-permute-start | bytes 466952 | tf_op jit(solution)/shard_map/ppermute | solution.py:167
  22.3 4.8 %collective-permute-start.10 = (bf16[2,304,128]{2,1,0:T(8,128)(2,1)S(1)}, bf16[2,304,128]{2,1,0:T(8,128)(2,1)S(1)}, u32[]{:S(2)}, u32[]{:S(2)}) collective-permute-start(bf16[2,304,128]{2,1,0:T(8,128)(2,1)S(1)} %get-tuple-element.57), channel_id=1, source_target_pairs={{0,16},{1,17},{2,18},{3,19},{4,20},{5,21},{6,22},{7,23},{8,24},{9,... | collective-permute-start | bytes 466952 | tf_op jit(solution)/shard_map/ppermute | solution.py:167
  27.1 0.4 collective-permute-done.7.refs_1_
  27.5 0.4 collective-permute-start.11
  27.9 0.7 collective-permute-start.9
  28.7 1.4 %collective-permute-done.4.refs_2_ = bf16[4,152,128]{2,1,0:T(8,128)(2,1)S(1)} collective-permute-done((bf16[4,152,128]{2,1,0:T(8,128)(2,1)S(1)}, bf16[4,152,128]{2,1,0:T(8,128)(2,1)S(1)}, u32[]{:S(2)}, u32[]{:S(2)}) %collective-permute-start.4) | collective-permute-done | bytes 155680 | tf_op jit(solution)/shard_map/ppermute | solution.py:167
  30.1 1.3 %shard_map.44 = (bf16[4,152,128]{2,1,0:T(8,128)(2,1)S(1)}, bf16[4,152,128]{2,1,0:T(8,128)(2,1)S(1)}, bf16[4,152,128]{2,1,0:T(8,128)(2,1)S(1)}, bf16[4,152,128]{2,1,0:T(8,128)(2,1)S(1)}) custom-call(bf16[4,152,128]{2,1,0:T(8,128)(2,1)S(1)} %get-tuple-element.49.refs_2_.refs_0_, bf16[4,152,128]{2,1,0:T(8,128)(2,1)S(1)} %collective-permute-done.3.refs_1_, ...), custom_call_target="tpu_custom_call" | custom-call | flops 737280000 | bytes 2880000 | tf_op jit(solution)/shard_map/pallas_call | solution.py:47
  31.4 4.4 %collective-permute-done.10.refs_2_ = bf16[2,304,128]{2,1,0:T(8,128)(2,1)S(1)} collective-permute-done((bf16[2,304,128]{2,1,0:T(8,128)(2,1)S(1)}, bf16[2,304,128]{2,1,0:T(8,128)(2,1)S(1)}, u32[]{:S(2)}, u32[]{:S(2)}) %collective-permute-start.10) | collective-permute-done | bytes 155680 | tf_op jit(solution)/shard_map/ppermute | solution.py:167
  35.8 4.5 %collective-permute-done.11.refs_3_ = bf16[2,304,128]{2,1,0:T(8,128)(2,1)S(1)} collective-permute-done((bf16[2,304,128]{2,1,0:T(8,128)(2,1)S(1)}, bf16[2,304,128]{2,1,0:T(8,128)(2,1)S(1)}, u32[]{:S(2)}, u32[]{:S(2)}) %collective-permute-start.11) | collective-permute-done | bytes 155680 | tf_op jit(solution)/shard_map/ppermute | solution.py:167
  40.4 0.1 collective-permute-start.12
  40.5 0.6 collective-permute-start.13
  41.1 1.3 %collective-permute-start.15 = (bf16[4,152,128]{2,1,0:T(8,128)(2,1)S(1)}, bf16[4,152,128]{2,1,0:T(8,128)(2,1)S(1)}, u32[]{:S(2)}, u32[]{:S(2)}) collective-permute-start(bf16[4,152,128]{2,1,0:T(8,128)(2,1)S(1)} %get-tuple-element.63), channel_id=1, source_target_pairs={{0,2},{1,3},{2,0},{3,1},{4,6},{5,7},{6,4},{7,5},{8,10},{9,11},{10,... | collective-permute-start | bytes 466952 | tf_op jit(solution)/shard_map/ppermute | solution.py:167
  42.4 1.4 %collective-permute-start.18 = (bf16[2,304,128]{2,1,0:T(8,128)(2,1)S(1)}, bf16[2,304,128]{2,1,0:T(8,128)(2,1)S(1)}, u32[]{:S(2)}, u32[]{:S(2)}) collective-permute-start(bf16[2,304,128]{2,1,0:T(8,128)(2,1)S(1)} %get-tuple-element.67), channel_id=1, source_target_pairs={{0,24},{1,25},{2,26},{3,27},{4,28},{5,29},{6,30},{7,31},{8,16},{9,... | collective-permute-start | bytes 466952 | tf_op jit(solution)/shard_map/ppermute | solution.py:167
  43.9 1.7 %collective-permute-start.19 = (bf16[2,304,128]{2,1,0:T(8,128)(2,1)S(1)}, bf16[2,304,128]{2,1,0:T(8,128)(2,1)S(1)}, u32[]{:S(2)}, u32[]{:S(2)}) collective-permute-start(bf16[2,304,128]{2,1,0:T(8,128)(2,1)S(1)} %get-tuple-element.68), channel_id=1, source_target_pairs={{0,16},{1,17},{2,18},{3,19},{4,20},{5,21},{6,22},{7,23},{8,24},{9,... | collective-permute-start | bytes 466952 | tf_op jit(solution)/shard_map/ppermute | solution.py:167
  45.6 7.8 %collective-permute-done.15.refs_2_ = bf16[4,152,128]{2,1,0:T(8,128)(2,1)S(1)} collective-permute-done((bf16[4,152,128]{2,1,0:T(8,128)(2,1)S(1)}, bf16[4,152,128]{2,1,0:T(8,128)(2,1)S(1)}, u32[]{:S(2)}, u32[]{:S(2)}) %collective-permute-start.15) | collective-permute-done | bytes 155680 | tf_op jit(solution)/shard_map/ppermute | solution.py:167
  53.4 1.4 %collective-permute-start.20 = (bf16[2,304,128]{2,1,0:T(8,128)(2,1)S(1)}, bf16[2,304,128]{2,1,0:T(8,128)(2,1)S(1)}, u32[]{:S(2)}, u32[]{:S(2)}) collective-permute-start(bf16[2,304,128]{2,1,0:T(8,128)(2,1)S(1)} %get-tuple-element.69), channel_id=1, source_target_pairs={{0,8},{1,9},{2,10},{3,11},{4,12},{5,13},{6,14},{7,15},{8,0},{9,1},... | collective-permute-start | bytes 466952 | tf_op jit(solution)/shard_map/ppermute | solution.py:167
  54.9 0.5 collective-permute-start.8
  55.4 4.3 %collective-permute-done.19.refs_2_ = bf16[2,304,128]{2,1,0:T(8,128)(2,1)S(1)} collective-permute-done((bf16[2,304,128]{2,1,0:T(8,128)(2,1)S(1)}, bf16[2,304,128]{2,1,0:T(8,128)(2,1)S(1)}, u32[]{:S(2)}, u32[]{:S(2)}) %collective-permute-start.19) | collective-permute-done | bytes 155680 | tf_op jit(solution)/shard_map/ppermute | solution.py:167
  59.7 0.7 collective-permute-start.26
  60.4 0.2 collective-permute-start.27
  60.5 3.5 %collective-permute-start.28 = (bf16[3,152,128]{2,1,0:T(8,128)(2,1)S(1)}, bf16[3,152,128]{2,1,0:T(8,128)(2,1)S(1)}, u32[]{:S(2)}, u32[]{:S(2)}) collective-permute-start(bf16[3,152,128]{2,1,0:T(8,128)(2,1)S(1)} %get-tuple-element.78), channel_id=1, source_target_pairs={{0,8},{1,9},{2,10},{3,11},{4,12},{5,13},{6,14},{7,15},{8,0},{9,1},... | collective-permute-start | bytes 350216 | tf_op jit(solution)/shard_map/ppermute | solution.py:167
  64.1 1.6 %shard_map.47 = (f32[8,128]{1,0:T(8,128)S(1)}, f32[8,128]{1,0:T(8,128)S(1)}) custom-call(bf16[4,304,128]{2,1,0:T(8,128)(2,1)S(1)} %collective-permute-done.12.refs_0_, bf16[4,304,128]{2,1,0:T(8,128)(2,1)S(1)} %collective-permute-done.13.refs_1_, bf16[1,1200,1200]{2,1,0:T(8,128)(2,1)S(1)} %copy-done, bf16[3,152,128]{2,1,0:T(8,128)(2,1)S(1)} %get-tuple-element.64.refs_3_.refs_2_), custom_call_target="tpu_custom_call" | custom-call | flops 368640000 | bytes 2880000 | tf_op jit(solution)/shard_map/pallas_call | solution.py:47
  65.7 1.7 %shard_map.48 = (f32[8,128]{1,0:T(8,128)S(1)}, f32[8,128]{1,0:T(8,128)S(1)}) custom-call(bf16[2,304,128]{2,1,0:T(8,128)(2,1)S(1)} %get-tuple-element.54.refs_5_.refs_0_, bf16[2,304,128]{2,1,0:T(8,128)(2,1)S(1)} %collective-permute-done.18.refs_1_, bf16[2,304,128]{2,1,0:T(8,128)(2,1)S(1)} %collective-permute-done.19.refs_2_, ...), custom_call_target="tpu_custom_call" | custom-call | flops 368640000 | bytes 2880000 | tf_op jit(solution)/shard_map/pallas_call | solution.py:47
  67.4 1.6 %collective-permute-start.21 = (f32[8,128]{1,0:T(8,128)S(1)}, f32[8,128]{1,0:T(8,128)S(1)}, u32[]{:S(2)}, u32[]{:S(2)}) collective-permute-start(f32[8,128]{1,0:T(8,128)S(1)} %get-tuple-element.70), channel_id=1, source_target_pairs={{0,6},{1,7},{2,4},{3,5},{4,2},{5,3},{6,0},{7,1},{8,14},{9,15},{10,... | collective-permute-start | bytes 12296 | tf_op jit(solution)/shard_map/ppermute | solution.py:167
  69.0 3.0 %collective-permute-done.21.refs_3_ = f32[8,128]{1,0:T(8,128)S(1)} collective-permute-done((f32[8,128]{1,0:T(8,128)S(1)}, f32[8,128]{1,0:T(8,128)S(1)}, u32[]{:S(2)}, u32[]{:S(2)}) %collective-permute-start.21) | collective-permute-done | bytes 4128 | tf_op jit(solution)/shard_map/ppermute | solution.py:167
  72.0 1.0 %collective-permute-done.22.refs_4_ = f32[8,128]{1,0:T(8,128)S(1)} collective-permute-done((f32[8,128]{1,0:T(8,128)S(1)}, f32[8,128]{1,0:T(8,128)S(1)}, u32[]{:S(2)}, u32[]{:S(2)}) %collective-permute-start.22) | collective-permute-done | bytes 4128 | tf_op jit(solution)/shard_map/ppermute | solution.py:167
  72.9 0.9 %collective-permute-start.17 = (f32[8,128]{1,0:T(8,128)S(1)}, f32[8,128]{1,0:T(8,128)S(1)}, u32[]{:S(2)}, u32[]{:S(2)}) collective-permute-start(f32[8,128]{1,0:T(8,128)S(1)} %get-tuple-element.66), channel_id=1, source_target_pairs={{0,5},{1,4},{2,7},{3,6},{4,1},{5,0},{6,3},{7,2},{8,13},{9,12},{10,... | collective-permute-start | bytes 12296 | tf_op jit(solution)/shard_map/ppermute | solution.py:167
  73.8 1.2 %collective-permute-done.16.refs_1_ = f32[8,128]{1,0:T(8,128)S(1)} collective-permute-done((f32[8,128]{1,0:T(8,128)S(1)}, f32[8,128]{1,0:T(8,128)S(1)}, u32[]{:S(2)}, u32[]{:S(2)}) %collective-permute-start.16) | collective-permute-done | bytes 4128 | tf_op jit(solution)/shard_map/ppermute | solution.py:167
  75.0 1.0 %collective-permute-done.17.refs_2_ = f32[8,128]{1,0:T(8,128)S(1)} collective-permute-done((f32[8,128]{1,0:T(8,128)S(1)}, f32[8,128]{1,0:T(8,128)S(1)}, u32[]{:S(2)}, u32[]{:S(2)}) %collective-permute-start.17) | collective-permute-done | bytes 4128 | tf_op jit(solution)/shard_map/ppermute | solution.py:167
  75.9 0.1 shard_map.49
  76.1 0.7 collective-permute-start.23
  76.8 0.7 collective-permute-start.24
  77.5 2.9 %collective-permute-start.25 = (bf16[160,128]{1,0:T(8,128)(2,1)S(1)}, bf16[160,128]{1,0:T(8,128)(2,1)S(1)}, u32[]{:S(2)}, u32[]{:S(2)}) collective-permute-start(bf16[160,128]{1,0:T(8,128)(2,1)S(1)} %get-tuple-element.75), channel_id=1, source_target_pairs={{0,8},{1,9},{2,10},{3,11},{4,12},{5,13},{6,14},{7,15},{8,0},{9,1},... | collective-permute-start | bytes 122888 | tf_op jit(solution)/shard_map/ppermute | solution.py:167
  80.6 0.6 shard_map.50.refs_6_
  81.2 0.7 collective-permute-done.23.refs_3_
  81.9 0.7 collective-permute-done.24.refs_4_
  82.7 1.1 %shard_map.51 = bf16[32,256]{1,0:T(8,128)(2,1)} custom-call(s32[1]{0:T(128)} %bitcast.refs_0_, bf16[4,16,1200]{2,1,0:T(8,128)(2,1)S(1)} %get-tuple-element.45.refs_1_, bf16[160,128]{1,0:T(8,128)(2,1)S(1)} %get-tuple-element.72.refs_6_.refs_2_, bf16[160,128]{1,0:T(8,128)(2,1)S(1)} %collective-permute-done.23.refs_3_, ...), custom_call_target="tpu_custom_call" | custom-call | flops 9830400 | bytes 1228800 | tf_op jit(solution)/shard_map/pallas_call | solution.py:47
  (30 shorter events, 0.6 us)
Async XLA Ops:
  3.1 13.4 %collective-permute-start.1 = (bf16[4,152,128]{2,1,0:T(8,128)(2,1)S(1)}, bf16[4,152,128]{2,1,0:T(8,128)(2,1)S(1)}, u32[]{:S(2)}, u32[]{:S(2)}) collective-permute-start(bf16[4,152,128]{2,1,0:T(8,128)(2,1)S(1)} %get-tuple-element.42.refs_2_), channel_id=1, source_target_pairs={{0,16},{1,17},{2,18},{3,19},{4,20},{5,21},{6,22},{7,23},{8,24},{9,... | collective-permute-start | bytes 466952 | tf_op jit(solution)/shard_map/ppermute | solution.py:167
  7.2 9.3 %collective-permute-start.2 = (bf16[4,152,128]{2,1,0:T(8,128)(2,1)S(1)}, bf16[4,152,128]{2,1,0:T(8,128)(2,1)S(1)}, u32[]{:S(2)}, u32[]{:S(2)}) collective-permute-start(bf16[4,152,128]{2,1,0:T(8,128)(2,1)S(1)} %get-tuple-element.47), channel_id=1, source_target_pairs={{0,8},{1,9},{2,10},{3,11},{4,12},{5,13},{6,14},{7,15},{8,0},{9,1},... | collective-permute-start | bytes 466952 | tf_op jit(solution)/shard_map/ppermute | solution.py:167
  10.5 11.8 %collective-permute-start.6 = (bf16[4,304,128]{2,1,0:T(8,128)(2,1)S(1)}, bf16[4,304,128]{2,1,0:T(8,128)(2,1)S(1)}, u32[]{:S(2)}, u32[]{:S(2)}) collective-permute-start(bf16[4,304,128]{2,1,0:T(8,128)(2,1)S(1)} %get-tuple-element.43.refs_2_), channel_id=1, source_target_pairs={{0,6},{1,7},{2,4},{3,5},{4,2},{5,3},{6,0},{7,1},{8,14},{9,15},{10,... | collective-permute-start | bytes 933896 | tf_op jit(solution)/shard_map/ppermute | solution.py:167
  13.0 7.0 %collective-permute-start = (bf16[4,152,128]{2,1,0:T(8,128)(2,1)S(1)}, bf16[4,152,128]{2,1,0:T(8,128)(2,1)S(1)}, u32[]{:S(2)}, u32[]{:S(2)}) collective-permute-start(bf16[4,152,128]{2,1,0:T(8,128)(2,1)S(1)} %shard_map.37.refs_2_), channel_id=1, source_target_pairs={{0,24},{1,25},{2,26},{3,27},{4,28},{5,29},{6,30},{7,31},{8,16},{9,... | collective-permute-start | bytes 466952 | tf_op jit(solution)/shard_map/ppermute | solution.py:167
  13.2 14.2 %collective-permute-start.7 = (bf16[4,304,128]{2,1,0:T(8,128)(2,1)S(1)}, bf16[4,304,128]{2,1,0:T(8,128)(2,1)S(1)}, u32[]{:S(2)}, u32[]{:S(2)}) collective-permute-start(bf16[4,304,128]{2,1,0:T(8,128)(2,1)S(1)} %get-tuple-element.53), channel_id=1, source_target_pairs={{0,7},{1,6},{2,5},{3,4},{4,3},{5,2},{6,1},{7,0},{8,15},{9,14},{10,... | collective-permute-start | bytes 933896 | tf_op jit(solution)/shard_map/ppermute | solution.py:167
  14.9 15.1 %copy-start = (bf16[1,1200,1200]{2,1,0:T(8,128)(2,1)S(1)}, bf16[1,1200,1200]{2,1,0:T(8,128)(2,1)}, u32[]{:S(2)}) copy-start(bf16[1,1200,1200]{2,1,0:T(8,128)(2,1)} %refs_4_.3) | copy-start | bytes 8640004
  20.1 7.8 %collective-permute-start.3 = (bf16[4,152,128]{2,1,0:T(8,128)(2,1)S(1)}, bf16[4,152,128]{2,1,0:T(8,128)(2,1)S(1)}, u32[]{:S(2)}, u32[]{:S(2)}) collective-permute-start(bf16[4,152,128]{2,1,0:T(8,128)(2,1)S(1)} %get-tuple-element.50), channel_id=1, source_target_pairs={{0,1},{1,0},{2,3},{3,2},{4,5},{5,4},{6,7},{7,6},{8,9},{9,8},{10,11... | collective-permute-start | bytes 466952 | tf_op jit(solution)/shard_map/ppermute | solution.py:167
  20.2 9.9 %collective-permute-start.4 = (bf16[4,152,128]{2,1,0:T(8,128)(2,1)S(1)}, bf16[4,152,128]{2,1,0:T(8,128)(2,1)S(1)}, u32[]{:S(2)}, u32[]{:S(2)}) collective-permute-start(bf16[4,152,128]{2,1,0:T(8,128)(2,1)S(1)} %get-tuple-element.51), channel_id=1, source_target_pairs={{0,2},{1,3},{2,0},{3,1},{4,6},{5,7},{6,4},{7,5},{8,10},{9,11},{10,... | collective-permute-start | bytes 466952 | tf_op jit(solution)/shard_map/ppermute | solution.py:167
  20.8 9.3 %collective-permute-start.5 = (bf16[4,152,128]{2,1,0:T(8,128)(2,1)S(1)}, bf16[4,152,128]{2,1,0:T(8,128)(2,1)S(1)}, u32[]{:S(2)}, u32[]{:S(2)}) collective-permute-start(bf16[4,152,128]{2,1,0:T(8,128)(2,1)S(1)} %get-tuple-element.52), channel_id=1, source_target_pairs={{0,4},{1,5},{2,6},{3,7},{4,0},{5,1},{6,2},{7,3},{8,12},{9,13},{10,... | collective-permute-start | bytes 466952 | tf_op jit(solution)/shard_map/ppermute | solution.py:167
  22.3 13.5 %collective-permute-start.10 = (bf16[2,304,128]{2,1,0:T(8,128)(2,1)S(1)}, bf16[2,304,128]{2,1,0:T(8,128)(2,1)S(1)}, u32[]{:S(2)}, u32[]{:S(2)}) collective-permute-start(bf16[2,304,128]{2,1,0:T(8,128)(2,1)S(1)} %get-tuple-element.57), channel_id=1, source_target_pairs={{0,16},{1,17},{2,18},{3,19},{4,20},{5,21},{6,22},{7,23},{8,24},{9,... | collective-permute-start | bytes 466952 | tf_op jit(solution)/shard_map/ppermute | solution.py:167
  27.5 12.8 %collective-permute-start.11 = (bf16[2,304,128]{2,1,0:T(8,128)(2,1)S(1)}, bf16[2,304,128]{2,1,0:T(8,128)(2,1)S(1)}, u32[]{:S(2)}, u32[]{:S(2)}) collective-permute-start(bf16[2,304,128]{2,1,0:T(8,128)(2,1)S(1)} %get-tuple-element.58), channel_id=1, source_target_pairs={{0,8},{1,9},{2,10},{3,11},{4,12},{5,13},{6,14},{7,15},{8,0},{9,1},... | collective-permute-start | bytes 466952 | tf_op jit(solution)/shard_map/ppermute | solution.py:167
  27.9 12.4 %collective-permute-start.9 = (bf16[2,304,128]{2,1,0:T(8,128)(2,1)S(1)}, bf16[2,304,128]{2,1,0:T(8,128)(2,1)S(1)}, u32[]{:S(2)}, u32[]{:S(2)}) collective-permute-start(bf16[2,304,128]{2,1,0:T(8,128)(2,1)S(1)} %get-tuple-element.56), channel_id=1, source_target_pairs={{0,24},{1,25},{2,26},{3,27},{4,28},{5,29},{6,30},{7,31},{8,16},{9,... | collective-permute-start | bytes 466952 | tf_op jit(solution)/shard_map/ppermute | solution.py:167
  31.3 12.5 %collective-permute-start.14 = (bf16[4,152,128]{2,1,0:T(8,128)(2,1)S(1)}, bf16[4,152,128]{2,1,0:T(8,128)(2,1)S(1)}, u32[]{:S(2)}, u32[]{:S(2)}) collective-permute-start(bf16[4,152,128]{2,1,0:T(8,128)(2,1)S(1)} %get-tuple-element.62), channel_id=1, source_target_pairs={{0,1},{1,0},{2,3},{3,2},{4,5},{5,4},{6,7},{7,6},{8,9},{9,8},{10,11... | collective-permute-start | bytes 466952 | tf_op jit(solution)/shard_map/ppermute | solution.py:167
  40.4 20.0 %collective-permute-start.12 = (bf16[4,304,128]{2,1,0:T(8,128)(2,1)S(1)}, bf16[4,304,128]{2,1,0:T(8,128)(2,1)S(1)}, u32[]{:S(2)}, u32[]{:S(2)}) collective-permute-start(bf16[4,304,128]{2,1,0:T(8,128)(2,1)S(1)} %get-tuple-element.60.refs_3_), channel_id=1, source_target_pairs={{0,3},{1,2},{2,1},{3,0},{4,7},{5,6},{6,5},{7,4},{8,11},{9,10},{10,... | collective-permute-start | bytes 933896 | tf_op jit(solution)/shard_map/ppermute | solution.py:167
  40.5 20.0 %collective-permute-start.13 = (bf16[4,304,128]{2,1,0:T(8,128)(2,1)S(1)}, bf16[4,304,128]{2,1,0:T(8,128)(2,1)S(1)}, u32[]{:S(2)}, u32[]{:S(2)}) collective-permute-start(bf16[4,304,128]{2,1,0:T(8,128)(2,1)S(1)} %get-tuple-element.61), channel_id=1, source_target_pairs={{0,5},{1,4},{2,7},{3,6},{4,1},{5,0},{6,3},{7,2},{8,13},{9,12},{10,... | collective-permute-start | bytes 933896 | tf_op jit(solution)/shard_map/ppermute | solution.py:167
  41.1 12.3 %collective-permute-start.15 = (bf16[4,152,128]{2,1,0:T(8,128)(2,1)S(1)}, bf16[4,152,128]{2,1,0:T(8,128)(2,1)S(1)}, u32[]{:S(2)}, u32[]{:S(2)}) collective-permute-start(bf16[4,152,128]{2,1,0:T(8,128)(2,1)S(1)} %get-tuple-element.63), channel_id=1, source_target_pairs={{0,2},{1,3},{2,0},{3,1},{4,6},{5,7},{6,4},{7,5},{8,10},{9,11},{10,... | collective-permute-start | bytes 466952 | tf_op jit(solution)/shard_map/ppermute | solution.py:167
  42.4 12.4 %collective-permute-start.18 = (bf16[2,304,128]{2,1,0:T(8,128)(2,1)S(1)}, bf16[2,304,128]{2,1,0:T(8,128)(2,1)S(1)}, u32[]{:S(2)}, u32[]{:S(2)}) collective-permute-start(bf16[2,304,128]{2,1,0:T(8,128)(2,1)S(1)} %get-tuple-element.67), channel_id=1, source_target_pairs={{0,24},{1,25},{2,26},{3,27},{4,28},{5,29},{6,30},{7,31},{8,16},{9,... | collective-permute-start | bytes 466952 | tf_op jit(solution)/shard_map/ppermute | solution.py:167
  43.9 15.8 %collective-permute-start.19 = (bf16[2,304,128]{2,1,0:T(8,128)(2,1)S(1)}, bf16[2,304,128]{2,1,0:T(8,128)(2,1)S(1)}, u32[]{:S(2)}, u32[]{:S(2)}) collective-permute-start(bf16[2,304,128]{2,1,0:T(8,128)(2,1)S(1)} %get-tuple-element.68), channel_id=1, source_target_pairs={{0,16},{1,17},{2,18},{3,19},{4,20},{5,21},{6,22},{7,23},{8,24},{9,... | collective-permute-start | bytes 466952 | tf_op jit(solution)/shard_map/ppermute | solution.py:167
  53.4 12.3 %collective-permute-start.20 = (bf16[2,304,128]{2,1,0:T(8,128)(2,1)S(1)}, bf16[2,304,128]{2,1,0:T(8,128)(2,1)S(1)}, u32[]{:S(2)}, u32[]{:S(2)}) collective-permute-start(bf16[2,304,128]{2,1,0:T(8,128)(2,1)S(1)} %get-tuple-element.69), channel_id=1, source_target_pairs={{0,8},{1,9},{2,10},{3,11},{4,12},{5,13},{6,14},{7,15},{8,0},{9,1},... | collective-permute-start | bytes 466952 | tf_op jit(solution)/shard_map/ppermute | solution.py:167
  54.9 14.1 %collective-permute-start.8 = (bf16[4,152,128]{2,1,0:T(8,128)(2,1)S(1)}, bf16[4,152,128]{2,1,0:T(8,128)(2,1)S(1)}, u32[]{:S(2)}, u32[]{:S(2)}) collective-permute-start(bf16[4,152,128]{2,1,0:T(8,128)(2,1)S(1)} %get-tuple-element.55), channel_id=1, source_target_pairs={{0,4},{1,5},{2,6},{3,7},{4,0},{5,1},{6,2},{7,3},{8,12},{9,13},{10,... | collective-permute-start | bytes 466952 | tf_op jit(solution)/shard_map/ppermute | solution.py:167
  59.7 17.9 %collective-permute-start.26 = (bf16[3,152,128]{2,1,0:T(8,128)(2,1)S(1)}, bf16[3,152,128]{2,1,0:T(8,128)(2,1)S(1)}, u32[]{:S(2)}, u32[]{:S(2)}) collective-permute-start(bf16[3,152,128]{2,1,0:T(8,128)(2,1)S(1)} %get-tuple-element.76), channel_id=1, source_target_pairs={{0,24},{1,25},{2,26},{3,27},{4,28},{5,29},{6,30},{7,31},{8,16},{9,... | collective-permute-start | bytes 350216 | tf_op jit(solution)/shard_map/ppermute | solution.py:167
  60.4 20.2 %collective-permute-start.27 = (bf16[3,152,128]{2,1,0:T(8,128)(2,1)S(1)}, bf16[3,152,128]{2,1,0:T(8,128)(2,1)S(1)}, u32[]{:S(2)}, u32[]{:S(2)}) collective-permute-start(bf16[3,152,128]{2,1,0:T(8,128)(2,1)S(1)} %get-tuple-element.77), channel_id=1, source_target_pairs={{0,16},{1,17},{2,18},{3,19},{4,20},{5,21},{6,22},{7,23},{8,24},{9,... | collective-permute-start | bytes 350216 | tf_op jit(solution)/shard_map/ppermute | solution.py:167
  60.5 20.0 %collective-permute-start.28 = (bf16[3,152,128]{2,1,0:T(8,128)(2,1)S(1)}, bf16[3,152,128]{2,1,0:T(8,128)(2,1)S(1)}, u32[]{:S(2)}, u32[]{:S(2)}) collective-permute-start(bf16[3,152,128]{2,1,0:T(8,128)(2,1)S(1)} %get-tuple-element.78), channel_id=1, source_target_pairs={{0,8},{1,9},{2,10},{3,11},{4,12},{5,13},{6,14},{7,15},{8,0},{9,1},... | collective-permute-start | bytes 350216 | tf_op jit(solution)/shard_map/ppermute | solution.py:167
  64.1 16.4 %copy-start.1 = (s32[32,1]{0,1:T(1,128)S(1)}, s32[32,1]{0,1:T(1,128)}, u32[]{:S(2)}) copy-start(s32[32,1]{0,1:T(1,128)} %param.5) | copy-start | bytes 388
  67.4 4.6 %collective-permute-start.21 = (f32[8,128]{1,0:T(8,128)S(1)}, f32[8,128]{1,0:T(8,128)S(1)}, u32[]{:S(2)}, u32[]{:S(2)}) collective-permute-start(f32[8,128]{1,0:T(8,128)S(1)} %get-tuple-element.70), channel_id=1, source_target_pairs={{0,6},{1,7},{2,4},{3,5},{4,2},{5,3},{6,0},{7,1},{8,14},{9,15},{10,... | collective-permute-start | bytes 12296 | tf_op jit(solution)/shard_map/ppermute | solution.py:167
  69.0 3.9 %collective-permute-start.22 = (f32[8,128]{1,0:T(8,128)S(1)}, f32[8,128]{1,0:T(8,128)S(1)}, u32[]{:S(2)}, u32[]{:S(2)}) collective-permute-start(f32[8,128]{1,0:T(8,128)S(1)} %get-tuple-element.71), channel_id=1, source_target_pairs={{0,7},{1,6},{2,5},{3,4},{4,3},{5,2},{6,1},{7,0},{8,15},{9,14},{10,... | collective-permute-start | bytes 12296 | tf_op jit(solution)/shard_map/ppermute | solution.py:167
  72.0 3.0 %collective-permute-start.16 = (f32[8,128]{1,0:T(8,128)S(1)}, f32[8,128]{1,0:T(8,128)S(1)}, u32[]{:S(2)}, u32[]{:S(2)}) collective-permute-start(f32[8,128]{1,0:T(8,128)S(1)} %get-tuple-element.65.refs_5_), channel_id=1, source_target_pairs={{0,3},{1,2},{2,1},{3,0},{4,7},{5,6},{6,5},{7,4},{8,11},{9,10},{10,... | collective-permute-start | bytes 12296 | tf_op jit(solution)/shard_map/ppermute | solution.py:167
  72.9 3.0 %collective-permute-start.17 = (f32[8,128]{1,0:T(8,128)S(1)}, f32[8,128]{1,0:T(8,128)S(1)}, u32[]{:S(2)}, u32[]{:S(2)}) collective-permute-start(f32[8,128]{1,0:T(8,128)S(1)} %get-tuple-element.66), channel_id=1, source_target_pairs={{0,5},{1,4},{2,7},{3,6},{4,1},{5,0},{6,3},{7,2},{8,13},{9,12},{10,... | collective-permute-start | bytes 12296 | tf_op jit(solution)/shard_map/ppermute | solution.py:167
  76.1 5.8 %collective-permute-start.23 = (bf16[160,128]{1,0:T(8,128)(2,1)S(1)}, bf16[160,128]{1,0:T(8,128)(2,1)S(1)}, u32[]{:S(2)}, u32[]{:S(2)}) collective-permute-start(bf16[160,128]{1,0:T(8,128)(2,1)S(1)} %get-tuple-element.73), channel_id=1, source_target_pairs={{0,24},{1,25},{2,26},{3,27},{4,28},{5,29},{6,30},{7,31},{8,16},{9,... | collective-permute-start | bytes 122888 | tf_op jit(solution)/shard_map/ppermute | solution.py:167
  76.8 5.8 %collective-permute-start.24 = (bf16[160,128]{1,0:T(8,128)(2,1)S(1)}, bf16[160,128]{1,0:T(8,128)(2,1)S(1)}, u32[]{:S(2)}, u32[]{:S(2)}) collective-permute-start(bf16[160,128]{1,0:T(8,128)(2,1)S(1)} %get-tuple-element.74), channel_id=1, source_target_pairs={{0,16},{1,17},{2,18},{3,19},{4,20},{5,21},{6,22},{7,23},{8,24},{9,... | collective-permute-start | bytes 122888 | tf_op jit(solution)/shard_map/ppermute | solution.py:167
  77.5 5.2 %collective-permute-start.25 = (bf16[160,128]{1,0:T(8,128)(2,1)S(1)}, bf16[160,128]{1,0:T(8,128)(2,1)S(1)}, u32[]{:S(2)}, u32[]{:S(2)}) collective-permute-start(bf16[160,128]{1,0:T(8,128)(2,1)S(1)} %get-tuple-element.75), channel_id=1, source_target_pairs={{0,8},{1,9},{2,10},{3,11},{4,12},{5,13},{6,14},{7,15},{8,0},{9,1},... | collective-permute-start | bytes 122888 | tf_op jit(solution)/shard_map/ppermute | solution.py:167

commit v3 on v2

--- a/solution.py
+++ b/solution.py
@@ -146,16 +146,16 @@
     outer, count = split(devices)
     inner = sorted(range(count), key=lambda p: (bin(p).count("1"), p))
     back, there = inner[: count // 2], inner[count // 2 :]
-    half, most = len(there) // 2, len(back) * 3 // 4
-    return [back[:most], back[most:]], [there[:half], there[half:]], list(range(outer - 1, 0, -1))
+    half = len(there) // 2
+    return back, (there[:half], there[half:]), list(range(outer - 1, 0, -1))
 
 
 def fast(s, densities, weights, live):
     me_arr = lax.axis_index("pb").astype(jnp.int32).reshape(1)
     O, I, N, n = s.outer, s.inner, s.devices, s.pairs
-    backs, (later, sooner), far = parts_of(N)
+    back, (later, sooner), far = parts_of(N)
     order = [0, *far]
-    back, there = backs[0] + backs[1], later + sooner
+    there = later + sooner
     h, g = len(back), len(later)
     T = n * n // LANES
     block = n * s.ng
@@ -238,20 +238,16 @@
     whole = take_cv([[dz * I + p for p in later] for dz in order], g, (sent[0],))
     azf = [whole[0]] + [hop(x, dz * I) for dz, x in zip(far, whole[1:])]
 
-    def take_c(me_ref, dens, *refs):
-        outs, sems = refs[:2], refs[2]
-        copies = []
-        for t, ps in enumerate(backs):
-            copies += gather(s, me_ref[0], dens, [dz * I + p for dz in order for p in ps], 0, outs[t], sems.at[t])
-        for c in copies:
+    def take_c(me_ref, dens, out, sem):
+        for c in gather(s, me_ref[0], dens, [dz * I + p for dz in order for p in back], 0, out, sem):
             c.wait()
 
     own_c = call(
         take_c,
-        [sds(O * len(ps), n, s.ng) for ps in backs],
+        [sds(O * h, n, s.ng)],
         (me_arr, densities),
         [SM, HBM],
-        [pltpu.SemaphoreType.DMA((2, O * h))],
+        [pltpu.SemaphoreType.DMA((O * h,))],
         moved=4 * O * h * block,
         after=(whole[0],),
     )
@@ -286,11 +282,10 @@
         after=(parts[0],),
     )
     sin = [sb[0]] + [hop(x, p) for x, p in zip(sb[1:], back[1:])]
-    half = len(backs[0])
     mine = regroup([[(zi, j) for zi in range(O)] for j in range(g)], O, 2, azf, (sb[0],))
     fin = [hop(x, p) for x, p in zip(mine, later)]
-    out0 = regroup([[(j, zi) for j in range(half)] for zi in range(O)], half, 1, sin[:half], (mine[0],))
-    sz0 = [out0[0]] + [hop(x, dz * I) for dz, x in zip(far, out0[1:])]
+    back_z = regroup([[(j, zi) for j in range(h)] for zi in range(O)], h, 1, sin, (mine[0],))
+    sz = [back_z[0]] + [hop(x, dz * I) for dz, x in zip(far, back_z[1:])]
 
     def blocks_at_owner(arrived, by_outer, after):
         count, k = O * g, len(arrived)
@@ -331,87 +326,69 @@
             after=after,
         )
 
-    done0 = blocks_at_owner(fin, False, (out0[0],))
-    done1 = blocks_at_owner(azn, True, (done0[0],))
+    done1 = blocks_at_owner(azn, True, (back_z[0],))
+    done0 = blocks_at_owner(fin, False, (done1[0],))
     returned = [hop(x, p) for x, p in zip([*done0, *done1], there)]
 
-    rows2 = len(backs[1]) * s.rows
     extra = len(there) * T
 
-    def outward1(*refs):
-        src, small, outs = refs[: h - half], refs[h - half : h - half + 2 * g], refs[h - half + 2 * g :]
+    def turn(*refs):
+        small, outs = refs[: 2 * g], refs[2 * g :]
         blocks = jnp.concatenate([x[...] for x in small], axis=0).astype(BF16)
-        turn = pick(
+        order01 = pick(
             (O * extra, O * extra),
             lambda r, k: (r % T == k % T) & (r // extra == k % (O * T) // T) & (r % extra // T == k // (O * T)),
         )
-        turned = jnp.dot(turn, blocks, preferred_element_type=F32)
+        turned = jnp.dot(order01, blocks, preferred_element_type=F32)
         for zi, o in enumerate(outs):
-            for j in range(h - half):
-                o[s.rows * j : s.rows * (j + 1), :] = src[j][zi]
-            o[rows2 : rows2 + extra, :] = turned[extra * zi : extra * (zi + 1), :].astype(BF16)
-
-    out1 = call(
-        outward1,
-        [sds(rows2 + extra, LANES)] * O,
-        (*sin[half:], *returned),
-        [VM] * (h - half + 2 * g),
-        moved=4 * O * rows2 * LANES,
+            o[...] = turned[extra * zi : extra * (zi + 1), :]
+
+    small = call(
+        turn, [jax.ShapeDtypeStruct((extra, LANES), F32)] * O, returned, [VM] * (2 * g), moved=8 * O * extra * LANES
     )
-    sz1 = [out1[0]] + [hop(x, dz * I) for dz, x in zip(far, out1[1:])]
+    kz = [small[0]] + [hop(x, dz * I) for dz, x in zip(far, small[1:])]
 
     def finish0(me_ref, c_ref, *refs):
         src, (out, c, sc) = refs[:O], refs[O:]
         for zi in range(O):
-            for j in range(half):
-                row = n * (zi * half + j)
-                c[row : row + n, :] = c_ref[zi * half + j]
+            for j in range(h):
+                row = n * (zi * h + j)
+                c[row : row + n, :] = c_ref[zi * h + j]
                 unpack(s, src[zi], j, 0, sc, row)
-        out[...] = rows_of_pairs(s, me_ref[0], [dz * I + p for dz in order for p in backs[0]], c[...], sc[...])
-
-    def finish1(me_ref, c_ref, *refs):
-        src, (before, live_ref, out, c, sc) = refs[:O], refs[O:]
-        me, k = me_ref[0], h - half
-        for zi in range(O):
-            for j in range(k):
-                row = n * (zi * k + j)
-                c[row : row + n, :] = c_ref[zi * k + j]
-                unpack(s, src[zi], None, s.rows * j, sc, row)
-        r = rows_of_pairs(s, me, [dz * I + p for dz in order for p in backs[1]], c[...], sc[...])
-        small = jnp.concatenate([x[rows2 : rows2 + extra, :].astype(F32) for x in src], axis=0).astype(BF16)
+        r, half = 0.0, m_rows // 2
+        offs = [dz * I + p for dz in order for p in back]
+        for i, lo in enumerate((0, half)):
+            chosen = offs[i * len(offs) // 2 : (i + 1) * len(offs) // 2]
+            r = r + rows_of_pairs(s, me_ref[0], chosen, c[lo : lo + half, :], sc[lo : lo + half, :])
+        out[...] = r
+
+    def finish1(me_ref, *refs):
+        src, (before, live_ref, out) = refs[:O], refs[O:]
+        rows = jnp.concatenate([x[...] for x in src], axis=0).astype(BF16)
         offs = [dz * I + p for dz in order for p in there]
         placed = [
             jnp.dot(
-                pick((N, O * extra), lambda q, x, t=t: (q == (table(x // T, offs) ^ me)) & (x % T == t)),
-                small,
+                pick((N, O * extra), lambda q, x, t=t: (q == (table(x // T, offs) ^ me_ref[0])) & (x % T == t)),
+                rows,
                 preferred_element_type=F32,
             )
             for t in range(T)
         ]
-        r = r + before[...] + jnp.concatenate(placed, axis=1)
+        r = before[...] + jnp.concatenate(placed, axis=1)
         out[...] = (r * live_ref[...].astype(F32)).astype(BF16)
-
-    def scratch(ps):
-        return [pltpu.VMEM((n * O * len(ps), s.ng), BF16)] * 2
 
     partial = call(
         finish0,
         [jax.ShapeDtypeStruct((N, n * n), F32)],
-        (me_arr, own_c[0], *sz0),
+        (me_arr, own_c[0], *sz),
         [SM] + [VM] * (1 + O),
-        scratch(backs[0]),
+        [pltpu.VMEM((m_rows, s.ng), BF16)] * 2,
         flops=2 * m_rows * s.ng * n,
         moved=4 * m_rows * s.ng,
-        after=(out1[0],),
+        after=(small[0],),
     )[0]
     return call(
-        finish1,
-        [sds(N, n * n)],
-        (me_arr, own_c[1], *sz1, partial, live),
-        [SM] + [VM] * (3 + O),
-        scratch(backs[1]),
-        flops=2 * m_rows * s.ng * n,
-        moved=4 * m_rows * s.ng,
+        finish1, [sds(N, n * n)], (me_arr, *kz, partial, live), [SM] + [VM] * (2 + O), moved=8 * N * n * n
     )[0][:, None, :]
 
 

time: 84.1 us -> 86.6 us (1.030)
  waiting for transfers between devices: 34 us -> 38.6 us
  starting transfers between devices: 35 us -> 33.2 us
    ppermute x29, waiting for transfers between devices: 34 us -> 38.6 us  [hop(): return lax.ppermute(x, 'pb', [(d, d ^ m) for d in range(N)])]
    ppermute x29, starting transfers between devices: 35 us -> 33.2 us  [hop(): return lax.ppermute(x, 'pb', [(d, d ^ m) for d in range(N)])]
  transfers between devices with their start and end apart: 29 -> 29, of which waited for: 14 -> 11; matrix products, arithmetic and copies ran while one was open for 0% -> 0% of each run, Pallas kernels for 12% -> 10%
where the time goes in v3:
time: 86.6 us; the launch traced here: 86.3 us
  waiting for transfers between devices  38.6 us (45%)
  starting transfers between devices  33.2 us (38%)
  Pallas kernels  14.3 us (17%)
    ppermute x29, waiting for transfers between devices, hop(): return lax.ppermute(x, 'pb', [(d, d ^ m) for d in range(N)])  38.6 us
    ppermute x29, starting transfers between devices, hop(): return lax.ppermute(x, 'pb', [(d, d ^ m) for d in range(N)])  33.2 us
    pallas_call x15, Pallas kernels, call(): return pallas(body, outs, specs, a, scratch, flops, moved)(*ins, *after)  14.3 us
  transfers between devices with their start and end apart: 29, of which 11 were waited for; matrix products, arithmetic and copies ran while one was open for 0% of the time, Pallas kernels for 10%

profile of v3, /device:TPU:0, one launch (start us, length us, event | category | flops | bytes accessed | tf_op | source)
XLA Modules:
  0.0 86.3 jit_solution(15628838329984609178)
XLA Ops:
  0.0 1.1 %shard_map.37.refs_2_ = bf16[4,152,128]{2,1,0:T(8,128)(2,1)S(1)} custom-call(s32[1]{0:T(128)} %bitcast.refs_0_, bf16[32,1,32,1200]{3,2,1,0:T(8,128)(2,1)} %refs_1_.9), custom_call_target="tpu_custom_call" | custom-call | bytes 307200 | tf_op jit(solution)/shard_map/pallas_call | solution.py:47
  1.2 1.9 %shard_map.38 = (bf16[4,152,128]{2,1,0:T(8,128)(2,1)S(1)}, bf16[4,152,128]{2,1,0:T(8,128)(2,1)S(1)}, bf16[4,152,128]{2,1,0:T(8,128)(2,1)S(1)}) custom-call(s32[1]{0:T(128)} %bitcast.refs_0_, bf16[32,1,32,1200]{3,2,1,0:T(8,128)(2,1)} %refs_1_.9, bf16[4,152,128]{2,1,0:T(8,128)(2,1)S(1)} %shard_map.37.refs_2_), custom_call_target="tpu_custom_call" | custom-call | bytes 921600 | tf_op jit(solution)/shard_map/pallas_call | solution.py:47
  3.1 1.7 %shard_map.39 = (bf16[4,304,128]{2,1,0:T(8,128)(2,1)S(1)}, bf16[4,304,128]{2,1,0:T(8,128)(2,1)S(1)}) custom-call(s32[1]{0:T(128)} %bitcast.refs_0_, bf16[32,1,32,1200]{3,2,1,0:T(8,128)(2,1)} %refs_1_.9, bf16[4,152,128]{2,1,0:T(8,128)(2,1)S(1)} %get-tuple-element.40.refs_2_), custom_call_target="tpu_custom_call" | custom-call | bytes 1228800 | tf_op jit(solution)/shard_map/pallas_call | solution.py:47
  4.8 4.0 %collective-permute-start.9 = (bf16[4,304,128]{2,1,0:T(8,128)(2,1)S(1)}, bf16[4,304,128]{2,1,0:T(8,128)(2,1)S(1)}, u32[]{:S(2)}, u32[]{:S(2)}) collective-permute-start(bf16[4,304,128]{2,1,0:T(8,128)(2,1)S(1)} %get-tuple-element.41.refs_2_), channel_id=1, source_target_pairs={{0,6},{1,7},{2,4},{3,5},{4,2},{5,3},{6,0},{7,1},{8,14},{9,15},{10,... | collective-permute-start | bytes 933896 | tf_op jit(solution)/shard_map/ppermute | solution.py:167
  8.8 2.6 %collective-permute-start.4 = (bf16[4,152,128]{2,1,0:T(8,128)(2,1)S(1)}, bf16[4,152,128]{2,1,0:T(8,128)(2,1)S(1)}, u32[]{:S(2)}, u32[]{:S(2)}) collective-permute-start(bf16[4,152,128]{2,1,0:T(8,128)(2,1)S(1)} %get-tuple-element.40.refs_2_), channel_id=1, source_target_pairs={{0,16},{1,17},{2,18},{3,19},{4,20},{5,21},{6,22},{7,23},{8,24},{9,... | collective-permute-start | bytes 466952 | tf_op jit(solution)/shard_map/ppermute | solution.py:167
  11.4 1.6 %collective-permute-start.5 = (bf16[4,152,128]{2,1,0:T(8,128)(2,1)S(1)}, bf16[4,152,128]{2,1,0:T(8,128)(2,1)S(1)}, u32[]{:S(2)}, u32[]{:S(2)}) collective-permute-start(bf16[4,152,128]{2,1,0:T(8,128)(2,1)S(1)} %get-tuple-element.47), channel_id=1, source_target_pairs={{0,8},{1,9},{2,10},{3,11},{4,12},{5,13},{6,14},{7,15},{8,0},{9,1},... | collective-permute-start | bytes 466952 | tf_op jit(solution)/shard_map/ppermute | solution.py:167
  12.9 0.2 collective-permute-start.3
  13.2 1.7 %shard_map.40 = (bf16[2,304,128]{2,1,0:T(8,128)(2,1)S(1)}, bf16[2,304,128]{2,1,0:T(8,128)(2,1)S(1)}, bf16[2,304,128]{2,1,0:T(8,128)(2,1)S(1)}, bf16[2,304,128]{2,1,0:T(8,128)(2,1)S(1)}) custom-call(s32[1]{0:T(128)} %bitcast.refs_0_, bf16[32,1,32,1200]{3,2,1,0:T(8,128)(2,1)} %refs_1_.9, bf16[4,304,128]{2,1,0:T(8,128)(2,1)S(1)} %get-tuple-element.41.refs_2_), custom_call_target="tpu_custom_call" | custom-call | bytes 1228800 | tf_op jit(solution)/shard_map/pallas_call | solution.py:47
  14.9 0.0 copy-start
  14.9 1.4 %shard_map.41.refs_4_.refs_1_ = bf16[16,16,1200]{2,1,0:T(8,128)(2,1)S(1)} custom-call(s32[1]{0:T(128)} %bitcast.refs_0_, bf16[32,1,32,1200]{3,2,1,0:T(8,128)(2,1)} %refs_1_.9, bf16[2,304,128]{2,1,0:T(8,128)(2,1)S(1)} %get-tuple-element.42.refs_2_.refs_0_), custom_call_target="tpu_custom_call" | custom-call | bytes 1228800 | tf_op jit(solution)/shard_map/pallas_call | solution.py:47
  16.3 4.7 %collective-permute-done.4.refs_2_ = bf16[4,152,128]{2,1,0:T(8,128)(2,1)S(1)} collective-permute-done((bf16[4,152,128]{2,1,0:T(8,128)(2,1)S(1)}, bf16[4,152,128]{2,1,0:T(8,128)(2,1)S(1)}, u32[]{:S(2)}, u32[]{:S(2)}) %collective-permute-start.4) | collective-permute-done | bytes 155680 | tf_op jit(solution)/shard_map/ppermute | solution.py:167
  21.0 2.5 %collective-permute-done.5.refs_3_ = bf16[4,152,128]{2,1,0:T(8,128)(2,1)S(1)} collective-permute-done((bf16[4,152,128]{2,1,0:T(8,128)(2,1)S(1)}, bf16[4,152,128]{2,1,0:T(8,128)(2,1)S(1)}, u32[]{:S(2)}, u32[]{:S(2)}) %collective-permute-start.5) | collective-permute-done | bytes 155680 | tf_op jit(solution)/shard_map/ppermute | solution.py:167
  23.5 0.1 collective-permute-start.6
  23.6 1.1 %collective-permute-start.7 = (bf16[4,152,128]{2,1,0:T(8,128)(2,1)S(1)}, bf16[4,152,128]{2,1,0:T(8,128)(2,1)S(1)}, u32[]{:S(2)}, u32[]{:S(2)}) collective-permute-start(bf16[4,152,128]{2,1,0:T(8,128)(2,1)S(1)} %get-tuple-element.50), channel_id=1, source_target_pairs={{0,2},{1,3},{2,0},{3,1},{4,6},{5,7},{6,4},{7,5},{8,10},{9,11},{10,... | collective-permute-start | bytes 466952 | tf_op jit(solution)/shard_map/ppermute | solution.py:167
  24.7 1.6 %collective-permute-start.8 = (bf16[4,152,128]{2,1,0:T(8,128)(2,1)S(1)}, bf16[4,152,128]{2,1,0:T(8,128)(2,1)S(1)}, u32[]{:S(2)}, u32[]{:S(2)}) collective-permute-start(bf16[4,152,128]{2,1,0:T(8,128)(2,1)S(1)} %get-tuple-element.51), channel_id=1, source_target_pairs={{0,4},{1,5},{2,6},{3,7},{4,0},{5,1},{6,2},{7,3},{8,12},{9,13},{10,... | collective-permute-start | bytes 466952 | tf_op jit(solution)/shard_map/ppermute | solution.py:167
  26.3 2.5 %collective-permute-start = (bf16[2,304,128]{2,1,0:T(8,128)(2,1)S(1)}, bf16[2,304,128]{2,1,0:T(8,128)(2,1)S(1)}, u32[]{:S(2)}, u32[]{:S(2)}) collective-permute-start(bf16[2,304,128]{2,1,0:T(8,128)(2,1)S(1)} %get-tuple-element.43), channel_id=1, source_target_pairs={{0,24},{1,25},{2,26},{3,27},{4,28},{5,29},{6,30},{7,31},{8,16},{9,... | collective-permute-start | bytes 466952 | tf_op jit(solution)/shard_map/ppermute | solution.py:167
  28.7 0.4 collective-permute-start.1
  29.2 1.6 %collective-permute-start.2 = (bf16[2,304,128]{2,1,0:T(8,128)(2,1)S(1)}, bf16[2,304,128]{2,1,0:T(8,128)(2,1)S(1)}, u32[]{:S(2)}, u32[]{:S(2)}) collective-permute-start(bf16[2,304,128]{2,1,0:T(8,128)(2,1)S(1)} %get-tuple-element.45), channel_id=1, source_target_pairs={{0,8},{1,9},{2,10},{3,11},{4,12},{5,13},{6,14},{7,15},{8,0},{9,1},... | collective-permute-start | bytes 466952 | tf_op jit(solution)/shard_map/ppermute | solution.py:167
  30.8 1.3 %shard_map.44 = (bf16[4,152,128]{2,1,0:T(8,128)(2,1)S(1)}, bf16[4,152,128]{2,1,0:T(8,128)(2,1)S(1)}, bf16[4,152,128]{2,1,0:T(8,128)(2,1)S(1)}, bf16[4,152,128]{2,1,0:T(8,128)(2,1)S(1)}) custom-call(bf16[4,152,128]{2,1,0:T(8,128)(2,1)S(1)} %get-tuple-element.48.refs_2_.refs_0_, bf16[4,152,128]{2,1,0:T(8,128)(2,1)S(1)} %collective-permute-done.6.refs_1_, ...), custom_call_target="tpu_custom_call" | custom-call | flops 737280000 | bytes 2880000 | tf_op jit(solution)/shard_map/pallas_call | solution.py:47
  32.0 0.1 collective-permute-start.16
  32.1 1.0 %collective-permute-start.17 = (bf16[4,152,128]{2,1,0:T(8,128)(2,1)S(1)}, bf16[4,152,128]{2,1,0:T(8,128)(2,1)S(1)}, u32[]{:S(2)}, u32[]{:S(2)}) collective-permute-start(bf16[4,152,128]{2,1,0:T(8,128)(2,1)S(1)} %get-tuple-element.61), channel_id=1, source_target_pairs={{0,2},{1,3},{2,0},{3,1},{4,6},{5,7},{6,4},{7,5},{8,10},{9,11},{10,... | collective-permute-start | bytes 466952 | tf_op jit(solution)/shard_map/ppermute | solution.py:167
  33.2 1.8 %collective-permute-done.refs_1_ = bf16[2,304,128]{2,1,0:T(8,128)(2,1)S(1)} collective-permute-done((bf16[2,304,128]{2,1,0:T(8,128)(2,1)S(1)}, bf16[2,304,128]{2,1,0:T(8,128)(2,1)S(1)}, u32[]{:S(2)}, u32[]{:S(2)}) %collective-permute-start) | collective-permute-done | bytes 155680 | tf_op jit(solution)/shard_map/ppermute | solution.py:167
  35.0 0.1 collective-permute-start.18
  35.1 8.0 %collective-permute-done.1.refs_2_ = bf16[2,304,128]{2,1,0:T(8,128)(2,1)S(1)} collective-permute-done((bf16[2,304,128]{2,1,0:T(8,128)(2,1)S(1)}, bf16[2,304,128]{2,1,0:T(8,128)(2,1)S(1)}, u32[]{:S(2)}, u32[]{:S(2)}) %collective-permute-start.1) | collective-permute-done | bytes 155680 | tf_op jit(solution)/shard_map/ppermute | solution.py:167
  43.2 0.9 %collective-permute-start.11 = (bf16[4,304,128]{2,1,0:T(8,128)(2,1)S(1)}, bf16[4,304,128]{2,1,0:T(8,128)(2,1)S(1)}, u32[]{:S(2)}, u32[]{:S(2)}) collective-permute-start(bf16[4,304,128]{2,1,0:T(8,128)(2,1)S(1)} %get-tuple-element.55.refs_4_), channel_id=1, source_target_pairs={{0,3},{1,2},{2,1},{3,0},{4,7},{5,6},{6,5},{7,4},{8,11},{9,10},{10,... | collective-permute-start | bytes 933896 | tf_op jit(solution)/shard_map/ppermute | solution.py:167
  44.1 1.1 %collective-permute-start.12 = (bf16[4,304,128]{2,1,0:T(8,128)(2,1)S(1)}, bf16[4,304,128]{2,1,0:T(8,128)(2,1)S(1)}, u32[]{:S(2)}, u32[]{:S(2)}) collective-permute-start(bf16[4,304,128]{2,1,0:T(8,128)(2,1)S(1)} %get-tuple-element.56), channel_id=1, source_target_pairs={{0,5},{1,4},{2,7},{3,6},{4,1},{5,0},{6,3},{7,2},{8,13},{9,12},{10,... | collective-permute-start | bytes 933896 | tf_op jit(solution)/shard_map/ppermute | solution.py:167
  45.1 2.4 %collective-permute-start.13 = (bf16[2,304,128]{2,1,0:T(8,128)(2,1)S(1)}, bf16[2,304,128]{2,1,0:T(8,128)(2,1)S(1)}, u32[]{:S(2)}, u32[]{:S(2)}) collective-permute-start(bf16[2,304,128]{2,1,0:T(8,128)(2,1)S(1)} %get-tuple-element.57), channel_id=1, source_target_pairs={{0,24},{1,25},{2,26},{3,27},{4,28},{5,29},{6,30},{7,31},{8,16},{9,... | collective-permute-start | bytes 466952 | tf_op jit(solution)/shard_map/ppermute | solution.py:167
  47.6 2.0 %collective-permute-start.15 = (bf16[2,304,128]{2,1,0:T(8,128)(2,1)S(1)}, bf16[2,304,128]{2,1,0:T(8,128)(2,1)S(1)}, u32[]{:S(2)}, u32[]{:S(2)}) collective-permute-start(bf16[2,304,128]{2,1,0:T(8,128)(2,1)S(1)} %get-tuple-element.59), channel_id=1, source_target_pairs={{0,8},{1,9},{2,10},{3,11},{4,12},{5,13},{6,14},{7,15},{8,0},{9,1},... | collective-permute-start | bytes 466952 | tf_op jit(solution)/shard_map/ppermute | solution.py:167
  49.6 4.4 %collective-permute-done.13.refs_1_ = bf16[2,304,128]{2,1,0:T(8,128)(2,1)S(1)} collective-permute-done((bf16[2,304,128]{2,1,0:T(8,128)(2,1)S(1)}, bf16[2,304,128]{2,1,0:T(8,128)(2,1)S(1)}, u32[]{:S(2)}, u32[]{:S(2)}) %collective-permute-start.13) | collective-permute-done | bytes 155680 | tf_op jit(solution)/shard_map/ppermute | solution.py:167
  54.0 2.4 %collective-permute-start.26 = (bf16[4,152,128]{2,1,0:T(8,128)(2,1)S(1)}, bf16[4,152,128]{2,1,0:T(8,128)(2,1)S(1)}, u32[]{:S(2)}, u32[]{:S(2)}) collective-permute-start(bf16[4,152,128]{2,1,0:T(8,128)(2,1)S(1)} %get-tuple-element.72), channel_id=1, source_target_pairs={{0,24},{1,25},{2,26},{3,27},{4,28},{5,29},{6,30},{7,31},{8,16},{9,... | collective-permute-start | bytes 466952 | tf_op jit(solution)/shard_map/ppermute | solution.py:167
  56.4 10.2 %collective-permute-done.14.refs_2_ = bf16[2,304,128]{2,1,0:T(8,128)(2,1)S(1)} collective-permute-done((bf16[2,304,128]{2,1,0:T(8,128)(2,1)S(1)}, bf16[2,304,128]{2,1,0:T(8,128)(2,1)S(1)}, u32[]{:S(2)}, u32[]{:S(2)}) %collective-permute-start.14) | collective-permute-done | bytes 155680 | tf_op jit(solution)/shard_map/ppermute | solution.py:167
  66.6 0.0 copy-start.1
  66.6 1.7 %shard_map.47 = (f32[8,128]{1,0:T(8,128)S(1)}, f32[8,128]{1,0:T(8,128)S(1)}) custom-call(bf16[2,304,128]{2,1,0:T(8,128)(2,1)S(1)} %get-tuple-element.53.refs_5_.refs_0_, bf16[2,304,128]{2,1,0:T(8,128)(2,1)S(1)} %collective-permute-done.13.refs_1_, bf16[2,304,128]{2,1,0:T(8,128)(2,1)S(1)} %collective-permute-done.14.refs_2_, ...), custom_call_target="tpu_custom_call" | custom-call | flops 368640000 | bytes 2880000 | tf_op jit(solution)/shard_map/pallas_call | solution.py:47
  68.3 1.3 %collective-permute-start.21 = (f32[8,128]{1,0:T(8,128)S(1)}, f32[8,128]{1,0:T(8,128)S(1)}, u32[]{:S(2)}, u32[]{:S(2)}) collective-permute-start(f32[8,128]{1,0:T(8,128)S(1)} %get-tuple-element.64.refs_3_), channel_id=1, source_target_pairs={{0,6},{1,7},{2,4},{3,5},{4,2},{5,3},{6,0},{7,1},{8,14},{9,15},{10,... | collective-permute-start | bytes 12296 | tf_op jit(solution)/shard_map/ppermute | solution.py:167
  69.6 1.6 %shard_map.48 = (f32[8,128]{1,0:T(8,128)S(1)}, f32[8,128]{1,0:T(8,128)S(1)}) custom-call(bf16[4,304,128]{2,1,0:T(8,128)(2,1)S(1)} %collective-permute-done.11.refs_0_, bf16[4,304,128]{2,1,0:T(8,128)(2,1)S(1)} %collective-permute-done.12.refs_1_, bf16[1,1200,1200]{2,1,0:T(8,128)(2,1)S(1)} %copy-done, f32[8,128]{1,0:T(8,128)S(1)} %get-tuple-element.64.refs_3_), custom_call_target="tpu_custom_call" | custom-call | flops 368640000 | bytes 2880000 | tf_op jit(solution)/shard_map/pallas_call | solution.py:47
  71.3 1.6 %collective-permute-done.21.refs_2_ = f32[8,128]{1,0:T(8,128)S(1)} collective-permute-done((f32[8,128]{1,0:T(8,128)S(1)}, f32[8,128]{1,0:T(8,128)S(1)}, u32[]{:S(2)}, u32[]{:S(2)}) %collective-permute-start.21) | collective-permute-done | bytes 4128 | tf_op jit(solution)/shard_map/ppermute | solution.py:167
  72.9 0.5 collective-permute-start.19
  73.4 0.1 collective-permute-done.22.refs_3_
  73.5 0.9 collective-permute-start.20
  74.4 1.5 %collective-permute-done.19.refs_0_ = f32[8,128]{1,0:T(8,128)S(1)} collective-permute-done((f32[8,128]{1,0:T(8,128)S(1)}, f32[8,128]{1,0:T(8,128)S(1)}, u32[]{:S(2)}, u32[]{:S(2)}) %collective-permute-start.19) | collective-permute-done | bytes 4128 | tf_op jit(solution)/shard_map/ppermute | solution.py:167
  75.9 0.7 collective-permute-done.20.refs_1_
  76.6 0.1 shard_map.49
  76.7 4.4 %collective-permute-start.23 = (f32[8,128]{1,0:T(8,128)S(1)}, f32[8,128]{1,0:T(8,128)S(1)}, u32[]{:S(2)}, u32[]{:S(2)}) collective-permute-start(f32[8,128]{1,0:T(8,128)S(1)} %get-tuple-element.69), channel_id=1, source_target_pairs={{0,24},{1,25},{2,26},{3,27},{4,28},{5,29},{6,30},{7,31},{8,16},{9,... | collective-permute-start | bytes 12296 | tf_op jit(solution)/shard_map/ppermute | solution.py:167
  81.1 0.6 collective-permute-start.25
  81.7 0.1 copy.4.refs_6_
  81.8 0.9 %shard_map.50.refs_5_ = f32[32,256]{1,0:T(8,128)S(1)} custom-call(s32[1]{0:T(128)} %bitcast.refs_0_, bf16[16,16,1200]{2,1,0:T(8,128)(2,1)S(1)} %shard_map.41.refs_4_.refs_1_, bf16[4,152,128]{2,1,0:T(8,128)(2,1)S(1)} %get-tuple-element.63.refs_5_.refs_2_, bf16[4,152,128]{2,1,0:T(8,128)(2,1)S(1)} %collective-permute-done.26.refs_3_, ...), custom_call_target="tpu_custom_call" | custom-call | flops 9830400 | bytes 1228800 | tf_op jit(solution)/shard_map/pallas_call | solution.py:47
  82.7 2.9 %collective-permute-done.24.refs_3_ = f32[8,128]{1,0:T(8,128)S(1)} collective-permute-done((f32[8,128]{1,0:T(8,128)S(1)}, f32[8,128]{1,0:T(8,128)S(1)}, u32[]{:S(2)}, u32[]{:S(2)}) %collective-permute-start.24) | collective-permute-done | bytes 4128 | tf_op jit(solution)/shard_map/ppermute | solution.py:167
  85.6 0.7 shard_map.51
  (30 shorter events, 0.2 us)
Async XLA Ops:
  4.8 21.5 %collective-permute-start.9 = (bf16[4,304,128]{2,1,0:T(8,128)(2,1)S(1)}, bf16[4,304,128]{2,1,0:T(8,128)(2,1)S(1)}, u32[]{:S(2)}, u32[]{:S(2)}) collective-permute-start(bf16[4,304,128]{2,1,0:T(8,128)(2,1)S(1)} %get-tuple-element.41.refs_2_), channel_id=1, source_target_pairs={{0,6},{1,7},{2,4},{3,5},{4,2},{5,3},{6,0},{7,1},{8,14},{9,15},{10,... | collective-permute-start | bytes 933896 | tf_op jit(solution)/shard_map/ppermute | solution.py:167
  8.8 12.2 %collective-permute-start.4 = (bf16[4,152,128]{2,1,0:T(8,128)(2,1)S(1)}, bf16[4,152,128]{2,1,0:T(8,128)(2,1)S(1)}, u32[]{:S(2)}, u32[]{:S(2)}) collective-permute-start(bf16[4,152,128]{2,1,0:T(8,128)(2,1)S(1)} %get-tuple-element.40.refs_2_), channel_id=1, source_target_pairs={{0,16},{1,17},{2,18},{3,19},{4,20},{5,21},{6,22},{7,23},{8,24},{9,... | collective-permute-start | bytes 466952 | tf_op jit(solution)/shard_map/ppermute | solution.py:167
  11.4 17.4 %collective-permute-start.10 = (bf16[4,304,128]{2,1,0:T(8,128)(2,1)S(1)}, bf16[4,304,128]{2,1,0:T(8,128)(2,1)S(1)}, u32[]{:S(2)}, u32[]{:S(2)}) collective-permute-start(bf16[4,304,128]{2,1,0:T(8,128)(2,1)S(1)} %get-tuple-element.52), channel_id=1, source_target_pairs={{0,7},{1,6},{2,5},{3,4},{4,3},{5,2},{6,1},{7,0},{8,15},{9,14},{10,... | collective-permute-start | bytes 933896 | tf_op jit(solution)/shard_map/ppermute | solution.py:167
  11.4 12.1 %collective-permute-start.5 = (bf16[4,152,128]{2,1,0:T(8,128)(2,1)S(1)}, bf16[4,152,128]{2,1,0:T(8,128)(2,1)S(1)}, u32[]{:S(2)}, u32[]{:S(2)}) collective-permute-start(bf16[4,152,128]{2,1,0:T(8,128)(2,1)S(1)} %get-tuple-element.47), channel_id=1, source_target_pairs={{0,8},{1,9},{2,10},{3,11},{4,12},{5,13},{6,14},{7,15},{8,0},{9,1},... | collective-permute-start | bytes 466952 | tf_op jit(solution)/shard_map/ppermute | solution.py:167
  12.9 10.5 %collective-permute-start.3 = (bf16[4,152,128]{2,1,0:T(8,128)(2,1)S(1)}, bf16[4,152,128]{2,1,0:T(8,128)(2,1)S(1)}, u32[]{:S(2)}, u32[]{:S(2)}) collective-permute-start(bf16[4,152,128]{2,1,0:T(8,128)(2,1)S(1)} %shard_map.37.refs_2_), channel_id=1, source_target_pairs={{0,24},{1,25},{2,26},{3,27},{4,28},{5,29},{6,30},{7,31},{8,16},{9,... | collective-permute-start | bytes 466952 | tf_op jit(solution)/shard_map/ppermute | solution.py:167
  14.9 15.9 %copy-start = (bf16[1,1200,1200]{2,1,0:T(8,128)(2,1)S(1)}, bf16[1,1200,1200]{2,1,0:T(8,128)(2,1)}, u32[]{:S(2)}) copy-start(bf16[1,1200,1200]{2,1,0:T(8,128)(2,1)} %refs_2_.1) | copy-start | bytes 8640004
  23.5 5.7 %collective-permute-start.6 = (bf16[4,152,128]{2,1,0:T(8,128)(2,1)S(1)}, bf16[4,152,128]{2,1,0:T(8,128)(2,1)S(1)}, u32[]{:S(2)}, u32[]{:S(2)}) collective-permute-start(bf16[4,152,128]{2,1,0:T(8,128)(2,1)S(1)} %get-tuple-element.49), channel_id=1, source_target_pairs={{0,1},{1,0},{2,3},{3,2},{4,5},{5,4},{6,7},{7,6},{8,9},{9,8},{10,11... | collective-permute-start | bytes 466952 | tf_op jit(solution)/shard_map/ppermute | solution.py:167
  23.6 7.2 %collective-permute-start.7 = (bf16[4,152,128]{2,1,0:T(8,128)(2,1)S(1)}, bf16[4,152,128]{2,1,0:T(8,128)(2,1)S(1)}, u32[]{:S(2)}, u32[]{:S(2)}) collective-permute-start(bf16[4,152,128]{2,1,0:T(8,128)(2,1)S(1)} %get-tuple-element.50), channel_id=1, source_target_pairs={{0,2},{1,3},{2,0},{3,1},{4,6},{5,7},{6,4},{7,5},{8,10},{9,11},{10,... | collective-permute-start | bytes 466952 | tf_op jit(solution)/shard_map/ppermute | solution.py:167
  24.7 6.1 %collective-permute-start.8 = (bf16[4,152,128]{2,1,0:T(8,128)(2,1)S(1)}, bf16[4,152,128]{2,1,0:T(8,128)(2,1)S(1)}, u32[]{:S(2)}, u32[]{:S(2)}) collective-permute-start(bf16[4,152,128]{2,1,0:T(8,128)(2,1)S(1)} %get-tuple-element.51), channel_id=1, source_target_pairs={{0,4},{1,5},{2,6},{3,7},{4,0},{5,1},{6,2},{7,3},{8,12},{9,13},{10,... | collective-permute-start | bytes 466952 | tf_op jit(solution)/shard_map/ppermute | solution.py:167
  26.3 8.8 %collective-permute-start = (bf16[2,304,128]{2,1,0:T(8,128)(2,1)S(1)}, bf16[2,304,128]{2,1,0:T(8,128)(2,1)S(1)}, u32[]{:S(2)}, u32[]{:S(2)}) collective-permute-start(bf16[2,304,128]{2,1,0:T(8,128)(2,1)S(1)} %get-tuple-element.43), channel_id=1, source_target_pairs={{0,24},{1,25},{2,26},{3,27},{4,28},{5,29},{6,30},{7,31},{8,16},{9,... | collective-permute-start | bytes 466952 | tf_op jit(solution)/shard_map/ppermute | solution.py:167
  28.7 14.4 %collective-permute-start.1 = (bf16[2,304,128]{2,1,0:T(8,128)(2,1)S(1)}, bf16[2,304,128]{2,1,0:T(8,128)(2,1)S(1)}, u32[]{:S(2)}, u32[]{:S(2)}) collective-permute-start(bf16[2,304,128]{2,1,0:T(8,128)(2,1)S(1)} %get-tuple-element.44), channel_id=1, source_target_pairs={{0,16},{1,17},{2,18},{3,19},{4,20},{5,21},{6,22},{7,23},{8,24},{9,... | collective-permute-start | bytes 466952 | tf_op jit(solution)/shard_map/ppermute | solution.py:167
  29.2 13.9 %collective-permute-start.2 = (bf16[2,304,128]{2,1,0:T(8,128)(2,1)S(1)}, bf16[2,304,128]{2,1,0:T(8,128)(2,1)S(1)}, u32[]{:S(2)}, u32[]{:S(2)}) collective-permute-start(bf16[2,304,128]{2,1,0:T(8,128)(2,1)S(1)} %get-tuple-element.45), channel_id=1, source_target_pairs={{0,8},{1,9},{2,10},{3,11},{4,12},{5,13},{6,14},{7,15},{8,0},{9,1},... | collective-permute-start | bytes 466952 | tf_op jit(solution)/shard_map/ppermute | solution.py:167
  32.0 13.1 %collective-permute-start.16 = (bf16[4,152,128]{2,1,0:T(8,128)(2,1)S(1)}, bf16[4,152,128]{2,1,0:T(8,128)(2,1)S(1)}, u32[]{:S(2)}, u32[]{:S(2)}) collective-permute-start(bf16[4,152,128]{2,1,0:T(8,128)(2,1)S(1)} %get-tuple-element.60), channel_id=1, source_target_pairs={{0,1},{1,0},{2,3},{3,2},{4,5},{5,4},{6,7},{7,6},{8,9},{9,8},{10,11... | collective-permute-start | bytes 466952 | tf_op jit(solution)/shard_map/ppermute | solution.py:167
  32.1 15.4 %collective-permute-start.17 = (bf16[4,152,128]{2,1,0:T(8,128)(2,1)S(1)}, bf16[4,152,128]{2,1,0:T(8,128)(2,1)S(1)}, u32[]{:S(2)}, u32[]{:S(2)}) collective-permute-start(bf16[4,152,128]{2,1,0:T(8,128)(2,1)S(1)} %get-tuple-element.61), channel_id=1, source_target_pairs={{0,2},{1,3},{2,0},{3,1},{4,6},{5,7},{6,4},{7,5},{8,10},{9,11},{10,... | collective-permute-start | bytes 466952 | tf_op jit(solution)/shard_map/ppermute | solution.py:167
  35.0 12.6 %collective-permute-start.18 = (bf16[4,152,128]{2,1,0:T(8,128)(2,1)S(1)}, bf16[4,152,128]{2,1,0:T(8,128)(2,1)S(1)}, u32[]{:S(2)}, u32[]{:S(2)}) collective-permute-start(bf16[4,152,128]{2,1,0:T(8,128)(2,1)S(1)} %get-tuple-element.62), channel_id=1, source_target_pairs={{0,4},{1,5},{2,6},{3,7},{4,0},{5,1},{6,2},{7,3},{8,12},{9,13},{10,... | collective-permute-start | bytes 466952 | tf_op jit(solution)/shard_map/ppermute | solution.py:167
  43.2 25.1 %collective-permute-start.11 = (bf16[4,304,128]{2,1,0:T(8,128)(2,1)S(1)}, bf16[4,304,128]{2,1,0:T(8,128)(2,1)S(1)}, u32[]{:S(2)}, u32[]{:S(2)}) collective-permute-start(bf16[4,304,128]{2,1,0:T(8,128)(2,1)S(1)} %get-tuple-element.55.refs_4_), channel_id=1, source_target_pairs={{0,3},{1,2},{2,1},{3,0},{4,7},{5,6},{6,5},{7,4},{8,11},{9,10},{10,... | collective-permute-start | bytes 933896 | tf_op jit(solution)/shard_map/ppermute | solution.py:167
  44.1 25.5 %collective-permute-start.12 = (bf16[4,304,128]{2,1,0:T(8,128)(2,1)S(1)}, bf16[4,304,128]{2,1,0:T(8,128)(2,1)S(1)}, u32[]{:S(2)}, u32[]{:S(2)}) collective-permute-start(bf16[4,304,128]{2,1,0:T(8,128)(2,1)S(1)} %get-tuple-element.56), channel_id=1, source_target_pairs={{0,5},{1,4},{2,7},{3,6},{4,1},{5,0},{6,3},{7,2},{8,13},{9,12},{10,... | collective-permute-start | bytes 933896 | tf_op jit(solution)/shard_map/ppermute | solution.py:167
  45.1 8.8 %collective-permute-start.13 = (bf16[2,304,128]{2,1,0:T(8,128)(2,1)S(1)}, bf16[2,304,128]{2,1,0:T(8,128)(2,1)S(1)}, u32[]{:S(2)}, u32[]{:S(2)}) collective-permute-start(bf16[2,304,128]{2,1,0:T(8,128)(2,1)S(1)} %get-tuple-element.57), channel_id=1, source_target_pairs={{0,24},{1,25},{2,26},{3,27},{4,28},{5,29},{6,30},{7,31},{8,16},{9,... | collective-permute-start | bytes 466952 | tf_op jit(solution)/shard_map/ppermute | solution.py:167
  47.6 19.0 %collective-permute-start.14 = (bf16[2,304,128]{2,1,0:T(8,128)(2,1)S(1)}, bf16[2,304,128]{2,1,0:T(8,128)(2,1)S(1)}, u32[]{:S(2)}, u32[]{:S(2)}) collective-permute-start(bf16[2,304,128]{2,1,0:T(8,128)(2,1)S(1)} %get-tuple-element.58), channel_id=1, source_target_pairs={{0,16},{1,17},{2,18},{3,19},{4,20},{5,21},{6,22},{7,23},{8,24},{9,... | collective-permute-start | bytes 466952 | tf_op jit(solution)/shard_map/ppermute | solution.py:167
  47.6 19.0 %collective-permute-start.15 = (bf16[2,304,128]{2,1,0:T(8,128)(2,1)S(1)}, bf16[2,304,128]{2,1,0:T(8,128)(2,1)S(1)}, u32[]{:S(2)}, u32[]{:S(2)}) collective-permute-start(bf16[2,304,128]{2,1,0:T(8,128)(2,1)S(1)} %get-tuple-element.59), channel_id=1, source_target_pairs={{0,8},{1,9},{2,10},{3,11},{4,12},{5,13},{6,14},{7,15},{8,0},{9,1},... | collective-permute-start | bytes 466952 | tf_op jit(solution)/shard_map/ppermute | solution.py:167
  54.0 27.1 %collective-permute-start.26 = (bf16[4,152,128]{2,1,0:T(8,128)(2,1)S(1)}, bf16[4,152,128]{2,1,0:T(8,128)(2,1)S(1)}, u32[]{:S(2)}, u32[]{:S(2)}) collective-permute-start(bf16[4,152,128]{2,1,0:T(8,128)(2,1)S(1)} %get-tuple-element.72), channel_id=1, source_target_pairs={{0,24},{1,25},{2,26},{3,27},{4,28},{5,29},{6,30},{7,31},{8,16},{9,... | collective-permute-start | bytes 466952 | tf_op jit(solution)/shard_map/ppermute | solution.py:167
  66.6 15.2 %collective-permute-start.27 = (bf16[4,152,128]{2,1,0:T(8,128)(2,1)S(1)}, bf16[4,152,128]{2,1,0:T(8,128)(2,1)S(1)}, u32[]{:S(2)}, u32[]{:S(2)}) collective-permute-start(bf16[4,152,128]{2,1,0:T(8,128)(2,1)S(1)} %get-tuple-element.73), channel_id=1, source_target_pairs={{0,16},{1,17},{2,18},{3,19},{4,20},{5,21},{6,22},{7,23},{8,24},{9,... | collective-permute-start | bytes 466952 | tf_op jit(solution)/shard_map/ppermute | solution.py:167
  66.6 15.2 %collective-permute-start.28 = (bf16[4,152,128]{2,1,0:T(8,128)(2,1)S(1)}, bf16[4,152,128]{2,1,0:T(8,128)(2,1)S(1)}, u32[]{:S(2)}, u32[]{:S(2)}) collective-permute-start(bf16[4,152,128]{2,1,0:T(8,128)(2,1)S(1)} %get-tuple-element.74), channel_id=1, source_target_pairs={{0,8},{1,9},{2,10},{3,11},{4,12},{5,13},{6,14},{7,15},{8,0},{9,1},... | collective-permute-start | bytes 466952 | tf_op jit(solution)/shard_map/ppermute | solution.py:167
  66.6 15.1 %copy-start.1 = (s32[32,1]{0,1:T(1,128)S(1)}, s32[32,1]{0,1:T(1,128)}, u32[]{:S(2)}) copy-start(s32[32,1]{0,1:T(1,128)} %param.5) | copy-start | bytes 388
  68.3 4.6 %collective-permute-start.21 = (f32[8,128]{1,0:T(8,128)S(1)}, f32[8,128]{1,0:T(8,128)S(1)}, u32[]{:S(2)}, u32[]{:S(2)}) collective-permute-start(f32[8,128]{1,0:T(8,128)S(1)} %get-tuple-element.64.refs_3_), channel_id=1, source_target_pairs={{0,6},{1,7},{2,4},{3,5},{4,2},{5,3},{6,0},{7,1},{8,14},{9,15},{10,... | collective-permute-start | bytes 12296 | tf_op jit(solution)/shard_map/ppermute | solution.py:167
  69.6 3.9 %collective-permute-start.22 = (f32[8,128]{1,0:T(8,128)S(1)}, f32[8,128]{1,0:T(8,128)S(1)}, u32[]{:S(2)}, u32[]{:S(2)}) collective-permute-start(f32[8,128]{1,0:T(8,128)S(1)} %get-tuple-element.67), channel_id=1, source_target_pairs={{0,7},{1,6},{2,5},{3,4},{4,3},{5,2},{6,1},{7,0},{8,15},{9,14},{10,... | collective-permute-start | bytes 12296 | tf_op jit(solution)/shard_map/ppermute | solution.py:167
  72.9 3.0 %collective-permute-start.19 = (f32[8,128]{1,0:T(8,128)S(1)}, f32[8,128]{1,0:T(8,128)S(1)}, u32[]{:S(2)}, u32[]{:S(2)}) collective-permute-start(f32[8,128]{1,0:T(8,128)S(1)} %get-tuple-element.65), channel_id=1, source_target_pairs={{0,3},{1,2},{2,1},{3,0},{4,7},{5,6},{6,5},{7,4},{8,11},{9,10},{10,... | collective-permute-start | bytes 12296 | tf_op jit(solution)/shard_map/ppermute | solution.py:167
  73.5 3.0 %collective-permute-start.20 = (f32[8,128]{1,0:T(8,128)S(1)}, f32[8,128]{1,0:T(8,128)S(1)}, u32[]{:S(2)}, u32[]{:S(2)}) collective-permute-start(f32[8,128]{1,0:T(8,128)S(1)} %get-tuple-element.66), channel_id=1, source_target_pairs={{0,5},{1,4},{2,7},{3,6},{4,1},{5,0},{6,3},{7,2},{8,13},{9,12},{10,... | collective-permute-start | bytes 12296 | tf_op jit(solution)/shard_map/ppermute | solution.py:167
  76.7 5.9 %collective-permute-start.23 = (f32[8,128]{1,0:T(8,128)S(1)}, f32[8,128]{1,0:T(8,128)S(1)}, u32[]{:S(2)}, u32[]{:S(2)}) collective-permute-start(f32[8,128]{1,0:T(8,128)S(1)} %get-tuple-element.69), channel_id=1, source_target_pairs={{0,24},{1,25},{2,26},{3,27},{4,28},{5,29},{6,30},{7,31},{8,16},{9,... | collective-permute-start | bytes 12296 | tf_op jit(solution)/shard_map/ppermute | solution.py:167
  81.1 4.5 %collective-permute-start.24 = (f32[8,128]{1,0:T(8,128)S(1)}, f32[8,128]{1,0:T(8,128)S(1)}, u32[]{:S(2)}, u32[]{:S(2)}) collective-permute-start(f32[8,128]{1,0:T(8,128)S(1)} %get-tuple-element.70), channel_id=1, source_target_pairs={{0,16},{1,17},{2,18},{3,19},{4,20},{5,21},{6,22},{7,23},{8,24},{9,... | collective-permute-start | bytes 12296 | tf_op jit(solution)/shard_map/ppermute | solution.py:167
  81.1 4.5 %collective-permute-start.25 = (f32[8,128]{1,0:T(8,128)S(1)}, f32[8,128]{1,0:T(8,128)S(1)}, u32[]{:S(2)}, u32[]{:S(2)}) collective-permute-start(f32[8,128]{1,0:T(8,128)S(1)} %get-tuple-element.71), channel_id=1, source_target_pairs={{0,8},{1,9},{2,10},{3,11},{4,12},{5,13},{6,14},{7,15},{8,0},{9,1},... | collective-permute-start | bytes 12296 | tf_op jit(solution)/shard_map/ppermute | solution.py:167

commit v4 on v2

--- a/solution.py
+++ b/solution.py
@@ -132,12 +132,12 @@
     return copies
 
 
-def reader(s, buf, i, row, edge):
+def reader(s, ref, row, edge):
     def read(lo, hi):
         if hi <= s.ng:
-            return buf[i, row : row + s.pairs, lo:hi]
-        edge[i, :, : s.tail] = buf[i, row : row + s.pairs, lo : s.ng]
-        return edge[i]
+            return ref[row : row + s.pairs, lo:hi]
+        edge[:, : s.tail] = ref[row : row + s.pairs, lo : s.ng]
+        return edge[...]
 
     return read
 
@@ -166,56 +166,46 @@
     def hop(x, m):
         return lax.ppermute(x, "pb", [(d, d ^ m) for d in range(N)])
 
-    densities = pltpu.with_memory_space_constraint(densities, pltpu.HBM)
-
-    def take_v(zs, after):
+
+    def take_v0(me_ref, dens, out, buf, edge, sem):
+        offs = [far[0] * I + p for p in back]
+        for i, c in enumerate(gather(s, me_ref[0], dens, offs, 1, buf, sem)):
+            c.wait()
+            pack(s, reader(s, buf.at[i], 0, edge.at[i]), out, i, 0)
+
+    first = call(
+        take_v0,
+        [sds(h, s.rows, LANES)],
+        (me_arr, pltpu.with_memory_space_constraint(densities, pltpu.HBM)),
+        [SM, HBM],
+        [pltpu.VMEM((h, n, s.ng), BF16), pltpu.VMEM((h, n, LANES), BF16), pltpu.SemaphoreType.DMA((h,))],
+        moved=4 * h * block,
+    )
+
+    def take(picks, count, parts, after):
         def kernel(me_ref, dens, *refs):
-            outs, (buf, edge, sem) = refs[: len(zs)], refs[len(zs) :]
-            offs = [dz * I + p for dz in zs for p in back]
-            for i, c in enumerate(gather(s, me_ref[0], dens, offs, 1, buf, sem)):
-                c.wait()
-                pack(s, reader(s, buf, i, 0, edge), outs[i // h], i % h, 0)
-
-        k = len(zs) * h
+            outs, edge = refs[: len(picks)], refs[len(picks)]
+            for o, chosen in enumerate(picks):
+                for i, m in enumerate(chosen):
+                    ref = dens.at[me_ref[0] ^ m, 0]
+                    for part in range(parts):
+                        at = (o * count + i) * parts + part
+                        pack(s, reader(s, ref, n * (2 - parts + part), edge.at[at]), outs[o], i, part * s.rows)
+
+        k = len(picks) * count * parts
         return call(
             kernel,
-            [sds(h, s.rows, LANES)] * len(zs),
+            [sds(count, parts * s.rows, LANES)] * len(picks),
             (me_arr, densities),
-            [SM, HBM],
-            [pltpu.VMEM((k, n, s.ng), BF16), pltpu.VMEM((k, n, LANES), BF16), pltpu.SemaphoreType.DMA((k,))],
+            [SM, VM],
+            [pltpu.VMEM((k, n, LANES), BF16)],
             moved=4 * k * block,
             after=after,
         )
 
-    first = take_v(far[:1], ())
-    rest = take_v([*far[1:], 0], (first[0],))
+    rest = take([[dz * I + p for p in back] for dz in [*far[1:], 0]], h, 1, (first[0],))
     vb = dict(zip([*far, 0], [*first, *rest]))
     vz = {dz: hop(vb[dz], dz * I) for dz in far}
-
-    def take_cv(picks, count, after):
-        def kernel(me_ref, dens, *refs):
-            outs, (buf, edge, edge2, sem) = refs[: len(picks)], refs[len(picks) :]
-            offs = [m for chosen in picks for m in chosen]
-            for i, c in enumerate(gather(s, me_ref[0], dens, offs, None, buf, sem)):
-                c.wait()
-                pack(s, reader(s, buf, i, 0, edge), outs[i // count], i % count, 0)
-                pack(s, reader(s, buf, i, n, edge2), outs[i // count], i % count, s.rows)
-
-        k = len(picks) * count
-        return call(
-            kernel,
-            [sds(count, 2 * s.rows, LANES)] * len(picks),
-            (me_arr, densities),
-            [SM, HBM],
-            [
-                pltpu.VMEM((k, 2 * n, s.ng), BF16),
-                pltpu.VMEM((k, n, LANES), BF16),
-                pltpu.VMEM((k, n, LANES), BF16),
-                pltpu.SemaphoreType.DMA((k,)),
-            ],
-            moved=8 * k * block,
-            after=after,
-        )
 
     def regroup(picks, count, parts, ins, after=()):
         def kernel(*refs):
@@ -233,31 +223,13 @@
             after=after,
         )
 
-    sent = take_cv([[dz * I + p for dz in order] for p in sooner], O, (rest[0],))
+    sent = take([[dz * I + p for dz in order] for p in sooner], O, 2, (rest[0],))
     near = [hop(x, p) for x, p in zip(sent, sooner)]
-    whole = take_cv([[dz * I + p for p in later] for dz in order], g, (sent[0],))
+    whole = take([[dz * I + p for p in later] for dz in order], g, 2, (sent[0],))
     azf = [whole[0]] + [hop(x, dz * I) for dz, x in zip(far, whole[1:])]
 
-    def take_c(me_ref, dens, *refs):
-        outs, sems = refs[:2], refs[2]
-        copies = []
-        for t, ps in enumerate(backs):
-            copies += gather(s, me_ref[0], dens, [dz * I + p for dz in order for p in ps], 0, outs[t], sems.at[t])
-        for c in copies:
-            c.wait()
-
-    own_c = call(
-        take_c,
-        [sds(O * len(ps), n, s.ng) for ps in backs],
-        (me_arr, densities),
-        [SM, HBM],
-        [pltpu.SemaphoreType.DMA((2, O * h))],
-        moved=4 * O * h * block,
-        after=(whole[0],),
-    )
-
     zs = [vb[0]] + [vz[dz] for dz in far]
-    pieces = regroup([[(zi, j) for zi in range(O)] for j in range(h)], O, 1, zs, (own_c[0],))
+    pieces = regroup([[(zi, j) for zi in range(O)] for j in range(h)], O, 1, zs, (whole[0],))
     vin = [pieces[0]] + [hop(x, p) for x, p in zip(pieces[1:], back[1:])]
 
     parts = regroup([[(j, zi) for j in range(g)] for zi in range(O)], g, 2, near, (pieces[0],))
@@ -360,22 +332,22 @@
     )
     sz1 = [out1[0]] + [hop(x, dz * I) for dz, x in zip(far, out1[1:])]
 
-    def finish0(me_ref, c_ref, *refs):
+    def finish0(me_ref, dens, *refs):
         src, (out, c, sc) = refs[:O], refs[O:]
         for zi in range(O):
             for j in range(half):
                 row = n * (zi * half + j)
-                c[row : row + n, :] = c_ref[zi * half + j]
+                c[row : row + n, :] = dens[me_ref[0] ^ (order[zi] * I + back[j]), 0, :n, :]
                 unpack(s, src[zi], j, 0, sc, row)
         out[...] = rows_of_pairs(s, me_ref[0], [dz * I + p for dz in order for p in backs[0]], c[...], sc[...])
 
-    def finish1(me_ref, c_ref, *refs):
+    def finish1(me_ref, dens, *refs):
         src, (before, live_ref, out, c, sc) = refs[:O], refs[O:]
         me, k = me_ref[0], h - half
         for zi in range(O):
             for j in range(k):
                 row = n * (zi * k + j)
-                c[row : row + n, :] = c_ref[zi * k + j]
+                c[row : row + n, :] = dens[me ^ (order[zi] * I + back[half + j]), 0, :n, :]
                 unpack(s, src[zi], None, s.rows * j, sc, row)
         r = rows_of_pairs(s, me, [dz * I + p for dz in order for p in backs[1]], c[...], sc[...])
         small = jnp.concatenate([x[rows2 : rows2 + extra, :].astype(F32) for x in src], axis=0).astype(BF16)
@@ -397,7 +369,7 @@
     partial = call(
         finish0,
         [jax.ShapeDtypeStruct((N, n * n), F32)],
-        (me_arr, own_c[0], *sz0),
+        (me_arr, densities, *sz0),
         [SM] + [VM] * (1 + O),
         scratch(backs[0]),
         flops=2 * m_rows * s.ng * n,
@@ -407,7 +379,7 @@
     return call(
         finish1,
         [sds(N, n * n)],
-        (me_arr, own_c[1], *sz1, partial, live),
+        (me_arr, densities, *sz1, partial, live),
         [SM] + [VM] * (3 + O),
         scratch(backs[1]),
         flops=2 * m_rows * s.ng * n,

time: 84.1 us -> 83.4 us (level)
  Pallas kernels: 14.6 us -> 9.07 us
  starting transfers between devices: 35 us -> 38.9 us
  local copies, waits for them, and re-layouts: 0.1 us -> 1.25 us
    pallas_call x15 -> x14, Pallas kernels: 14.6 us -> 9.07 us  [call(): return pallas(body, outs, specs, a, scratch, flops, moved)(*ins, *after)]
    ppermute x29, starting transfers between devices: 35 us -> 38.9 us  [hop(): return lax.ppermute(x, 'pb', [(d, d ^ m) for d in range(N)])]
    unnamed x5, local copies, waits for them, and re-layouts: 0.1 us -> 1.25 us
  transfers between devices with their start and end apart: 29 -> 29, of which waited for: 14 -> 12; matrix products, arithmetic and copies ran while one was open for 0% -> 1% of each run, Pallas kernels for 12% -> 8%
where the time goes in v4:
time: 83.4 us; the launch traced here: 83.2 us
  starting transfers between devices  38.9 us (47%)
  waiting for transfers between devices  33.9 us (41%)
  Pallas kernels  9.07 us (11%)
  local copies, waits for them, and re-layouts  1.25 us (1%)
    ppermute x29, starting transfers between devices, hop(): return lax.ppermute(x, 'pb', [(d, d ^ m) for d in range(N)])  38.9 us
    ppermute x29, waiting for transfers between devices, hop(): return lax.ppermute(x, 'pb', [(d, d ^ m) for d in range(N)])  33.9 us
    pallas_call x14, Pallas kernels, call(): return pallas(body, outs, specs, a, scratch, flops, moved)(*ins, *after)  9.07 us
  transfers between devices with their start and end apart: 29, of which 12 were waited for; matrix products, arithmetic and copies ran while one was open for 1% of the time, Pallas kernels for 8%

profile of v4, /device:TPU:0, one launch (start us, length us, event | category | flops | bytes accessed | tf_op | source)
XLA Modules:
  0.0 83.2 jit_solution(2853439047416119939)
XLA Ops:
  0.0 1.3 %shard_map.37.refs_2_ = bf16[4,152,128]{2,1,0:T(8,128)(2,1)S(1)} custom-call(s32[1]{0:T(128)} %bitcast.refs_0_, bf16[32,1,32,1200]{3,2,1,0:T(8,128)(2,1)} %refs_1_.11), custom_call_target="tpu_custom_call" | custom-call | bytes 307200 | tf_op jit(solution)/shard_map/pallas_call | solution.py:47
  1.3 0.5 copy-done
  1.8 0.2 shard_map.38
  2.0 4.1 %collective-permute-start.1 = (bf16[4,152,128]{2,1,0:T(8,128)(2,1)S(1)}, bf16[4,152,128]{2,1,0:T(8,128)(2,1)S(1)}, u32[]{:S(2)}, u32[]{:S(2)}) collective-permute-start(bf16[4,152,128]{2,1,0:T(8,128)(2,1)S(1)} %get-tuple-element.41.refs_2_), channel_id=1, source_target_pairs={{0,16},{1,17},{2,18},{3,19},{4,20},{5,21},{6,22},{7,23},{8,24},{9,... | collective-permute-start | bytes 466952 | tf_op jit(solution)/shard_map/ppermute | solution.py:167
  6.1 1.6 %collective-permute-start.2 = (bf16[4,152,128]{2,1,0:T(8,128)(2,1)S(1)}, bf16[4,152,128]{2,1,0:T(8,128)(2,1)S(1)}, u32[]{:S(2)}, u32[]{:S(2)}) collective-permute-start(bf16[4,152,128]{2,1,0:T(8,128)(2,1)S(1)} %get-tuple-element.42), channel_id=1, source_target_pairs={{0,8},{1,9},{2,10},{3,11},{4,12},{5,13},{6,14},{7,15},{8,0},{9,1},... | collective-permute-start | bytes 466952 | tf_op jit(solution)/shard_map/ppermute | solution.py:167
  7.7 0.2 shard_map.39
  7.8 2.5 %collective-permute-start.6 = (bf16[4,304,128]{2,1,0:T(8,128)(2,1)S(1)}, bf16[4,304,128]{2,1,0:T(8,128)(2,1)S(1)}, u32[]{:S(2)}, u32[]{:S(2)}) collective-permute-start(bf16[4,304,128]{2,1,0:T(8,128)(2,1)S(1)} %get-tuple-element.43.refs_2_), channel_id=1, source_target_pairs={{0,6},{1,7},{2,4},{3,5},{4,2},{5,3},{6,0},{7,1},{8,14},{9,15},{10,... | collective-permute-start | bytes 933896 | tf_op jit(solution)/shard_map/ppermute | solution.py:167
  10.3 0.2 collective-permute-start
  10.6 0.2 shard_map.40
  10.7 4.1 %collective-permute-done.1.refs_2_ = bf16[4,152,128]{2,1,0:T(8,128)(2,1)S(1)} collective-permute-done((bf16[4,152,128]{2,1,0:T(8,128)(2,1)S(1)}, bf16[4,152,128]{2,1,0:T(8,128)(2,1)S(1)}, u32[]{:S(2)}, u32[]{:S(2)}) %collective-permute-start.1) | collective-permute-done | bytes 155680 | tf_op jit(solution)/shard_map/ppermute | solution.py:167
  14.9 3.1 %collective-permute-done.refs_1_ = bf16[4,152,128]{2,1,0:T(8,128)(2,1)S(1)} collective-permute-done((bf16[4,152,128]{2,1,0:T(8,128)(2,1)S(1)}, bf16[4,152,128]{2,1,0:T(8,128)(2,1)S(1)}, u32[]{:S(2)}, u32[]{:S(2)}) %collective-permute-start) | collective-permute-done | bytes 155680 | tf_op jit(solution)/shard_map/ppermute | solution.py:167
  18.0 0.1 collective-permute-start.3
  18.1 1.6 %collective-permute-start.4 = (bf16[4,152,128]{2,1,0:T(8,128)(2,1)S(1)}, bf16[4,152,128]{2,1,0:T(8,128)(2,1)S(1)}, u32[]{:S(2)}, u32[]{:S(2)}) collective-permute-start(bf16[4,152,128]{2,1,0:T(8,128)(2,1)S(1)} %get-tuple-element.47), channel_id=1, source_target_pairs={{0,2},{1,3},{2,0},{3,1},{4,6},{5,7},{6,4},{7,5},{8,10},{9,11},{10,... | collective-permute-start | bytes 466952 | tf_op jit(solution)/shard_map/ppermute | solution.py:167
  19.7 1.5 %collective-permute-start.5 = (bf16[4,152,128]{2,1,0:T(8,128)(2,1)S(1)}, bf16[4,152,128]{2,1,0:T(8,128)(2,1)S(1)}, u32[]{:S(2)}, u32[]{:S(2)}) collective-permute-start(bf16[4,152,128]{2,1,0:T(8,128)(2,1)S(1)} %get-tuple-element.48), channel_id=1, source_target_pairs={{0,4},{1,5},{2,6},{3,7},{4,0},{5,1},{6,2},{7,3},{8,12},{9,13},{10,... | collective-permute-start | bytes 466952 | tf_op jit(solution)/shard_map/ppermute | solution.py:167
  21.2 4.8 %collective-permute-start.10 = (bf16[2,304,128]{2,1,0:T(8,128)(2,1)S(1)}, bf16[2,304,128]{2,1,0:T(8,128)(2,1)S(1)}, u32[]{:S(2)}, u32[]{:S(2)}) collective-permute-start(bf16[2,304,128]{2,1,0:T(8,128)(2,1)S(1)} %get-tuple-element.53), channel_id=1, source_target_pairs={{0,16},{1,17},{2,18},{3,19},{4,20},{5,21},{6,22},{7,23},{8,24},{9,... | collective-permute-start | bytes 466952 | tf_op jit(solution)/shard_map/ppermute | solution.py:167
  26.0 1.5 %collective-permute-start.9 = (bf16[2,304,128]{2,1,0:T(8,128)(2,1)S(1)}, bf16[2,304,128]{2,1,0:T(8,128)(2,1)S(1)}, u32[]{:S(2)}, u32[]{:S(2)}) collective-permute-start(bf16[2,304,128]{2,1,0:T(8,128)(2,1)S(1)} %get-tuple-element.52), channel_id=1, source_target_pairs={{0,24},{1,25},{2,26},{3,27},{4,28},{5,29},{6,30},{7,31},{8,16},{9,... | collective-permute-start | bytes 466952 | tf_op jit(solution)/shard_map/ppermute | solution.py:167
  27.6 1.3 %shard_map.43 = (bf16[4,152,128]{2,1,0:T(8,128)(2,1)S(1)}, bf16[4,152,128]{2,1,0:T(8,128)(2,1)S(1)}, bf16[4,152,128]{2,1,0:T(8,128)(2,1)S(1)}, bf16[4,152,128]{2,1,0:T(8,128)(2,1)S(1)}) custom-call(bf16[4,152,128]{2,1,0:T(8,128)(2,1)S(1)} %get-tuple-element.45.refs_2_.refs_0_, bf16[4,152,128]{2,1,0:T(8,128)(2,1)S(1)} %collective-permute-done.3.refs_1_, ...), custom_call_target="tpu_custom_call" | custom-call | flops 737280000 | bytes 2880000 | tf_op jit(solution)/shard_map/pallas_call | solution.py:47
  28.8 0.1 collective-permute-start.14
  28.9 5.8 %collective-permute-done.10.refs_2_ = bf16[2,304,128]{2,1,0:T(8,128)(2,1)S(1)} collective-permute-done((bf16[2,304,128]{2,1,0:T(8,128)(2,1)S(1)}, bf16[2,304,128]{2,1,0:T(8,128)(2,1)S(1)}, u32[]{:S(2)}, u32[]{:S(2)}) %collective-permute-start.10) | collective-permute-done | bytes 155680 | tf_op jit(solution)/shard_map/ppermute | solution.py:167
  34.7 3.2 %collective-permute-done.11.refs_3_ = bf16[2,304,128]{2,1,0:T(8,128)(2,1)S(1)} collective-permute-done((bf16[2,304,128]{2,1,0:T(8,128)(2,1)S(1)}, bf16[2,304,128]{2,1,0:T(8,128)(2,1)S(1)}, u32[]{:S(2)}, u32[]{:S(2)}) %collective-permute-start.11) | collective-permute-done | bytes 155680 | tf_op jit(solution)/shard_map/ppermute | solution.py:167
  38.0 0.8 collective-permute-start.12
  38.8 1.0 %collective-permute-start.13 = (bf16[4,304,128]{2,1,0:T(8,128)(2,1)S(1)}, bf16[4,304,128]{2,1,0:T(8,128)(2,1)S(1)}, u32[]{:S(2)}, u32[]{:S(2)}) collective-permute-start(bf16[4,304,128]{2,1,0:T(8,128)(2,1)S(1)} %get-tuple-element.57), channel_id=1, source_target_pairs={{0,5},{1,4},{2,7},{3,6},{4,1},{5,0},{6,3},{7,2},{8,13},{9,12},{10,... | collective-permute-start | bytes 933896 | tf_op jit(solution)/shard_map/ppermute | solution.py:167
  39.8 1.5 %collective-permute-start.15 = (bf16[4,152,128]{2,1,0:T(8,128)(2,1)S(1)}, bf16[4,152,128]{2,1,0:T(8,128)(2,1)S(1)}, u32[]{:S(2)}, u32[]{:S(2)}) collective-permute-start(bf16[4,152,128]{2,1,0:T(8,128)(2,1)S(1)} %get-tuple-element.59), channel_id=1, source_target_pairs={{0,2},{1,3},{2,0},{3,1},{4,6},{5,7},{6,4},{7,5},{8,10},{9,11},{10,... | collective-permute-start | bytes 466952 | tf_op jit(solution)/shard_map/ppermute | solution.py:167
  41.3 1.4 %collective-permute-start.18 = (bf16[2,304,128]{2,1,0:T(8,128)(2,1)S(1)}, bf16[2,304,128]{2,1,0:T(8,128)(2,1)S(1)}, u32[]{:S(2)}, u32[]{:S(2)}) collective-permute-start(bf16[2,304,128]{2,1,0:T(8,128)(2,1)S(1)} %get-tuple-element.63), channel_id=1, source_target_pairs={{0,24},{1,25},{2,26},{3,27},{4,28},{5,29},{6,30},{7,31},{8,16},{9,... | collective-permute-start | bytes 466952 | tf_op jit(solution)/shard_map/ppermute | solution.py:167
  42.7 1.7 %collective-permute-start.19 = (bf16[2,304,128]{2,1,0:T(8,128)(2,1)S(1)}, bf16[2,304,128]{2,1,0:T(8,128)(2,1)S(1)}, u32[]{:S(2)}, u32[]{:S(2)}) collective-permute-start(bf16[2,304,128]{2,1,0:T(8,128)(2,1)S(1)} %get-tuple-element.64), channel_id=1, source_target_pairs={{0,16},{1,17},{2,18},{3,19},{4,20},{5,21},{6,22},{7,23},{8,24},{9,... | collective-permute-start | bytes 466952 | tf_op jit(solution)/shard_map/ppermute | solution.py:167
  44.5 6.5 %collective-permute-done.15.refs_2_ = bf16[4,152,128]{2,1,0:T(8,128)(2,1)S(1)} collective-permute-done((bf16[4,152,128]{2,1,0:T(8,128)(2,1)S(1)}, bf16[4,152,128]{2,1,0:T(8,128)(2,1)S(1)}, u32[]{:S(2)}, u32[]{:S(2)}) %collective-permute-start.15) | collective-permute-done | bytes 155680 | tf_op jit(solution)/shard_map/ppermute | solution.py:167
  50.9 2.8 %collective-permute-start.20 = (bf16[2,304,128]{2,1,0:T(8,128)(2,1)S(1)}, bf16[2,304,128]{2,1,0:T(8,128)(2,1)S(1)}, u32[]{:S(2)}, u32[]{:S(2)}) collective-permute-start(bf16[2,304,128]{2,1,0:T(8,128)(2,1)S(1)} %get-tuple-element.65), channel_id=1, source_target_pairs={{0,8},{1,9},{2,10},{3,11},{4,12},{5,13},{6,14},{7,15},{8,0},{9,1},... | collective-permute-start | bytes 466952 | tf_op jit(solution)/shard_map/ppermute | solution.py:167
  53.7 0.5 collective-permute-start.8
  54.3 3.8 %collective-permute-done.19.refs_2_ = bf16[2,304,128]{2,1,0:T(8,128)(2,1)S(1)} collective-permute-done((bf16[2,304,128]{2,1,0:T(8,128)(2,1)S(1)}, bf16[2,304,128]{2,1,0:T(8,128)(2,1)S(1)}, u32[]{:S(2)}, u32[]{:S(2)}) %collective-permute-start.19) | collective-permute-done | bytes 155680 | tf_op jit(solution)/shard_map/ppermute | solution.py:167
  58.1 1.2 %collective-permute-start.26 = (bf16[3,152,128]{2,1,0:T(8,128)(2,1)S(1)}, bf16[3,152,128]{2,1,0:T(8,128)(2,1)S(1)}, u32[]{:S(2)}, u32[]{:S(2)}) collective-permute-start(bf16[3,152,128]{2,1,0:T(8,128)(2,1)S(1)} %get-tuple-element.72), channel_id=1, source_target_pairs={{0,24},{1,25},{2,26},{3,27},{4,28},{5,29},{6,30},{7,31},{8,16},{9,... | collective-permute-start | bytes 350216 | tf_op jit(solution)/shard_map/ppermute | solution.py:167
  59.3 3.2 %collective-permute-start.28 = (bf16[3,152,128]{2,1,0:T(8,128)(2,1)S(1)}, bf16[3,152,128]{2,1,0:T(8,128)(2,1)S(1)}, u32[]{:S(2)}, u32[]{:S(2)}) collective-permute-start(bf16[3,152,128]{2,1,0:T(8,128)(2,1)S(1)} %get-tuple-element.74), channel_id=1, source_target_pairs={{0,8},{1,9},{2,10},{3,11},{4,12},{5,13},{6,14},{7,15},{8,0},{9,1},... | collective-permute-start | bytes 350216 | tf_op jit(solution)/shard_map/ppermute | solution.py:167
  62.5 1.6 %shard_map.46 = (f32[8,128]{1,0:T(8,128)S(1)}, f32[8,128]{1,0:T(8,128)S(1)}) custom-call(bf16[4,304,128]{2,1,0:T(8,128)(2,1)S(1)} %collective-permute-done.12.refs_0_, bf16[4,304,128]{2,1,0:T(8,128)(2,1)S(1)} %collective-permute-done.13.refs_1_, bf16[1,1200,1200]{2,1,0:T(8,128)(2,1)S(1)} %copy-done.1, bf16[3,152,128]{2,1,0:T(8,128)(2,1)S(1)} %get-tuple-element.60.refs_3_.refs_2_), custom_call_target="tpu_custom_call" | custom-call | flops 368640000 | bytes 2880000 | tf_op jit(solution)/shard_map/pallas_call | solution.py:47
  64.1 1.7 %shard_map.47 = (f32[8,128]{1,0:T(8,128)S(1)}, f32[8,128]{1,0:T(8,128)S(1)}) custom-call(bf16[2,304,128]{2,1,0:T(8,128)(2,1)S(1)} %get-tuple-element.50.refs_5_.refs_0_, bf16[2,304,128]{2,1,0:T(8,128)(2,1)S(1)} %collective-permute-done.18.refs_1_, bf16[2,304,128]{2,1,0:T(8,128)(2,1)S(1)} %collective-permute-done.19.refs_2_, ...), custom_call_target="tpu_custom_call" | custom-call | flops 368640000 | bytes 2880000 | tf_op jit(solution)/shard_map/pallas_call | solution.py:47
  65.8 1.6 %collective-permute-start.21 = (f32[8,128]{1,0:T(8,128)S(1)}, f32[8,128]{1,0:T(8,128)S(1)}, u32[]{:S(2)}, u32[]{:S(2)}) collective-permute-start(f32[8,128]{1,0:T(8,128)S(1)} %get-tuple-element.66), channel_id=1, source_target_pairs={{0,6},{1,7},{2,4},{3,5},{4,2},{5,3},{6,0},{7,1},{8,14},{9,15},{10,... | collective-permute-start | bytes 12296 | tf_op jit(solution)/shard_map/ppermute | solution.py:167
  67.4 3.0 %collective-permute-done.21.refs_3_ = f32[8,128]{1,0:T(8,128)S(1)} collective-permute-done((f32[8,128]{1,0:T(8,128)S(1)}, f32[8,128]{1,0:T(8,128)S(1)}, u32[]{:S(2)}, u32[]{:S(2)}) %collective-permute-start.21) | collective-permute-done | bytes 4128 | tf_op jit(solution)/shard_map/ppermute | solution.py:167
  70.4 1.0 %collective-permute-done.22.refs_4_ = f32[8,128]{1,0:T(8,128)S(1)} collective-permute-done((f32[8,128]{1,0:T(8,128)S(1)}, f32[8,128]{1,0:T(8,128)S(1)}, u32[]{:S(2)}, u32[]{:S(2)}) %collective-permute-start.22) | collective-permute-done | bytes 4128 | tf_op jit(solution)/shard_map/ppermute | solution.py:167
  71.3 0.9 %collective-permute-start.17 = (f32[8,128]{1,0:T(8,128)S(1)}, f32[8,128]{1,0:T(8,128)S(1)}, u32[]{:S(2)}, u32[]{:S(2)}) collective-permute-start(f32[8,128]{1,0:T(8,128)S(1)} %get-tuple-element.62), channel_id=1, source_target_pairs={{0,5},{1,4},{2,7},{3,6},{4,1},{5,0},{6,3},{7,2},{8,13},{9,12},{10,... | collective-permute-start | bytes 12296 | tf_op jit(solution)/shard_map/ppermute | solution.py:167
  72.2 1.2 %collective-permute-done.16.refs_1_ = f32[8,128]{1,0:T(8,128)S(1)} collective-permute-done((f32[8,128]{1,0:T(8,128)S(1)}, f32[8,128]{1,0:T(8,128)S(1)}, u32[]{:S(2)}, u32[]{:S(2)}) %collective-permute-start.16) | collective-permute-done | bytes 4128 | tf_op jit(solution)/shard_map/ppermute | solution.py:167
  73.4 1.0 %collective-permute-done.17.refs_2_ = f32[8,128]{1,0:T(8,128)S(1)} collective-permute-done((f32[8,128]{1,0:T(8,128)S(1)}, f32[8,128]{1,0:T(8,128)S(1)}, u32[]{:S(2)}, u32[]{:S(2)}) %collective-permute-start.17) | collective-permute-done | bytes 4128 | tf_op jit(solution)/shard_map/ppermute | solution.py:167
  74.4 0.8 shard_map.48
  75.1 1.2 %collective-permute-start.23 = (bf16[160,128]{1,0:T(8,128)(2,1)}, bf16[160,128]{1,0:T(8,128)(2,1)S(1)}, u32[]{:S(2)}, u32[]{:S(2)}) collective-permute-start(bf16[160,128]{1,0:T(8,128)(2,1)} %get-tuple-element.69), channel_id=1, source_target_pairs={{0,24},{1,25},{2,26},{3,27},{4,28},{5,29},{6,30},{7,31},{8,16},{9,... | collective-permute-start | bytes 122888 | tf_op jit(solution)/shard_map/ppermute | solution.py:167
  76.3 0.3 collective-permute-start.24
  76.6 2.9 %collective-permute-start.25 = (bf16[160,128]{1,0:T(8,128)(2,1)S(1)}, bf16[160,128]{1,0:T(8,128)(2,1)S(1)}, u32[]{:S(2)}, u32[]{:S(2)}) collective-permute-start(bf16[160,128]{1,0:T(8,128)(2,1)S(1)} %get-tuple-element.71), channel_id=1, source_target_pairs={{0,8},{1,9},{2,10},{3,11},{4,12},{5,13},{6,14},{7,15},{8,0},{9,1},... | collective-permute-start | bytes 122888 | tf_op jit(solution)/shard_map/ppermute | solution.py:167
  79.5 0.7 copy.4.refs_7_
  80.3 0.6 shard_map.49.refs_6_
  80.9 0.4 collective-permute-done.23.refs_3_
  81.3 0.8 collective-permute-done.24.refs_4_
  82.2 1.1 %shard_map.50 = bf16[32,256]{1,0:T(8,128)(2,1)} custom-call(s32[1]{0:T(128)} %bitcast.refs_0_, bf16[32,1,32,1200]{3,2,1,0:T(8,128)(2,1)S(1)} %copy-done, bf16[160,128]{1,0:T(8,128)(2,1)S(1)} %get-tuple-element.68.refs_6_.refs_2_, bf16[160,128]{1,0:T(8,128)(2,1)S(1)} %collective-permute-done.23.refs_3_, bf16[160,128]{1,0:T(8,128)(2,1)S(1)} %collective-permute-done.24.refs_4_, ...), custom_call_target="tpu_custom_call" | custom-call | flops 9830400 | bytes 1228800 | tf_op jit(solution)/shard_map/pallas_call | solution.py:47
  (29 shorter events, 0.2 us)
Async XLA Ops:
  0.0 1.8 %copy-start = (bf16[32,1,32,1200]{3,2,1,0:T(8,128)(2,1)S(1)}, bf16[32,1,32,1200]{3,2,1,0:T(8,128)(2,1)}, u32[]{:S(2)}) copy-start(bf16[32,1,32,1200]{3,2,1,0:T(8,128)(2,1)} %refs_1_.11) | copy-start | bytes 7372804
  2.0 12.9 %collective-permute-start.1 = (bf16[4,152,128]{2,1,0:T(8,128)(2,1)S(1)}, bf16[4,152,128]{2,1,0:T(8,128)(2,1)S(1)}, u32[]{:S(2)}, u32[]{:S(2)}) collective-permute-start(bf16[4,152,128]{2,1,0:T(8,128)(2,1)S(1)} %get-tuple-element.41.refs_2_), channel_id=1, source_target_pairs={{0,16},{1,17},{2,18},{3,19},{4,20},{5,21},{6,22},{7,23},{8,24},{9,... | collective-permute-start | bytes 466952 | tf_op jit(solution)/shard_map/ppermute | solution.py:167
  6.1 21.5 %copy-start.1 = (bf16[1,1200,1200]{2,1,0:T(8,128)(2,1)S(1)}, bf16[1,1200,1200]{2,1,0:T(8,128)(2,1)}, u32[]{:S(2)}) copy-start(bf16[1,1200,1200]{2,1,0:T(8,128)(2,1)} %refs_4_.3) | copy-start | bytes 8640004
  6.1 8.8 %collective-permute-start.2 = (bf16[4,152,128]{2,1,0:T(8,128)(2,1)S(1)}, bf16[4,152,128]{2,1,0:T(8,128)(2,1)S(1)}, u32[]{:S(2)}, u32[]{:S(2)}) collective-permute-start(bf16[4,152,128]{2,1,0:T(8,128)(2,1)S(1)} %get-tuple-element.42), channel_id=1, source_target_pairs={{0,8},{1,9},{2,10},{3,11},{4,12},{5,13},{6,14},{7,15},{8,0},{9,1},... | collective-permute-start | bytes 466952 | tf_op jit(solution)/shard_map/ppermute | solution.py:167
  7.8 13.3 %collective-permute-start.6 = (bf16[4,304,128]{2,1,0:T(8,128)(2,1)S(1)}, bf16[4,304,128]{2,1,0:T(8,128)(2,1)S(1)}, u32[]{:S(2)}, u32[]{:S(2)}) collective-permute-start(bf16[4,304,128]{2,1,0:T(8,128)(2,1)S(1)} %get-tuple-element.43.refs_2_), channel_id=1, source_target_pairs={{0,6},{1,7},{2,4},{3,5},{4,2},{5,3},{6,0},{7,1},{8,14},{9,15},{10,... | collective-permute-start | bytes 933896 | tf_op jit(solution)/shard_map/ppermute | solution.py:167
  10.3 7.7 %collective-permute-start = (bf16[4,152,128]{2,1,0:T(8,128)(2,1)S(1)}, bf16[4,152,128]{2,1,0:T(8,128)(2,1)S(1)}, u32[]{:S(2)}, u32[]{:S(2)}) collective-permute-start(bf16[4,152,128]{2,1,0:T(8,128)(2,1)S(1)} %shard_map.37.refs_2_), channel_id=1, source_target_pairs={{0,24},{1,25},{2,26},{3,27},{4,28},{5,29},{6,30},{7,31},{8,16},{9,... | collective-permute-start | bytes 466952 | tf_op jit(solution)/shard_map/ppermute | solution.py:167
  10.6 15.4 %collective-permute-start.7 = (bf16[4,304,128]{2,1,0:T(8,128)(2,1)S(1)}, bf16[4,304,128]{2,1,0:T(8,128)(2,1)S(1)}, u32[]{:S(2)}, u32[]{:S(2)}) collective-permute-start(bf16[4,304,128]{2,1,0:T(8,128)(2,1)S(1)} %get-tuple-element.49), channel_id=1, source_target_pairs={{0,7},{1,6},{2,5},{3,4},{4,3},{5,2},{6,1},{7,0},{8,15},{9,14},{10,... | collective-permute-start | bytes 933896 | tf_op jit(solution)/shard_map/ppermute | solution.py:167
  18.0 7.9 %collective-permute-start.3 = (bf16[4,152,128]{2,1,0:T(8,128)(2,1)S(1)}, bf16[4,152,128]{2,1,0:T(8,128)(2,1)S(1)}, u32[]{:S(2)}, u32[]{:S(2)}) collective-permute-start(bf16[4,152,128]{2,1,0:T(8,128)(2,1)S(1)} %get-tuple-element.46), channel_id=1, source_target_pairs={{0,1},{1,0},{2,3},{3,2},{4,5},{5,4},{6,7},{7,6},{8,9},{9,8},{10,11... | collective-permute-start | bytes 466952 | tf_op jit(solution)/shard_map/ppermute | solution.py:167
  18.1 9.4 %collective-permute-start.4 = (bf16[4,152,128]{2,1,0:T(8,128)(2,1)S(1)}, bf16[4,152,128]{2,1,0:T(8,128)(2,1)S(1)}, u32[]{:S(2)}, u32[]{:S(2)}) collective-permute-start(bf16[4,152,128]{2,1,0:T(8,128)(2,1)S(1)} %get-tuple-element.47), channel_id=1, source_target_pairs={{0,2},{1,3},{2,0},{3,1},{4,6},{5,7},{6,4},{7,5},{8,10},{9,11},{10,... | collective-permute-start | bytes 466952 | tf_op jit(solution)/shard_map/ppermute | solution.py:167
  19.7 7.9 %collective-permute-start.5 = (bf16[4,152,128]{2,1,0:T(8,128)(2,1)S(1)}, bf16[4,152,128]{2,1,0:T(8,128)(2,1)S(1)}, u32[]{:S(2)}, u32[]{:S(2)}) collective-permute-start(bf16[4,152,128]{2,1,0:T(8,128)(2,1)S(1)} %get-tuple-element.48), channel_id=1, source_target_pairs={{0,4},{1,5},{2,6},{3,7},{4,0},{5,1},{6,2},{7,3},{8,12},{9,13},{10,... | collective-permute-start | bytes 466952 | tf_op jit(solution)/shard_map/ppermute | solution.py:167
  21.2 13.5 %collective-permute-start.10 = (bf16[2,304,128]{2,1,0:T(8,128)(2,1)S(1)}, bf16[2,304,128]{2,1,0:T(8,128)(2,1)S(1)}, u32[]{:S(2)}, u32[]{:S(2)}) collective-permute-start(bf16[2,304,128]{2,1,0:T(8,128)(2,1)S(1)} %get-tuple-element.53), channel_id=1, source_target_pairs={{0,16},{1,17},{2,18},{3,19},{4,20},{5,21},{6,22},{7,23},{8,24},{9,... | collective-permute-start | bytes 466952 | tf_op jit(solution)/shard_map/ppermute | solution.py:167
  26.0 12.0 %collective-permute-start.11 = (bf16[2,304,128]{2,1,0:T(8,128)(2,1)S(1)}, bf16[2,304,128]{2,1,0:T(8,128)(2,1)S(1)}, u32[]{:S(2)}, u32[]{:S(2)}) collective-permute-start(bf16[2,304,128]{2,1,0:T(8,128)(2,1)S(1)} %get-tuple-element.54), channel_id=1, source_target_pairs={{0,8},{1,9},{2,10},{3,11},{4,12},{5,13},{6,14},{7,15},{8,0},{9,1},... | collective-permute-start | bytes 466952 | tf_op jit(solution)/shard_map/ppermute | solution.py:167
  26.0 11.9 %collective-permute-start.9 = (bf16[2,304,128]{2,1,0:T(8,128)(2,1)S(1)}, bf16[2,304,128]{2,1,0:T(8,128)(2,1)S(1)}, u32[]{:S(2)}, u32[]{:S(2)}) collective-permute-start(bf16[2,304,128]{2,1,0:T(8,128)(2,1)S(1)} %get-tuple-element.52), channel_id=1, source_target_pairs={{0,24},{1,25},{2,26},{3,27},{4,28},{5,29},{6,30},{7,31},{8,16},{9,... | collective-permute-start | bytes 466952 | tf_op jit(solution)/shard_map/ppermute | solution.py:167
  28.8 13.9 %collective-permute-start.14 = (bf16[4,152,128]{2,1,0:T(8,128)(2,1)S(1)}, bf16[4,152,128]{2,1,0:T(8,128)(2,1)S(1)}, u32[]{:S(2)}, u32[]{:S(2)}) collective-permute-start(bf16[4,152,128]{2,1,0:T(8,128)(2,1)S(1)} %get-tuple-element.58), channel_id=1, source_target_pairs={{0,1},{1,0},{2,3},{3,2},{4,5},{5,4},{6,7},{7,6},{8,9},{9,8},{10,11... | collective-permute-start | bytes 466952 | tf_op jit(solution)/shard_map/ppermute | solution.py:167
  38.0 21.3 %collective-permute-start.12 = (bf16[4,304,128]{2,1,0:T(8,128)(2,1)S(1)}, bf16[4,304,128]{2,1,0:T(8,128)(2,1)S(1)}, u32[]{:S(2)}, u32[]{:S(2)}) collective-permute-start(bf16[4,304,128]{2,1,0:T(8,128)(2,1)S(1)} %get-tuple-element.56.refs_3_), channel_id=1, source_target_pairs={{0,3},{1,2},{2,1},{3,0},{4,7},{5,6},{6,5},{7,4},{8,11},{9,10},{10,... | collective-permute-start | bytes 933896 | tf_op jit(solution)/shard_map/ppermute | solution.py:167
  38.8 20.5 %collective-permute-start.13 = (bf16[4,304,128]{2,1,0:T(8,128)(2,1)S(1)}, bf16[4,304,128]{2,1,0:T(8,128)(2,1)S(1)}, u32[]{:S(2)}, u32[]{:S(2)}) collective-permute-start(bf16[4,304,128]{2,1,0:T(8,128)(2,1)S(1)} %get-tuple-element.57), channel_id=1, source_target_pairs={{0,5},{1,4},{2,7},{3,6},{4,1},{5,0},{6,3},{7,2},{8,13},{9,12},{10,... | collective-permute-start | bytes 933896 | tf_op jit(solution)/shard_map/ppermute | solution.py:167
  39.8 11.2 %collective-permute-start.15 = (bf16[4,152,128]{2,1,0:T(8,128)(2,1)S(1)}, bf16[4,152,128]{2,1,0:T(8,128)(2,1)S(1)}, u32[]{:S(2)}, u32[]{:S(2)}) collective-permute-start(bf16[4,152,128]{2,1,0:T(8,128)(2,1)S(1)} %get-tuple-element.59), channel_id=1, source_target_pairs={{0,2},{1,3},{2,0},{3,1},{4,6},{5,7},{6,4},{7,5},{8,10},{9,11},{10,... | collective-permute-start | bytes 466952 | tf_op jit(solution)/shard_map/ppermute | solution.py:167
  41.3 12.4 %collective-permute-start.18 = (bf16[2,304,128]{2,1,0:T(8,128)(2,1)S(1)}, bf16[2,304,128]{2,1,0:T(8,128)(2,1)S(1)}, u32[]{:S(2)}, u32[]{:S(2)}) collective-permute-start(bf16[2,304,128]{2,1,0:T(8,128)(2,1)S(1)} %get-tuple-element.63), channel_id=1, source_target_pairs={{0,24},{1,25},{2,26},{3,27},{4,28},{5,29},{6,30},{7,31},{8,16},{9,... | collective-permute-start | bytes 466952 | tf_op jit(solution)/shard_map/ppermute | solution.py:167
  42.7 15.3 %collective-permute-start.19 = (bf16[2,304,128]{2,1,0:T(8,128)(2,1)S(1)}, bf16[2,304,128]{2,1,0:T(8,128)(2,1)S(1)}, u32[]{:S(2)}, u32[]{:S(2)}) collective-permute-start(bf16[2,304,128]{2,1,0:T(8,128)(2,1)S(1)} %get-tuple-element.64), channel_id=1, source_target_pairs={{0,16},{1,17},{2,18},{3,19},{4,20},{5,21},{6,22},{7,23},{8,24},{9,... | collective-permute-start | bytes 466952 | tf_op jit(solution)/shard_map/ppermute | solution.py:167
  50.9 13.2 %collective-permute-start.20 = (bf16[2,304,128]{2,1,0:T(8,128)(2,1)S(1)}, bf16[2,304,128]{2,1,0:T(8,128)(2,1)S(1)}, u32[]{:S(2)}, u32[]{:S(2)}) collective-permute-start(bf16[2,304,128]{2,1,0:T(8,128)(2,1)S(1)} %get-tuple-element.65), channel_id=1, source_target_pairs={{0,8},{1,9},{2,10},{3,11},{4,12},{5,13},{6,14},{7,15},{8,0},{9,1},... | collective-permute-start | bytes 466952 | tf_op jit(solution)/shard_map/ppermute | solution.py:167
  53.7 13.7 %collective-permute-start.8 = (bf16[4,152,128]{2,1,0:T(8,128)(2,1)S(1)}, bf16[4,152,128]{2,1,0:T(8,128)(2,1)S(1)}, u32[]{:S(2)}, u32[]{:S(2)}) collective-permute-start(bf16[4,152,128]{2,1,0:T(8,128)(2,1)S(1)} %get-tuple-element.51), channel_id=1, source_target_pairs={{0,4},{1,5},{2,6},{3,7},{4,0},{5,1},{6,2},{7,3},{8,12},{9,13},{10,... | collective-permute-start | bytes 466952 | tf_op jit(solution)/shard_map/ppermute | solution.py:167
  58.1 18.5 %collective-permute-start.26 = (bf16[3,152,128]{2,1,0:T(8,128)(2,1)S(1)}, bf16[3,152,128]{2,1,0:T(8,128)(2,1)S(1)}, u32[]{:S(2)}, u32[]{:S(2)}) collective-permute-start(bf16[3,152,128]{2,1,0:T(8,128)(2,1)S(1)} %get-tuple-element.72), channel_id=1, source_target_pairs={{0,24},{1,25},{2,26},{3,27},{4,28},{5,29},{6,30},{7,31},{8,16},{9,... | collective-permute-start | bytes 350216 | tf_op jit(solution)/shard_map/ppermute | solution.py:167
  59.3 21.0 %collective-permute-start.27 = (bf16[3,152,128]{2,1,0:T(8,128)(2,1)S(1)}, bf16[3,152,128]{2,1,0:T(8,128)(2,1)S(1)}, u32[]{:S(2)}, u32[]{:S(2)}) collective-permute-start(bf16[3,152,128]{2,1,0:T(8,128)(2,1)S(1)} %get-tuple-element.73), channel_id=1, source_target_pairs={{0,16},{1,17},{2,18},{3,19},{4,20},{5,21},{6,22},{7,23},{8,24},{9,... | collective-permute-start | bytes 350216 | tf_op jit(solution)/shard_map/ppermute | solution.py:167
  59.3 21.0 %collective-permute-start.28 = (bf16[3,152,128]{2,1,0:T(8,128)(2,1)S(1)}, bf16[3,152,128]{2,1,0:T(8,128)(2,1)S(1)}, u32[]{:S(2)}, u32[]{:S(2)}) collective-permute-start(bf16[3,152,128]{2,1,0:T(8,128)(2,1)S(1)} %get-tuple-element.74), channel_id=1, source_target_pairs={{0,8},{1,9},{2,10},{3,11},{4,12},{5,13},{6,14},{7,15},{8,0},{9,1},... | collective-permute-start | bytes 350216 | tf_op jit(solution)/shard_map/ppermute | solution.py:167
  65.8 4.6 %collective-permute-start.21 = (f32[8,128]{1,0:T(8,128)S(1)}, f32[8,128]{1,0:T(8,128)S(1)}, u32[]{:S(2)}, u32[]{:S(2)}) collective-permute-start(f32[8,128]{1,0:T(8,128)S(1)} %get-tuple-element.66), channel_id=1, source_target_pairs={{0,6},{1,7},{2,4},{3,5},{4,2},{5,3},{6,0},{7,1},{8,14},{9,15},{10,... | collective-permute-start | bytes 12296 | tf_op jit(solution)/shard_map/ppermute | solution.py:167
  67.4 3.9 %collective-permute-start.22 = (f32[8,128]{1,0:T(8,128)S(1)}, f32[8,128]{1,0:T(8,128)S(1)}, u32[]{:S(2)}, u32[]{:S(2)}) collective-permute-start(f32[8,128]{1,0:T(8,128)S(1)} %get-tuple-element.67), channel_id=1, source_target_pairs={{0,7},{1,6},{2,5},{3,4},{4,3},{5,2},{6,1},{7,0},{8,15},{9,14},{10,... | collective-permute-start | bytes 12296 | tf_op jit(solution)/shard_map/ppermute | solution.py:167
  70.4 3.0 %collective-permute-start.16 = (f32[8,128]{1,0:T(8,128)S(1)}, f32[8,128]{1,0:T(8,128)S(1)}, u32[]{:S(2)}, u32[]{:S(2)}) collective-permute-start(f32[8,128]{1,0:T(8,128)S(1)} %get-tuple-element.61.refs_5_), channel_id=1, source_target_pairs={{0,3},{1,2},{2,1},{3,0},{4,7},{5,6},{6,5},{7,4},{8,11},{9,10},{10,... | collective-permute-start | bytes 12296 | tf_op jit(solution)/shard_map/ppermute | solution.py:167
  71.3 3.0 %collective-permute-start.17 = (f32[8,128]{1,0:T(8,128)S(1)}, f32[8,128]{1,0:T(8,128)S(1)}, u32[]{:S(2)}, u32[]{:S(2)}) collective-permute-start(f32[8,128]{1,0:T(8,128)S(1)} %get-tuple-element.62), channel_id=1, source_target_pairs={{0,5},{1,4},{2,7},{3,6},{4,1},{5,0},{6,3},{7,2},{8,13},{9,12},{10,... | collective-permute-start | bytes 12296 | tf_op jit(solution)/shard_map/ppermute | solution.py:167
  75.1 6.2 %collective-permute-start.23 = (bf16[160,128]{1,0:T(8,128)(2,1)}, bf16[160,128]{1,0:T(8,128)(2,1)S(1)}, u32[]{:S(2)}, u32[]{:S(2)}) collective-permute-start(bf16[160,128]{1,0:T(8,128)(2,1)} %get-tuple-element.69), channel_id=1, source_target_pairs={{0,24},{1,25},{2,26},{3,27},{4,28},{5,29},{6,30},{7,31},{8,16},{9,... | collective-permute-start | bytes 122888 | tf_op jit(solution)/shard_map/ppermute | solution.py:167
  76.3 5.8 %collective-permute-start.24 = (bf16[160,128]{1,0:T(8,128)(2,1)}, bf16[160,128]{1,0:T(8,128)(2,1)S(1)}, u32[]{:S(2)}, u32[]{:S(2)}) collective-permute-start(bf16[160,128]{1,0:T(8,128)(2,1)} %get-tuple-element.70), channel_id=1, source_target_pairs={{0,16},{1,17},{2,18},{3,19},{4,20},{5,21},{6,22},{7,23},{8,24},{9,... | collective-permute-start | bytes 122888 | tf_op jit(solution)/shard_map/ppermute | solution.py:167
  76.6 5.6 %collective-permute-start.25 = (bf16[160,128]{1,0:T(8,128)(2,1)S(1)}, bf16[160,128]{1,0:T(8,128)(2,1)S(1)}, u32[]{:S(2)}, u32[]{:S(2)}) collective-permute-start(bf16[160,128]{1,0:T(8,128)(2,1)S(1)} %get-tuple-element.71), channel_id=1, source_target_pairs={{0,8},{1,9},{2,10},{3,11},{4,12},{5,13},{6,14},{7,15},{8,0},{9,1},... | collective-permute-start | bytes 122888 | tf_op jit(solution)/shard_map/ppermute | solution.py:167

commit v5 on v4

v5 whole, which is shorter than its diff:
```python
import jax
import jax.numpy as jnp
from jax import lax
from jax.experimental import pallas as pl
from jax.experimental.pallas import tpu as pltpu
from jax.sharding import PartitionSpec as P


STEP = 12
BF16, F32 = jnp.bfloat16, jnp.float32
LANES = 128
HALF = LANES // 2
COLS = 256


VM = pl.BlockSpec(memory_space=pltpu.VMEM)
SM = pl.BlockSpec(memory_space=pltpu.SMEM)
ANY = pl.BlockSpec(memory_space=pl.ANY)
HBM = pl.BlockSpec(memory_space=pltpu.HBM)


def split(devices):
    outer = 2 ** ((devices.bit_length() - 1) // 2)
    return outer, devices // outer


class Sizes:
    def __init__(self, shape, devices):
        self.q, _, both, self.ng = shape
        self.pairs = both // 2
        self.full, self.tail = divmod(self.ng, LANES)
        self.rows = self.pairs * self.full + (self.pairs // 2 if self.tail else 0)
        self.wide = LANES * (self.full + (1 if self.tail else 0))
        self.devices = devices
        self.outer, self.inner = split(devices)

    def fits(self):
        power = self.devices & (self.devices - 1) == 0
        return power and self.inner >= 4 and self.pairs == 16 and 0 < self.tail <= HALF


def call(kernel, outs, ins, specs, scratch=(), flops=0, moved=0, after=()):
    k, a = len(ins), len(after)

    def body(*refs):
        kernel(*refs[:k], *refs[k + a :])

    return pallas(body, outs, specs, a, scratch, flops, moved)(*ins, *after)


def pallas(body, outs, specs, a, scratch, flops, moved):
    return pl.pallas_call(
        body,
        out_shape=tuple(outs),
        in_specs=[*specs, *[ANY] * a],
        out_specs=tuple(pl.BlockSpec(memory_space=pltpu.VMEM) for _ in outs),
        scratch_shapes=list(scratch),
        compiler_params=pltpu.CompilerParams(vmem_limit_bytes=24 << 20),
        cost_estimate=pl.CostEstimate(flops=flops, bytes_accessed=moved, transcendentals=0),
    )


def pack(s, read, dst, b, base):
    n = s.pairs
    for j in range(s.full):
        dst[b, base + n * j : base + n * (j + 1), :] = read(LANES * j, LANES * (j + 1))
    last = read(LANES * s.full, s.wide).astype(F32)
    lane = lax.broadcasted_iota(jnp.int32, (n // 2, LANES), 1)
    folded = jnp.where(lane < HALF, last[: n // 2], pltpu.roll(last[n // 2 :], HALF, 1))
    dst[b, base + n * s.full : base + s.rows, :] = folded.astype(BF16)


def unpack(s, src, b, base, dst, row):
    n = s.pairs
    src = src if b is None else src.at[b]
    for j in range(s.full):
        dst[row : row + n, LANES * j : LANES * (j + 1)] = src[base + n * j : base + n * (j + 1), :]
    folded = src[base + n * s.full : base + s.rows, :].astype(F32)
    last = jnp.concatenate([folded, pltpu.roll(folded, HALF, 1)], axis=0).astype(BF16)
    dst[row : row + n, LANES * s.full : s.ng] = last[:, : s.tail]


def nt(x, y):
    return lax.dot_general(x, y, (((1,), (1,)), ((), ())), preferred_element_type=F32)


def screen(s, v, w_ref, out):
    for lo in range(0, s.ng, COLS):
        hi = min(lo + COLS, s.ng)
        out[:, lo:hi] = nt(v[...], w_ref[0, lo:hi, :]).astype(BF16)


def spread(s, c, sc):
    n, count = s.pairs, c.shape[0]
    full = nt(c, sc)
    r = lax.broadcasted_iota(jnp.int32, (count, count), 0)
    k = lax.broadcasted_iota(jnp.int32, (count, count), 1)
    own = jnp.where(r // n == k // n, full, 0.0).astype(BF16)
    e = lax.broadcasted_iota(jnp.int32, (count, n * n), 0)
    f = lax.broadcasted_iota(jnp.int32, (count, n * n), 1)
    copies = jnp.where(e % n == f % n, 1.0, 0.0).astype(BF16)
    x = jnp.dot(own, copies, preferred_element_type=F32)
    return jnp.where(f // n == e % n, x, 0.0).astype(BF16)


def pick(shape, wanted):
    row = lax.broadcasted_iota(jnp.int32, shape, 0)
    column = lax.broadcasted_iota(jnp.int32, shape, 1)
    return jnp.where(wanted(row, column), 1.0, 0.0).astype(BF16)


def table(index, values):
    out = jnp.zeros_like(index)
    for i, value in enumerate(values):
        out = jnp.where(index == i, value, out)
    return out


def rows_of_pairs(s, me, offsets, c, sc):
    x = spread(s, c, sc)
    place = pick((s.devices, x.shape[0]), lambda q, r: q == (table(r // s.pairs, offsets) ^ me))
    return jnp.dot(place, x, preferred_element_type=F32)


def gather(s, me, dens, offsets, half, buf, sem):
    lo, n = (0, 2 * s.pairs) if half is None else (half * s.pairs, s.pairs)
    copies = [
        pltpu.make_async_copy(dens.at[me ^ m, 0, pl.ds(lo, n), :], buf.at[i], sem.at[i])
        for i, m in enumerate(offsets)
    ]
    for c in copies:
        c.start()
    return copies


def reader(s, ref, row, edge):
    def read(lo, hi):
        if hi <= s.ng:
            return ref[row : row + s.pairs, lo:hi]
        edge[:, : s.tail] = ref[row : row + s.pairs, lo : s.ng]
        return edge[...]

    return read


def parts_of(devices):
    outer, count = split(devices)
    inner = sorted(range(count), key=lambda p: (bin(p).count("1"), p))
    quarter = count // 4
    low, middle = inner[:quarter] + inner[-quarter:], inner[quarter:-quarter]
    return (low, middle), (low, middle), far_of(outer)


def far_of(outer):
    return sorted(range(1, outer), key=lambda dz: (dz != outer // 2, -dz))


def fast(s, densities, weights, live):
    me_arr = lax.axis_index("pb").astype(jnp.int32).reshape(1)
    O, I, N, n = s.outer, s.inner, s.devices, s.pairs
    (out_first, in_first), (s_out, s_in), far = parts_of(N)
    order = [0, *far]
    block = n * s.ng

    def sds(*shape):
        return jax.ShapeDtypeStruct(shape, BF16)

    def hop(x, m):
        if m == 0:
            return x
        return lax.ppermute(x, "pb", [(d, d ^ m) for d in range(N)])

    def outer_hops(xs):
        return [xs[0]] + [hop(x, dz * I) for dz, x in zip(far, xs[1:])]

    def inner_hops(xs, ps):
        return [hop(x, p) for x, p in zip(xs, ps)]

    def take_v0(me_ref, dens, out, buf, edge, sem):
        offs = [far[0] * I + p for p in out_first]
        for i, c in enumerate(gather(s, me_ref[0], dens, offs, 1, buf, sem)):
            c.wait()
            pack(s, reader(s, buf.at[i], 0, edge.at[i]), out, i, 0)

    k = len(out_first)
    first = call(
        take_v0,
        [sds(k, s.rows, LANES)],
        (me_arr, pltpu.with_memory_space_constraint(densities, pltpu.HBM)),
        [SM, HBM],
        [pltpu.VMEM((k, n, s.ng), BF16), pltpu.VMEM((k, n, LANES), BF16), pltpu.SemaphoreType.DMA((k,))],
        moved=4 * k * block,
    )

    def take(picks, after):
        count = len(picks[0])

        def kernel(me_ref, dens, *refs):
            outs, edge = refs[: len(picks)], refs[len(picks)]
            for o, chosen in enumerate(picks):
                for i, m in enumerate(chosen):
                    pack(s, reader(s, dens.at[me_ref[0] ^ m, 0], n, edge.at[o * count + i]), outs[o], i, 0)

        return call(
            kernel,
            [sds(count, s.rows, LANES)] * len(picks),
            (me_arr, densities),
            [SM, VM],
            [pltpu.VMEM((len(picks) * count, n, LANES), BF16)],
            moved=4 * len(picks) * count * block,
            after=after,
        )

    def turn(ins, after=()):
        count = ins[0].shape[0]

        def kernel(*refs):
            src, outs = refs[: len(ins)], refs[len(ins) :]
            for i, o in enumerate(outs):
                for j, x in enumerate(src):
                    o[j] = x[i]

        return call(
            kernel,
            [sds(len(ins), s.rows, LANES)] * count,
            ins,
            [VM] * len(ins),
            moved=4 * len(ins) * count * block,
            after=after,
        )

    sent = take([[dz * I + p for dz in order] for p in in_first], (first[0],))
    near = inner_hops(sent, in_first)
    rest = take([[dz * I + p for p in out_first] for dz in [*far[1:], 0]], (sent[0],))
    vz = outer_hops([rest[-1], *first, *rest[:-1]])
    wz = outer_hops(turn(near, (rest[0],)))
    pieces = turn(vz, (wz[0],))
    vin = inner_hops(pieces, out_first)

    def screened(ins, picks, shapes, after):
        rows = n * len(picks)

        def kernel(*refs):
            src, w_ref, outs, (v, sc) = refs[: len(ins)], refs[len(ins)], refs[len(ins) + 1 : -2], refs[-2:]
            for x, (a, b, _, _) in enumerate(picks):
                unpack(s, src[a], b, 0, v, n * x)
            screen(s, v, w_ref, sc)
            for x, (_, _, o, i) in enumerate(picks):
                pack(s, lambda lo, hi, row=n * x: sc[row : row + n, lo:hi], outs[o], i, 0)

        return call(
            kernel,
            [sds(count, s.rows, LANES) for count in shapes],
            (*ins, weights),
            [VM] * (len(ins) + 1),
            [pltpu.VMEM((rows, s.ng), BF16), pltpu.VMEM((rows, s.wide), BF16)],
            flops=2 * rows * s.ng * s.ng,
            moved=2 * s.ng * s.ng,
            after=after,
        )

    low, extra = len(s_out), out_first[len(s_out) :]
    picks = [(j, zi, zi, j) for j in range(low) for zi in range(O)]
    picks += [(low + j, zi, O + j, zi) for j in range(len(extra)) for zi in range(O)]
    made = screened(vin, picks, [low] * O + [O] * len(extra), (pieces[0],))
    s1z = outer_hops(made[:O])
    early = inner_hops(made[O:], extra)
    count = len(in_first)
    picks = [(zi, j, j, zi) for j in range(count) for zi in range(O)]
    made = screened(wz, picks, [O] * count, (made[0],))
    sin = early + inner_hops(made, in_first)
    s2z = outer_hops(turn(sin))
    fin = inner_hops(turn(s1z, (s2z[0],)), s_out)

    def finish(ins, picks, others, after=()):
        rows, last = n * len(picks), len(others) > 0

        def kernel(me_ref, dens, *refs):
            src, more, (out, c, sc) = refs[: len(ins)], refs[len(ins) : -3], refs[-3:]
            me = me_ref[0]
            for x, (a, b, m) in enumerate(picks):
                c[n * x : n * (x + 1), :] = dens[me ^ m, 0, :n, :]
                unpack(s, src[a], b, 0, sc, n * x)
            r, step = 0.0, STEP * n
            for lo in range(0, rows, step):
                hi = min(lo + step, rows)
                offs = [m for _, _, m in picks[lo // n : hi // n]]
                r = r + rows_of_pairs(s, me, offs, c[lo:hi, :], sc[lo:hi, :])
            if last:
                before, live_ref = more
                out[...] = ((r + before[...]) * live_ref[...].astype(F32)).astype(BF16)
            else:
                out[...] = r

        return call(
            kernel,
            [jax.ShapeDtypeStruct((N, n * n), BF16 if last else F32)],
            (me_arr, densities, *ins, *others),
            [SM] + [VM] * (1 + len(ins) + len(others)),
            [pltpu.VMEM((rows, s.ng), BF16)] * 2,
            flops=2 * rows * s.ng * n,
            moved=4 * rows * s.ng,
            after=after,
        )[0]

    picks = [(j, zi, dz * I + p) for j, p in enumerate(s_out) for zi, dz in enumerate(order)]
    picks += [(len(s_out), j, p) for j, p in enumerate(s_in)]
    partial = finish([*fin, s2z[0]], picks, ())
    picks = [(zi, j, dz * I + p) for zi, dz in enumerate(far) for j, p in enumerate(s_in)]
    return finish(s2z[1:], picks, (partial, live))[:, None, :]


def plain(densities, screening, live):
    pairs = densities.shape[2] // 2
    arrived = lax.all_to_all(densities, "pb", split_axis=0, concat_axis=0, tiled=True)
    screened = jnp.einsum(
        "nkbh,gh->nkbg", arrived[:, :, pairs:, :], screening[0], preferred_element_type=F32
    ).astype(BF16)
    blocks = jnp.einsum("nkag,nkbg->nkab", arrived[:, :, :pairs, :], screened, preferred_element_type=F32)
    blocks = blocks.reshape(blocks.shape[0], blocks.shape[1], -1).astype(BF16)
    result = lax.all_to_all(blocks, "pb", split_axis=0, concat_axis=0, tiled=True)
    return result * live.astype(BF16)[:, :, None]


def solution(mesh):
    devices = mesh.shape["pb"]

    def on_device(densities, screening, live):
        s = Sizes(densities.shape, devices)
        if s.q == devices and s.fits():
            return fast(s, densities, screening, live)
        return plain(densities, screening, live)

    in_specs = (P(None, "pb", None, None), P("pb", None, None), P(None, "pb"))
    return jax.shard_map(
        on_device, mesh=mesh, in_specs=in_specs, out_specs=P(None, "pb", None), check_vma=False
    )
```

time: 83.4 us -> 84.3 us (1.011)
  waiting for transfers between devices: 33.9 us -> 36.6 us
  starting transfers between devices: 38.9 us -> 36.5 us
    ppermute x29 -> x26, waiting for transfers between devices: 33.9 us -> 36.6 us  [hop(): return lax.ppermute(x, 'pb', [(d, d ^ m) for d in range(N)])]
    ppermute x29 -> x26, starting transfers between devices: 38.9 us -> 36.5 us  [hop(): return lax.ppermute(x, 'pb', [(d, d ^ m) for d in range(N)])]
    unnamed x5 -> x7, local copies, waits for them, and re-layouts: 1.25 us -> 1.86 us
    pallas_call x14 -> x11, Pallas kernels: 9.07 us -> 9.05 us  [call(): return pallas(body, outs, specs, a, scratch, flops, moved)(*ins, *after)]
  transfers between devices with their start and end apart: 29 -> 26, of which waited for: 12 -> 13; matrix products, arithmetic and copies ran while one was open for 1% -> 2% of each run, Pallas kernels for 8% -> 4%
where the time goes in v5:
time: 84.3 us; the launch traced here: 84.1 us
  waiting for transfers between devices  36.6 us (43%)
  starting transfers between devices  36.5 us (43%)
  Pallas kernels  9.05 us (11%)
  local copies, waits for them, and re-layouts  1.86 us (2%)
    ppermute x26, waiting for transfers between devices, hop(): return lax.ppermute(x, 'pb', [(d, d ^ m) for d in range(N)])  36.6 us
    ppermute x26, starting transfers between devices, hop(): return lax.ppermute(x, 'pb', [(d, d ^ m) for d in range(N)])  36.5 us
    pallas_call x11, Pallas kernels, call(): return pallas(body, outs, specs, a, scratch, flops, moved)(*ins, *after)  9.05 us
    unnamed x7, local copies, waits for them, and re-layouts  1.86 us
  transfers between devices with their start and end apart: 26, of which 13 were waited for; matrix products, arithmetic and copies ran while one was open for 2% of the time, Pallas kernels for 4%

profile of v5, /device:TPU:0, one launch (start us, length us, event | category | flops | bytes accessed | tf_op | source)
XLA Modules:
  0.0 84.1 jit_solution(7877455172721011136)
XLA Ops:
  0.0 1.3 %shard_map.37.refs_2_ = bf16[4,152,128]{2,1,0:T(8,128)(2,1)S(1)} custom-call(s32[1]{0:T(128)} %bitcast.refs_0_, bf16[32,1,32,1200]{3,2,1,0:T(8,128)(2,1)} %refs_1_.9), custom_call_target="tpu_custom_call" | custom-call | bytes 307200 | tf_op jit(solution)/shard_map/pallas_call | solution.py:48
  1.3 0.5 copy-done
  1.8 0.2 shard_map.38
  2.0 3.0 %collective-permute-start = (bf16[4,152,128]{2,1,0:T(8,128)(2,1)S(1)}, bf16[4,152,128]{2,1,0:T(8,128)(2,1)S(1)}, u32[]{:S(2)}, u32[]{:S(2)}) collective-permute-start(bf16[4,152,128]{2,1,0:T(8,128)(2,1)S(1)} %get-tuple-element.36.refs_2_), channel_id=1, source_target_pairs={{0,2},{1,3},{2,0},{3,1},{4,6},{5,7},{6,4},{7,5},{8,10},{9,11},{10,... | collective-permute-start | bytes 466952 | tf_op jit(solution)/shard_map/ppermute | solution.py:171
  5.0 1.5 %collective-permute-start.1 = (bf16[4,152,128]{2,1,0:T(8,128)(2,1)S(1)}, bf16[4,152,128]{2,1,0:T(8,128)(2,1)S(1)}, u32[]{:S(2)}, u32[]{:S(2)}) collective-permute-start(bf16[4,152,128]{2,1,0:T(8,128)(2,1)S(1)} %get-tuple-element.37), channel_id=1, source_target_pairs={{0,4},{1,5},{2,6},{3,7},{4,0},{5,1},{6,2},{7,3},{8,12},{9,13},{10,... | collective-permute-start | bytes 466952 | tf_op jit(solution)/shard_map/ppermute | solution.py:171
  6.5 0.0 collective-permute-start.2
  6.5 0.3 collective-permute-start.3
  6.8 0.2 shard_map.39
  7.0 4.1 %collective-permute-start.8 = (bf16[4,152,128]{2,1,0:T(8,128)(2,1)S(1)}, bf16[4,152,128]{2,1,0:T(8,128)(2,1)S(1)}, u32[]{:S(2)}, u32[]{:S(2)}) collective-permute-start(bf16[4,152,128]{2,1,0:T(8,128)(2,1)S(1)} %get-tuple-element.40.refs_4_), channel_id=1, source_target_pairs={{0,24},{1,25},{2,26},{3,27},{4,28},{5,29},{6,30},{7,31},{8,16},{9,... | collective-permute-start | bytes 466952 | tf_op jit(solution)/shard_map/ppermute | solution.py:171
  11.1 0.0 collective-permute-done.refs_0_
  11.1 0.0 collective-permute-start.9
  11.1 0.4 collective-permute-done.1.refs_1_
  11.5 2.6 %collective-permute-start.7 = (bf16[4,152,128]{2,1,0:T(8,128)(2,1)S(1)}, bf16[4,152,128]{2,1,0:T(8,128)(2,1)S(1)}, u32[]{:S(2)}, u32[]{:S(2)}) collective-permute-start(bf16[4,152,128]{2,1,0:T(8,128)(2,1)S(1)} %shard_map.37.refs_2_), channel_id=1, source_target_pairs={{0,16},{1,17},{2,18},{3,19},{4,20},{5,21},{6,22},{7,23},{8,24},{9,... | collective-permute-start | bytes 466952 | tf_op jit(solution)/shard_map/ppermute | solution.py:171
  14.1 1.9 %collective-permute-done.8.refs_2_ = bf16[4,152,128]{2,1,0:T(8,128)(2,1)S(1)} collective-permute-done((bf16[4,152,128]{2,1,0:T(8,128)(2,1)S(1)}, bf16[4,152,128]{2,1,0:T(8,128)(2,1)S(1)}, u32[]{:S(2)}, u32[]{:S(2)}) %collective-permute-start.8) | collective-permute-done | bytes 155680 | tf_op jit(solution)/shard_map/ppermute | solution.py:171
  16.0 3.6 %collective-permute-done.9.refs_3_ = bf16[4,152,128]{2,1,0:T(8,128)(2,1)S(1)} collective-permute-done((bf16[4,152,128]{2,1,0:T(8,128)(2,1)S(1)}, bf16[4,152,128]{2,1,0:T(8,128)(2,1)S(1)}, u32[]{:S(2)}, u32[]{:S(2)}) %collective-permute-start.9) | collective-permute-done | bytes 155680 | tf_op jit(solution)/shard_map/ppermute | solution.py:171
  19.6 4.7 %collective-permute-done.7.refs_1_ = bf16[4,152,128]{2,1,0:T(8,128)(2,1)S(1)} collective-permute-done((bf16[4,152,128]{2,1,0:T(8,128)(2,1)S(1)}, bf16[4,152,128]{2,1,0:T(8,128)(2,1)S(1)}, u32[]{:S(2)}, u32[]{:S(2)}) %collective-permute-start.7) | collective-permute-done | bytes 155680 | tf_op jit(solution)/shard_map/ppermute | solution.py:171
  24.4 0.1 collective-permute-start.10
  24.5 1.9 %collective-permute-start.11 = (bf16[4,152,128]{2,1,0:T(8,128)(2,1)S(1)}, bf16[4,152,128]{2,1,0:T(8,128)(2,1)S(1)}, u32[]{:S(2)}, u32[]{:S(2)}) collective-permute-start(bf16[4,152,128]{2,1,0:T(8,128)(2,1)S(1)} %get-tuple-element.49), channel_id=1, source_target_pairs={{0,6},{1,7},{2,4},{3,5},{4,2},{5,3},{6,0},{7,1},{8,14},{9,15},{10,... | collective-permute-start | bytes 466952 | tf_op jit(solution)/shard_map/ppermute | solution.py:171
  26.4 0.9 %collective-permute-start.12 = (bf16[4,152,128]{2,1,0:T(8,128)(2,1)S(1)}, bf16[4,152,128]{2,1,0:T(8,128)(2,1)S(1)}, u32[]{:S(2)}, u32[]{:S(2)}) collective-permute-start(bf16[4,152,128]{2,1,0:T(8,128)(2,1)S(1)} %get-tuple-element.50), channel_id=1, source_target_pairs={{0,7},{1,6},{2,5},{3,4},{4,3},{5,2},{6,1},{7,0},{8,15},{9,14},{10,... | collective-permute-start | bytes 466952 | tf_op jit(solution)/shard_map/ppermute | solution.py:171
  27.2 0.3 collective-permute-start.4
  27.5 2.2 %collective-permute-start.5 = (bf16[4,152,128]{2,1,0:T(8,128)(2,1)S(1)}, bf16[4,152,128]{2,1,0:T(8,128)(2,1)S(1)}, u32[]{:S(2)}, u32[]{:S(2)}) collective-permute-start(bf16[4,152,128]{2,1,0:T(8,128)(2,1)S(1)} %get-tuple-element.43), channel_id=1, source_target_pairs={{0,24},{1,25},{2,26},{3,27},{4,28},{5,29},{6,30},{7,31},{8,16},{9,... | collective-permute-start | bytes 466952 | tf_op jit(solution)/shard_map/ppermute | solution.py:171
  29.7 1.0 %collective-permute-start.6 = (bf16[4,152,128]{2,1,0:T(8,128)(2,1)S(1)}, bf16[4,152,128]{2,1,0:T(8,128)(2,1)S(1)}, u32[]{:S(2)}, u32[]{:S(2)}) collective-permute-start(bf16[4,152,128]{2,1,0:T(8,128)(2,1)S(1)} %get-tuple-element.44), channel_id=1, source_target_pairs={{0,8},{1,9},{2,10},{3,11},{4,12},{5,13},{6,14},{7,15},{8,0},{9,1},... | collective-permute-start | bytes 466952 | tf_op jit(solution)/shard_map/ppermute | solution.py:171
  30.7 1.6 %collective-permute-done.11.refs_2_ = bf16[4,152,128]{2,1,0:T(8,128)(2,1)S(1)} collective-permute-done((bf16[4,152,128]{2,1,0:T(8,128)(2,1)S(1)}, bf16[4,152,128]{2,1,0:T(8,128)(2,1)S(1)}, u32[]{:S(2)}, u32[]{:S(2)}) %collective-permute-start.11) | collective-permute-done | bytes 155680 | tf_op jit(solution)/shard_map/ppermute | solution.py:171
  32.3 2.3 %collective-permute-done.12.refs_3_ = bf16[4,152,128]{2,1,0:T(8,128)(2,1)S(1)} collective-permute-done((bf16[4,152,128]{2,1,0:T(8,128)(2,1)S(1)}, bf16[4,152,128]{2,1,0:T(8,128)(2,1)S(1)}, u32[]{:S(2)}, u32[]{:S(2)}) %collective-permute-start.12) | collective-permute-done | bytes 155680 | tf_op jit(solution)/shard_map/ppermute | solution.py:171
  34.6 1.3 %shard_map.42 = (bf16[4,152,128]{2,1,0:T(8,128)(2,1)S(1)}, bf16[4,152,128]{2,1,0:T(8,128)(2,1)S(1)}, bf16[4,152,128]{2,1,0:T(8,128)(2,1)S(1)}, bf16[4,152,128]{2,1,0:T(8,128)(2,1)S(1)}) custom-call(bf16[4,152,128]{2,1,0:T(8,128)(2,1)S(1)} %get-tuple-element.47.refs_0_.refs_5_, bf16[4,152,128]{2,1,0:T(8,128)(2,1)S(1)} %collective-permute-done.10.refs_1_, ...), custom_call_target="tpu_custom_call" | custom-call | flops 737280000 | bytes 2880000 | tf_op jit(solution)/shard_map/pallas_call | solution.py:48
  35.9 5.1 %collective-permute-done.4.refs_1_ = bf16[4,152,128]{2,1,0:T(8,128)(2,1)S(1)} collective-permute-done((bf16[4,152,128]{2,1,0:T(8,128)(2,1)S(1)}, bf16[4,152,128]{2,1,0:T(8,128)(2,1)S(1)}, u32[]{:S(2)}, u32[]{:S(2)}) %collective-permute-start.4) | collective-permute-done | bytes 155680 | tf_op jit(solution)/shard_map/ppermute | solution.py:171
  41.0 1.3 %collective-permute-done.6.refs_3_ = bf16[4,152,128]{2,1,0:T(8,128)(2,1)S(1)} collective-permute-done((bf16[4,152,128]{2,1,0:T(8,128)(2,1)S(1)}, bf16[4,152,128]{2,1,0:T(8,128)(2,1)S(1)}, u32[]{:S(2)}, u32[]{:S(2)}) %collective-permute-start.6) | collective-permute-done | bytes 155680 | tf_op jit(solution)/shard_map/ppermute | solution.py:171
  42.3 1.3 %shard_map.43 = (bf16[4,152,128]{2,1,0:T(8,128)(2,1)S(1)}, bf16[4,152,128]{2,1,0:T(8,128)(2,1)S(1)}, bf16[4,152,128]{2,1,0:T(8,128)(2,1)S(1)}, bf16[4,152,128]{2,1,0:T(8,128)(2,1)S(1)}) custom-call(bf16[4,152,128]{2,1,0:T(8,128)(2,1)S(1)} %get-tuple-element.41.refs_4_.refs_0_, bf16[4,152,128]{2,1,0:T(8,128)(2,1)S(1)} %collective-permute-done.4.refs_1_, ...), custom_call_target="tpu_custom_call" | custom-call | flops 737280000 | bytes 2880000 | tf_op jit(solution)/shard_map/pallas_call | solution.py:48
  43.5 1.6 %collective-permute-start.13 = (bf16[4,152,128]{2,1,0:T(8,128)(2,1)S(1)}, bf16[4,152,128]{2,1,0:T(8,128)(2,1)S(1)}, u32[]{:S(2)}, u32[]{:S(2)}) collective-permute-start(bf16[4,152,128]{2,1,0:T(8,128)(2,1)S(1)} %get-tuple-element.52), channel_id=1, source_target_pairs={{0,2},{1,3},{2,0},{3,1},{4,6},{5,7},{6,4},{7,5},{8,10},{9,11},{10,... | collective-permute-start | bytes 466952 | tf_op jit(solution)/shard_map/ppermute | solution.py:171
  45.1 0.9 %collective-permute-start.14 = (bf16[4,152,128]{2,1,0:T(8,128)(2,1)S(1)}, bf16[4,152,128]{2,1,0:T(8,128)(2,1)S(1)}, u32[]{:S(2)}, u32[]{:S(2)}) collective-permute-start(bf16[4,152,128]{2,1,0:T(8,128)(2,1)S(1)} %get-tuple-element.53), channel_id=1, source_target_pairs={{0,4},{1,5},{2,6},{3,7},{4,0},{5,1},{6,2},{7,3},{8,12},{9,13},{10,... | collective-permute-start | bytes 466952 | tf_op jit(solution)/shard_map/ppermute | solution.py:171
  46.0 1.3 %collective-permute-start.16 = (bf16[4,152,128]{2,1,0:T(8,128)(2,1)S(1)}, bf16[4,152,128]{2,1,0:T(8,128)(2,1)S(1)}, u32[]{:S(2)}, u32[]{:S(2)}) collective-permute-start(bf16[4,152,128]{2,1,0:T(8,128)(2,1)S(1)} %get-tuple-element.55), channel_id=1, source_target_pairs={{0,5},{1,4},{2,7},{3,6},{4,1},{5,0},{6,3},{7,2},{8,13},{9,12},{10,... | collective-permute-start | bytes 466952 | tf_op jit(solution)/shard_map/ppermute | solution.py:171
  47.4 2.5 %collective-permute-start.20 = (bf16[4,152,128]{2,1,0:T(8,128)(2,1)S(1)}, bf16[4,152,128]{2,1,0:T(8,128)(2,1)S(1)}, u32[]{:S(2)}, u32[]{:S(2)}) collective-permute-start(bf16[4,152,128]{2,1,0:T(8,128)(2,1)S(1)} %get-tuple-element.59), channel_id=1, source_target_pairs={{0,16},{1,17},{2,18},{3,19},{4,20},{5,21},{6,22},{7,23},{8,24},{9,... | collective-permute-start | bytes 466952 | tf_op jit(solution)/shard_map/ppermute | solution.py:171
  49.9 2.5 %collective-permute-start.21 = (bf16[4,152,128]{2,1,0:T(8,128)(2,1)S(1)}, bf16[4,152,128]{2,1,0:T(8,128)(2,1)S(1)}, u32[]{:S(2)}, u32[]{:S(2)}) collective-permute-start(bf16[4,152,128]{2,1,0:T(8,128)(2,1)S(1)} %get-tuple-element.60), channel_id=1, source_target_pairs={{0,24},{1,25},{2,26},{3,27},{4,28},{5,29},{6,30},{7,31},{8,16},{9,... | collective-permute-start | bytes 466952 | tf_op jit(solution)/shard_map/ppermute | solution.py:171
  52.3 2.2 %collective-permute-start.22 = (bf16[4,152,128]{2,1,0:T(8,128)(2,1)S(1)}, bf16[4,152,128]{2,1,0:T(8,128)(2,1)S(1)}, u32[]{:S(2)}, u32[]{:S(2)}) collective-permute-start(bf16[4,152,128]{2,1,0:T(8,128)(2,1)S(1)} %get-tuple-element.61), channel_id=1, source_target_pairs={{0,8},{1,9},{2,10},{3,11},{4,12},{5,13},{6,14},{7,15},{8,0},{9,1},... | collective-permute-start | bytes 466952 | tf_op jit(solution)/shard_map/ppermute | solution.py:171
  54.6 0.8 shard_map.44
  55.4 6.5 %collective-permute-done.20.refs_1_ = bf16[4,152,128]{2,1,0:T(8,128)(2,1)S(1)} collective-permute-done((bf16[4,152,128]{2,1,0:T(8,128)(2,1)S(1)}, bf16[4,152,128]{2,1,0:T(8,128)(2,1)S(1)}, u32[]{:S(2)}, u32[]{:S(2)}) %collective-permute-start.20) | collective-permute-done | bytes 155680 | tf_op jit(solution)/shard_map/ppermute | solution.py:171
  61.9 0.2 collective-permute-done.22.refs_3_
  62.1 0.8 shard_map.45
  62.9 1.5 %collective-permute-start.24 = (bf16[4,152,128]{2,1,0:T(8,128)(2,1)}, bf16[4,152,128]{2,1,0:T(8,128)(2,1)S(1)}, u32[]{:S(2)}, u32[]{:S(2)}) collective-permute-start(bf16[4,152,128]{2,1,0:T(8,128)(2,1)} %get-tuple-element.65), channel_id=1, source_target_pairs={{0,6},{1,7},{2,4},{3,5},{4,2},{5,3},{6,0},{7,1},{8,14},{9,15},{10,... | collective-permute-start | bytes 466952 | tf_op jit(solution)/shard_map/ppermute | solution.py:171
  64.3 1.3 %collective-permute-start.25 = (bf16[4,152,128]{2,1,0:T(8,128)(2,1)}, bf16[4,152,128]{2,1,0:T(8,128)(2,1)S(1)}, u32[]{:S(2)}, u32[]{:S(2)}) collective-permute-start(bf16[4,152,128]{2,1,0:T(8,128)(2,1)} %get-tuple-element.66), channel_id=1, source_target_pairs={{0,7},{1,6},{2,5},{3,4},{4,3},{5,2},{6,1},{7,0},{8,15},{9,14},{10,... | collective-permute-start | bytes 466952 | tf_op jit(solution)/shard_map/ppermute | solution.py:171
  65.6 3.4 %collective-permute-start.17 = (bf16[4,152,128]{2,1,0:T(8,128)(2,1)}, bf16[4,152,128]{2,1,0:T(8,128)(2,1)S(1)}, u32[]{:S(2)}, u32[]{:S(2)}) collective-permute-start(bf16[4,152,128]{2,1,0:T(8,128)(2,1)} %get-tuple-element.56), channel_id=1, source_target_pairs={{0,16},{1,17},{2,18},{3,19},{4,20},{5,21},{6,22},{7,23},{8,24},{9,... | collective-permute-start | bytes 466952 | tf_op jit(solution)/shard_map/ppermute | solution.py:171
  69.0 1.5 %collective-permute-start.18 = (bf16[4,152,128]{2,1,0:T(8,128)(2,1)}, bf16[4,152,128]{2,1,0:T(8,128)(2,1)}, u32[]{:S(2)}, u32[]{:S(2)}) collective-permute-start(bf16[4,152,128]{2,1,0:T(8,128)(2,1)} %get-tuple-element.57), channel_id=1, source_target_pairs={{0,24},{1,25},{2,26},{3,27},{4,28},{5,29},{6,30},{7,31},{8,16},{9,... | collective-permute-start | bytes 466952 | tf_op jit(solution)/shard_map/ppermute | solution.py:171
  70.6 1.3 %copy.4.refs_6_ = s32[32,1]{1,0:T(8,128)} copy(s32[32,1]{0,1:T(1,128)} %param.5) | data formatting | bytes 256 | tf_op args[2]
  71.9 1.4 %collective-permute-done.25.refs_5_ = bf16[4,152,128]{2,1,0:T(8,128)(2,1)S(1)} collective-permute-done((bf16[4,152,128]{2,1,0:T(8,128)(2,1)}, bf16[4,152,128]{2,1,0:T(8,128)(2,1)S(1)}, u32[]{:S(2)}, u32[]{:S(2)}) %collective-permute-start.25) | collective-permute-done | bytes 155680 | tf_op jit(solution)/shard_map/ppermute | solution.py:171
  73.3 1.0 %shard_map.46.refs_5_ = f32[32,256]{1,0:T(8,128)S(1)} custom-call(s32[1]{0:T(128)} %bitcast.refs_0_, bf16[32,1,32,1200]{3,2,1,0:T(8,128)(2,1)S(1)} %copy-done, bf16[4,152,128]{2,1,0:T(8,128)(2,1)S(1)} %get-tuple-element.63.refs_2_, bf16[4,152,128]{2,1,0:T(8,128)(2,1)S(1)} %collective-permute-done.23.refs_3_, ...), custom_call_target="tpu_custom_call" | custom-call | flops 12288000 | bytes 1536000 | tf_op jit(solution)/shard_map/pallas_call | solution.py:48
  74.3 6.6 %collective-permute-done.17.refs_2_ = bf16[4,152,128]{2,1,0:T(8,128)(2,1)S(1)} collective-permute-done((bf16[4,152,128]{2,1,0:T(8,128)(2,1)}, bf16[4,152,128]{2,1,0:T(8,128)(2,1)S(1)}, u32[]{:S(2)}, u32[]{:S(2)}) %collective-permute-start.17) | collective-permute-done | bytes 155680 | tf_op jit(solution)/shard_map/ppermute | solution.py:171
  80.8 1.0 %collective-permute-done.19.refs_4_ = bf16[4,152,128]{2,1,0:T(8,128)(2,1)} collective-permute-done((bf16[4,152,128]{2,1,0:T(8,128)(2,1)}, bf16[4,152,128]{2,1,0:T(8,128)(2,1)}, u32[]{:S(2)}, u32[]{:S(2)}) %collective-permute-start.19) | collective-permute-done | bytes 155680 | tf_op jit(solution)/shard_map/ppermute | solution.py:171
  81.9 2.2 %shard_map.47 = bf16[32,256]{1,0:T(8,128)(2,1)} custom-call(s32[1]{0:T(128)} %bitcast.refs_0_, bf16[32,1,32,1200]{3,2,1,0:T(8,128)(2,1)S(1)} %copy-done, bf16[4,152,128]{2,1,0:T(8,128)(2,1)S(1)} %collective-permute-done.17.refs_2_, bf16[4,152,128]{2,1,0:T(8,128)(2,1)} %collective-permute-done.18.refs_3_, ...), custom_call_target="tpu_custom_call" | custom-call | flops 7372800 | bytes 921600 | tf_op jit(solution)/shard_map/pallas_call | solution.py:48
  (22 shorter events, 0.1 us)
Async XLA Ops:
  0.0 1.8 %copy-start = (bf16[32,1,32,1200]{3,2,1,0:T(8,128)(2,1)S(1)}, bf16[32,1,32,1200]{3,2,1,0:T(8,128)(2,1)}, u32[]{:S(2)}) copy-start(bf16[32,1,32,1200]{3,2,1,0:T(8,128)(2,1)} %refs_1_.9) | copy-start | bytes 7372804
  1.8 32.8 %copy-start.1 = (bf16[1,1200,1200]{2,1,0:T(8,128)(2,1)S(1)}, bf16[1,1200,1200]{2,1,0:T(8,128)(2,1)}, u32[]{:S(2)}) copy-start(bf16[1,1200,1200]{2,1,0:T(8,128)(2,1)} %refs_4_.3) | copy-start | bytes 8640004
  2.0 9.1 %collective-permute-start = (bf16[4,152,128]{2,1,0:T(8,128)(2,1)S(1)}, bf16[4,152,128]{2,1,0:T(8,128)(2,1)S(1)}, u32[]{:S(2)}, u32[]{:S(2)}) collective-permute-start(bf16[4,152,128]{2,1,0:T(8,128)(2,1)S(1)} %get-tuple-element.36.refs_2_), channel_id=1, source_target_pairs={{0,2},{1,3},{2,0},{3,1},{4,6},{5,7},{6,4},{7,5},{8,10},{9,11},{10,... | collective-permute-start | bytes 466952 | tf_op jit(solution)/shard_map/ppermute | solution.py:171
  5.0 6.5 %collective-permute-start.1 = (bf16[4,152,128]{2,1,0:T(8,128)(2,1)S(1)}, bf16[4,152,128]{2,1,0:T(8,128)(2,1)S(1)}, u32[]{:S(2)}, u32[]{:S(2)}) collective-permute-start(bf16[4,152,128]{2,1,0:T(8,128)(2,1)S(1)} %get-tuple-element.37), channel_id=1, source_target_pairs={{0,4},{1,5},{2,6},{3,7},{4,0},{5,1},{6,2},{7,3},{8,12},{9,13},{10,... | collective-permute-start | bytes 466952 | tf_op jit(solution)/shard_map/ppermute | solution.py:171
  6.5 7.5 %collective-permute-start.2 = (bf16[4,152,128]{2,1,0:T(8,128)(2,1)S(1)}, bf16[4,152,128]{2,1,0:T(8,128)(2,1)S(1)}, u32[]{:S(2)}, u32[]{:S(2)}) collective-permute-start(bf16[4,152,128]{2,1,0:T(8,128)(2,1)S(1)} %get-tuple-element.38), channel_id=1, source_target_pairs={{0,3},{1,2},{2,1},{3,0},{4,7},{5,6},{6,5},{7,4},{8,11},{9,10},{10,... | collective-permute-start | bytes 466952 | tf_op jit(solution)/shard_map/ppermute | solution.py:171
  6.5 7.5 %collective-permute-start.3 = (bf16[4,152,128]{2,1,0:T(8,128)(2,1)S(1)}, bf16[4,152,128]{2,1,0:T(8,128)(2,1)S(1)}, u32[]{:S(2)}, u32[]{:S(2)}) collective-permute-start(bf16[4,152,128]{2,1,0:T(8,128)(2,1)S(1)} %get-tuple-element.39), channel_id=1, source_target_pairs={{0,5},{1,4},{2,7},{3,6},{4,1},{5,0},{6,3},{7,2},{8,13},{9,12},{10,... | collective-permute-start | bytes 466952 | tf_op jit(solution)/shard_map/ppermute | solution.py:171
  7.0 9.0 %collective-permute-start.8 = (bf16[4,152,128]{2,1,0:T(8,128)(2,1)S(1)}, bf16[4,152,128]{2,1,0:T(8,128)(2,1)S(1)}, u32[]{:S(2)}, u32[]{:S(2)}) collective-permute-start(bf16[4,152,128]{2,1,0:T(8,128)(2,1)S(1)} %get-tuple-element.40.refs_4_), channel_id=1, source_target_pairs={{0,24},{1,25},{2,26},{3,27},{4,28},{5,29},{6,30},{7,31},{8,16},{9,... | collective-permute-start | bytes 466952 | tf_op jit(solution)/shard_map/ppermute | solution.py:171
  11.1 8.5 %collective-permute-start.9 = (bf16[4,152,128]{2,1,0:T(8,128)(2,1)S(1)}, bf16[4,152,128]{2,1,0:T(8,128)(2,1)S(1)}, u32[]{:S(2)}, u32[]{:S(2)}) collective-permute-start(bf16[4,152,128]{2,1,0:T(8,128)(2,1)S(1)} %get-tuple-element.46), channel_id=1, source_target_pairs={{0,8},{1,9},{2,10},{3,11},{4,12},{5,13},{6,14},{7,15},{8,0},{9,1},... | collective-permute-start | bytes 466952 | tf_op jit(solution)/shard_map/ppermute | solution.py:171
  11.5 12.9 %collective-permute-start.7 = (bf16[4,152,128]{2,1,0:T(8,128)(2,1)S(1)}, bf16[4,152,128]{2,1,0:T(8,128)(2,1)S(1)}, u32[]{:S(2)}, u32[]{:S(2)}) collective-permute-start(bf16[4,152,128]{2,1,0:T(8,128)(2,1)S(1)} %shard_map.37.refs_2_), channel_id=1, source_target_pairs={{0,16},{1,17},{2,18},{3,19},{4,20},{5,21},{6,22},{7,23},{8,24},{9,... | collective-permute-start | bytes 466952 | tf_op jit(solution)/shard_map/ppermute | solution.py:171
  24.4 5.3 %collective-permute-start.10 = (bf16[4,152,128]{2,1,0:T(8,128)(2,1)S(1)}, bf16[4,152,128]{2,1,0:T(8,128)(2,1)S(1)}, u32[]{:S(2)}, u32[]{:S(2)}) collective-permute-start(bf16[4,152,128]{2,1,0:T(8,128)(2,1)S(1)} %get-tuple-element.48), channel_id=1, source_target_pairs={{0,1},{1,0},{2,3},{3,2},{4,5},{5,4},{6,7},{7,6},{8,9},{9,8},{10,11... | collective-permute-start | bytes 466952 | tf_op jit(solution)/shard_map/ppermute | solution.py:171
  24.5 7.9 %collective-permute-start.11 = (bf16[4,152,128]{2,1,0:T(8,128)(2,1)S(1)}, bf16[4,152,128]{2,1,0:T(8,128)(2,1)S(1)}, u32[]{:S(2)}, u32[]{:S(2)}) collective-permute-start(bf16[4,152,128]{2,1,0:T(8,128)(2,1)S(1)} %get-tuple-element.49), channel_id=1, source_target_pairs={{0,6},{1,7},{2,4},{3,5},{4,2},{5,3},{6,0},{7,1},{8,14},{9,15},{10,... | collective-permute-start | bytes 466952 | tf_op jit(solution)/shard_map/ppermute | solution.py:171
  26.4 8.2 %collective-permute-start.12 = (bf16[4,152,128]{2,1,0:T(8,128)(2,1)S(1)}, bf16[4,152,128]{2,1,0:T(8,128)(2,1)S(1)}, u32[]{:S(2)}, u32[]{:S(2)}) collective-permute-start(bf16[4,152,128]{2,1,0:T(8,128)(2,1)S(1)} %get-tuple-element.50), channel_id=1, source_target_pairs={{0,7},{1,6},{2,5},{3,4},{4,3},{5,2},{6,1},{7,0},{8,15},{9,14},{10,... | collective-permute-start | bytes 466952 | tf_op jit(solution)/shard_map/ppermute | solution.py:171
  27.2 13.8 %collective-permute-start.4 = (bf16[4,152,128]{2,1,0:T(8,128)(2,1)S(1)}, bf16[4,152,128]{2,1,0:T(8,128)(2,1)S(1)}, u32[]{:S(2)}, u32[]{:S(2)}) collective-permute-start(bf16[4,152,128]{2,1,0:T(8,128)(2,1)S(1)} %get-tuple-element.42), channel_id=1, source_target_pairs={{0,16},{1,17},{2,18},{3,19},{4,20},{5,21},{6,22},{7,23},{8,24},{9,... | collective-permute-start | bytes 466952 | tf_op jit(solution)/shard_map/ppermute | solution.py:171
  27.5 13.5 %collective-permute-start.5 = (bf16[4,152,128]{2,1,0:T(8,128)(2,1)S(1)}, bf16[4,152,128]{2,1,0:T(8,128)(2,1)S(1)}, u32[]{:S(2)}, u32[]{:S(2)}) collective-permute-start(bf16[4,152,128]{2,1,0:T(8,128)(2,1)S(1)} %get-tuple-element.43), channel_id=1, source_target_pairs={{0,24},{1,25},{2,26},{3,27},{4,28},{5,29},{6,30},{7,31},{8,16},{9,... | collective-permute-start | bytes 466952 | tf_op jit(solution)/shard_map/ppermute | solution.py:171
  29.7 12.6 %collective-permute-start.6 = (bf16[4,152,128]{2,1,0:T(8,128)(2,1)S(1)}, bf16[4,152,128]{2,1,0:T(8,128)(2,1)S(1)}, u32[]{:S(2)}, u32[]{:S(2)}) collective-permute-start(bf16[4,152,128]{2,1,0:T(8,128)(2,1)S(1)} %get-tuple-element.44), channel_id=1, source_target_pairs={{0,8},{1,9},{2,10},{3,11},{4,12},{5,13},{6,14},{7,15},{8,0},{9,1},... | collective-permute-start | bytes 466952 | tf_op jit(solution)/shard_map/ppermute | solution.py:171
  43.5 6.3 %collective-permute-start.13 = (bf16[4,152,128]{2,1,0:T(8,128)(2,1)S(1)}, bf16[4,152,128]{2,1,0:T(8,128)(2,1)S(1)}, u32[]{:S(2)}, u32[]{:S(2)}) collective-permute-start(bf16[4,152,128]{2,1,0:T(8,128)(2,1)S(1)} %get-tuple-element.52), channel_id=1, source_target_pairs={{0,2},{1,3},{2,0},{3,1},{4,6},{5,7},{6,4},{7,5},{8,10},{9,11},{10,... | collective-permute-start | bytes 466952 | tf_op jit(solution)/shard_map/ppermute | solution.py:171
  45.1 7.2 %collective-permute-start.14 = (bf16[4,152,128]{2,1,0:T(8,128)(2,1)S(1)}, bf16[4,152,128]{2,1,0:T(8,128)(2,1)S(1)}, u32[]{:S(2)}, u32[]{:S(2)}) collective-permute-start(bf16[4,152,128]{2,1,0:T(8,128)(2,1)S(1)} %get-tuple-element.53), channel_id=1, source_target_pairs={{0,4},{1,5},{2,6},{3,7},{4,0},{5,1},{6,2},{7,3},{8,12},{9,13},{10,... | collective-permute-start | bytes 466952 | tf_op jit(solution)/shard_map/ppermute | solution.py:171
  46.0 8.5 %collective-permute-start.15 = (bf16[4,152,128]{2,1,0:T(8,128)(2,1)S(1)}, bf16[4,152,128]{2,1,0:T(8,128)(2,1)S(1)}, u32[]{:S(2)}, u32[]{:S(2)}) collective-permute-start(bf16[4,152,128]{2,1,0:T(8,128)(2,1)S(1)} %get-tuple-element.54), channel_id=1, source_target_pairs={{0,3},{1,2},{2,1},{3,0},{4,7},{5,6},{6,5},{7,4},{8,11},{9,10},{10,... | collective-permute-start | bytes 466952 | tf_op jit(solution)/shard_map/ppermute | solution.py:171
  46.0 8.5 %collective-permute-start.16 = (bf16[4,152,128]{2,1,0:T(8,128)(2,1)S(1)}, bf16[4,152,128]{2,1,0:T(8,128)(2,1)S(1)}, u32[]{:S(2)}, u32[]{:S(2)}) collective-permute-start(bf16[4,152,128]{2,1,0:T(8,128)(2,1)S(1)} %get-tuple-element.55), channel_id=1, source_target_pairs={{0,5},{1,4},{2,7},{3,6},{4,1},{5,0},{6,3},{7,2},{8,13},{9,12},{10,... | collective-permute-start | bytes 466952 | tf_op jit(solution)/shard_map/ppermute | solution.py:171
  47.4 14.5 %collective-permute-start.20 = (bf16[4,152,128]{2,1,0:T(8,128)(2,1)S(1)}, bf16[4,152,128]{2,1,0:T(8,128)(2,1)S(1)}, u32[]{:S(2)}, u32[]{:S(2)}) collective-permute-start(bf16[4,152,128]{2,1,0:T(8,128)(2,1)S(1)} %get-tuple-element.59), channel_id=1, source_target_pairs={{0,16},{1,17},{2,18},{3,19},{4,20},{5,21},{6,22},{7,23},{8,24},{9,... | collective-permute-start | bytes 466952 | tf_op jit(solution)/shard_map/ppermute | solution.py:171
  49.9 12.0 %collective-permute-start.21 = (bf16[4,152,128]{2,1,0:T(8,128)(2,1)S(1)}, bf16[4,152,128]{2,1,0:T(8,128)(2,1)S(1)}, u32[]{:S(2)}, u32[]{:S(2)}) collective-permute-start(bf16[4,152,128]{2,1,0:T(8,128)(2,1)S(1)} %get-tuple-element.60), channel_id=1, source_target_pairs={{0,24},{1,25},{2,26},{3,27},{4,28},{5,29},{6,30},{7,31},{8,16},{9,... | collective-permute-start | bytes 466952 | tf_op jit(solution)/shard_map/ppermute | solution.py:171
  52.3 9.8 %collective-permute-start.22 = (bf16[4,152,128]{2,1,0:T(8,128)(2,1)S(1)}, bf16[4,152,128]{2,1,0:T(8,128)(2,1)S(1)}, u32[]{:S(2)}, u32[]{:S(2)}) collective-permute-start(bf16[4,152,128]{2,1,0:T(8,128)(2,1)S(1)} %get-tuple-element.61), channel_id=1, source_target_pairs={{0,8},{1,9},{2,10},{3,11},{4,12},{5,13},{6,14},{7,15},{8,0},{9,1},... | collective-permute-start | bytes 466952 | tf_op jit(solution)/shard_map/ppermute | solution.py:171
  62.9 7.7 %collective-permute-start.23 = (bf16[4,152,128]{2,1,0:T(8,128)(2,1)S(1)}, bf16[4,152,128]{2,1,0:T(8,128)(2,1)S(1)}, u32[]{:S(2)}, u32[]{:S(2)}) collective-permute-start(bf16[4,152,128]{2,1,0:T(8,128)(2,1)S(1)} %get-tuple-element.64), channel_id=1, source_target_pairs={{0,1},{1,0},{2,3},{3,2},{4,5},{5,4},{6,7},{7,6},{8,9},{9,8},{10,11... | collective-permute-start | bytes 466952 | tf_op jit(solution)/shard_map/ppermute | solution.py:171
  62.9 9.0 %collective-permute-start.24 = (bf16[4,152,128]{2,1,0:T(8,128)(2,1)}, bf16[4,152,128]{2,1,0:T(8,128)(2,1)S(1)}, u32[]{:S(2)}, u32[]{:S(2)}) collective-permute-start(bf16[4,152,128]{2,1,0:T(8,128)(2,1)} %get-tuple-element.65), channel_id=1, source_target_pairs={{0,6},{1,7},{2,4},{3,5},{4,2},{5,3},{6,0},{7,1},{8,14},{9,15},{10,... | collective-permute-start | bytes 466952 | tf_op jit(solution)/shard_map/ppermute | solution.py:171
  64.3 8.9 %collective-permute-start.25 = (bf16[4,152,128]{2,1,0:T(8,128)(2,1)}, bf16[4,152,128]{2,1,0:T(8,128)(2,1)S(1)}, u32[]{:S(2)}, u32[]{:S(2)}) collective-permute-start(bf16[4,152,128]{2,1,0:T(8,128)(2,1)} %get-tuple-element.66), channel_id=1, source_target_pairs={{0,7},{1,6},{2,5},{3,4},{4,3},{5,2},{6,1},{7,0},{8,15},{9,14},{10,... | collective-permute-start | bytes 466952 | tf_op jit(solution)/shard_map/ppermute | solution.py:171
  65.6 15.2 %collective-permute-start.17 = (bf16[4,152,128]{2,1,0:T(8,128)(2,1)}, bf16[4,152,128]{2,1,0:T(8,128)(2,1)S(1)}, u32[]{:S(2)}, u32[]{:S(2)}) collective-permute-start(bf16[4,152,128]{2,1,0:T(8,128)(2,1)} %get-tuple-element.56), channel_id=1, source_target_pairs={{0,16},{1,17},{2,18},{3,19},{4,20},{5,21},{6,22},{7,23},{8,24},{9,... | collective-permute-start | bytes 466952 | tf_op jit(solution)/shard_map/ppermute | solution.py:171
  69.0 11.8 %collective-permute-start.18 = (bf16[4,152,128]{2,1,0:T(8,128)(2,1)}, bf16[4,152,128]{2,1,0:T(8,128)(2,1)}, u32[]{:S(2)}, u32[]{:S(2)}) collective-permute-start(bf16[4,152,128]{2,1,0:T(8,128)(2,1)} %get-tuple-element.57), channel_id=1, source_target_pairs={{0,24},{1,25},{2,26},{3,27},{4,28},{5,29},{6,30},{7,31},{8,16},{9,... | collective-permute-start | bytes 466952 | tf_op jit(solution)/shard_map/ppermute | solution.py:171
  70.6 11.3 %collective-permute-start.19 = (bf16[4,152,128]{2,1,0:T(8,128)(2,1)}, bf16[4,152,128]{2,1,0:T(8,128)(2,1)}, u32[]{:S(2)}, u32[]{:S(2)}) collective-permute-start(bf16[4,152,128]{2,1,0:T(8,128)(2,1)} %get-tuple-element.58), channel_id=1, source_target_pairs={{0,8},{1,9},{2,10},{3,11},{4,12},{5,13},{6,14},{7,15},{8,0},{9,1},... | collective-permute-start | bytes 466952 | tf_op jit(solution)/shard_map/ppermute | solution.py:171
  71.9 10.0 %copy-start.2 = (s32[32,1]{1,0:T(8,128)S(1)}, s32[32,1]{1,0:T(8,128)}, u32[]{:S(2)}) copy-start(s32[32,1]{1,0:T(8,128)} %copy.4.refs_6_) | copy-start | bytes 388

commit v6 on v5

--- a/solution.py
+++ b/solution.py
@@ -288,7 +288,8 @@
                 r = r + rows_of_pairs(s, me, offs, c[lo:hi, :], sc[lo:hi, :])
             if last:
                 before, live_ref = more
-                out[...] = ((r + before[...]) * live_ref[...].astype(F32)).astype(BF16)
+                alive = pick((N, N), lambda q, k: q == k).astype(F32) * live_ref[...].astype(F32)
+                out[...] = ((r + before[...]) * jnp.sum(alive, axis=1, keepdims=True)).astype(BF16)
             else:
                 out[...] = r
 
@@ -307,7 +308,7 @@
     picks += [(len(s_out), j, p) for j, p in enumerate(s_in)]
     partial = finish([*fin, s2z[0]], picks, ())
     picks = [(zi, j, dz * I + p) for zi, dz in enumerate(far) for j, p in enumerate(s_in)]
-    return finish(s2z[1:], picks, (partial, live))[:, None, :]
+    return finish(s2z[1:], picks, (partial, live.T))[:, None, :]
 
 
 def plain(densities, screening, live):

time: 84.3 us -> 81.1 us (0.962)
  Pallas kernels: 9.05 us -> 6.59 us
  starting transfers between devices: 36.5 us -> 38.2 us
  local copies, waits for them, and re-layouts: 1.86 us -> 0.52 us
  waiting for transfers between devices: 36.6 us -> 35.6 us
    pallas_call x11, Pallas kernels: 9.05 us -> 6.59 us  [call(): return pallas(body, outs, specs, a, scratch, flops, moved)(*ins, *after)]
    ppermute x26, starting transfers between devices: 36.5 us -> 38.2 us  [hop(): return lax.ppermute(x, 'pb', [(d, d ^ m) for d in range(N)])]
    unnamed x7 -> x6, local copies, waits for them, and re-layouts: 1.86 us -> 0.52 us
    ppermute x26, waiting for transfers between devices: 36.6 us -> 35.6 us  [hop(): return lax.ppermute(x, 'pb', [(d, d ^ m) for d in range(N)])]
  transfers between devices with their start and end apart: 26 -> 26, of which waited for: 13 -> 13; matrix products, arithmetic and copies ran while one was open for 2% -> 0% of each run, Pallas kernels for 4% -> 3%
where the time goes in v6:
time: 81.1 us; the launch traced here: 81 us
  starting transfers between devices  38.2 us (47%)
  waiting for transfers between devices  35.6 us (44%)
  Pallas kernels  6.59 us (8%)
    ppermute x26, starting transfers between devices, hop(): return lax.ppermute(x, 'pb', [(d, d ^ m) for d in range(N)])  38.2 us
    ppermute x26, waiting for transfers between devices, hop(): return lax.ppermute(x, 'pb', [(d, d ^ m) for d in range(N)])  35.6 us
    pallas_call x11, Pallas kernels, call(): return pallas(body, outs, specs, a, scratch, flops, moved)(*ins, *after)  6.59 us
  transfers between devices with their start and end apart: 26, of which 13 were waited for; matrix products, arithmetic and copies ran while one was open for 0% of the time, Pallas kernels for 3%

profile of v6, /device:TPU:0, one launch (start us, length us, event | category | flops | bytes accessed | tf_op | source)
XLA Modules:
  0.0 81.0 jit_solution(6182995233502163501)
XLA Ops:
  0.0 1.3 %shard_map.37.refs_2_ = bf16[4,152,128]{2,1,0:T(8,128)(2,1)S(1)} custom-call(s32[1]{0:T(128)} %bitcast.refs_0_, bf16[32,1,32,1200]{3,2,1,0:T(8,128)(2,1)} %refs_1_.9), custom_call_target="tpu_custom_call" | custom-call | bytes 307200 | tf_op jit(solution)/shard_map/pallas_call | solution.py:48
  1.3 0.5 copy-done
  1.8 0.2 shard_map.38
  2.0 3.0 %collective-permute-start.1 = (bf16[4,152,128]{2,1,0:T(8,128)(2,1)S(1)}, bf16[4,152,128]{2,1,0:T(8,128)(2,1)S(1)}, u32[]{:S(2)}, u32[]{:S(2)}) collective-permute-start(bf16[4,152,128]{2,1,0:T(8,128)(2,1)S(1)} %get-tuple-element.37), channel_id=1, source_target_pairs={{0,4},{1,5},{2,6},{3,7},{4,0},{5,1},{6,2},{7,3},{8,12},{9,13},{10,... | collective-permute-start | bytes 466952 | tf_op jit(solution)/shard_map/ppermute | solution.py:171
  5.0 0.7 collective-permute-start.2
  5.7 2.6 %collective-permute-start.7 = (bf16[4,152,128]{2,1,0:T(8,128)(2,1)S(1)}, bf16[4,152,128]{2,1,0:T(8,128)(2,1)S(1)}, u32[]{:S(2)}, u32[]{:S(2)}) collective-permute-start(bf16[4,152,128]{2,1,0:T(8,128)(2,1)S(1)} %shard_map.37.refs_2_), channel_id=1, source_target_pairs={{0,16},{1,17},{2,18},{3,19},{4,20},{5,21},{6,22},{7,23},{8,24},{9,... | collective-permute-start | bytes 466952 | tf_op jit(solution)/shard_map/ppermute | solution.py:171
  8.3 0.8 collective-permute-start.3
  9.1 0.5 collective-permute-start
  9.6 0.2 shard_map.39
  9.8 0.0 collective-permute-done.1.refs_1_
  9.8 1.6 %collective-permute-start.9 = (bf16[4,152,128]{2,1,0:T(8,128)(2,1)S(1)}, bf16[4,152,128]{2,1,0:T(8,128)(2,1)S(1)}, u32[]{:S(2)}, u32[]{:S(2)}) collective-permute-start(bf16[4,152,128]{2,1,0:T(8,128)(2,1)S(1)} %get-tuple-element.46), channel_id=1, source_target_pairs={{0,8},{1,9},{2,10},{3,11},{4,12},{5,13},{6,14},{7,15},{8,0},{9,1},... | collective-permute-start | bytes 466952 | tf_op jit(solution)/shard_map/ppermute | solution.py:171
  11.4 3.5 %collective-permute-start.8 = (bf16[4,152,128]{2,1,0:T(8,128)(2,1)S(1)}, bf16[4,152,128]{2,1,0:T(8,128)(2,1)S(1)}, u32[]{:S(2)}, u32[]{:S(2)}) collective-permute-start(bf16[4,152,128]{2,1,0:T(8,128)(2,1)S(1)} %get-tuple-element.40.refs_4_), channel_id=1, source_target_pairs={{0,24},{1,25},{2,26},{3,27},{4,28},{5,29},{6,30},{7,31},{8,16},{9,... | collective-permute-start | bytes 466952 | tf_op jit(solution)/shard_map/ppermute | solution.py:171
  14.9 0.0 collective-permute-done.3.refs_3_
  15.0 1.9 %collective-permute-done.7.refs_1_ = bf16[4,152,128]{2,1,0:T(8,128)(2,1)S(1)} collective-permute-done((bf16[4,152,128]{2,1,0:T(8,128)(2,1)S(1)}, bf16[4,152,128]{2,1,0:T(8,128)(2,1)S(1)}, u32[]{:S(2)}, u32[]{:S(2)}) %collective-permute-start.7) | collective-permute-done | bytes 155680 | tf_op jit(solution)/shard_map/ppermute | solution.py:171
  16.9 1.5 %collective-permute-done.9.refs_3_ = bf16[4,152,128]{2,1,0:T(8,128)(2,1)S(1)} collective-permute-done((bf16[4,152,128]{2,1,0:T(8,128)(2,1)S(1)}, bf16[4,152,128]{2,1,0:T(8,128)(2,1)S(1)}, u32[]{:S(2)}, u32[]{:S(2)}) %collective-permute-start.9) | collective-permute-done | bytes 155680 | tf_op jit(solution)/shard_map/ppermute | solution.py:171
  18.4 2.9 %collective-permute-done.8.refs_2_ = bf16[4,152,128]{2,1,0:T(8,128)(2,1)S(1)} collective-permute-done((bf16[4,152,128]{2,1,0:T(8,128)(2,1)S(1)}, bf16[4,152,128]{2,1,0:T(8,128)(2,1)S(1)}, u32[]{:S(2)}, u32[]{:S(2)}) %collective-permute-start.8) | collective-permute-done | bytes 155680 | tf_op jit(solution)/shard_map/ppermute | solution.py:171
  21.4 0.1 collective-permute-start.10
  21.4 2.0 %collective-permute-start.11 = (bf16[4,152,128]{2,1,0:T(8,128)(2,1)S(1)}, bf16[4,152,128]{2,1,0:T(8,128)(2,1)S(1)}, u32[]{:S(2)}, u32[]{:S(2)}) collective-permute-start(bf16[4,152,128]{2,1,0:T(8,128)(2,1)S(1)} %get-tuple-element.49), channel_id=1, source_target_pairs={{0,6},{1,7},{2,4},{3,5},{4,2},{5,3},{6,0},{7,1},{8,14},{9,15},{10,... | collective-permute-start | bytes 466952 | tf_op jit(solution)/shard_map/ppermute | solution.py:171
  23.4 0.7 collective-permute-start.12
  24.2 4.8 %collective-permute-start.4 = (bf16[4,152,128]{2,1,0:T(8,128)(2,1)S(1)}, bf16[4,152,128]{2,1,0:T(8,128)(2,1)S(1)}, u32[]{:S(2)}, u32[]{:S(2)}) collective-permute-start(bf16[4,152,128]{2,1,0:T(8,128)(2,1)S(1)} %get-tuple-element.42), channel_id=1, source_target_pairs={{0,16},{1,17},{2,18},{3,19},{4,20},{5,21},{6,22},{7,23},{8,24},{9,... | collective-permute-start | bytes 466952 | tf_op jit(solution)/shard_map/ppermute | solution.py:171
  29.0 0.4 collective-permute-start.5
  29.4 0.1 collective-permute-start.6
  29.6 2.0 %collective-permute-done.12.refs_3_ = bf16[4,152,128]{2,1,0:T(8,128)(2,1)S(1)} collective-permute-done((bf16[4,152,128]{2,1,0:T(8,128)(2,1)S(1)}, bf16[4,152,128]{2,1,0:T(8,128)(2,1)S(1)}, u32[]{:S(2)}, u32[]{:S(2)}) %collective-permute-start.12) | collective-permute-done | bytes 155680 | tf_op jit(solution)/shard_map/ppermute | solution.py:171
  31.6 1.3 %shard_map.42 = (bf16[4,152,128]{2,1,0:T(8,128)(2,1)S(1)}, bf16[4,152,128]{2,1,0:T(8,128)(2,1)S(1)}, bf16[4,152,128]{2,1,0:T(8,128)(2,1)S(1)}, bf16[4,152,128]{2,1,0:T(8,128)(2,1)S(1)}) custom-call(bf16[4,152,128]{2,1,0:T(8,128)(2,1)S(1)} %get-tuple-element.47.refs_0_.refs_5_, bf16[4,152,128]{2,1,0:T(8,128)(2,1)S(1)} %collective-permute-done.10.refs_1_, ...), custom_call_target="tpu_custom_call" | custom-call | flops 737280000 | bytes 2880000 | tf_op jit(solution)/shard_map/pallas_call | solution.py:48
  32.8 7.7 %collective-permute-done.4.refs_1_ = bf16[4,152,128]{2,1,0:T(8,128)(2,1)S(1)} collective-permute-done((bf16[4,152,128]{2,1,0:T(8,128)(2,1)S(1)}, bf16[4,152,128]{2,1,0:T(8,128)(2,1)S(1)}, u32[]{:S(2)}, u32[]{:S(2)}) %collective-permute-start.4) | collective-permute-done | bytes 155680 | tf_op jit(solution)/shard_map/ppermute | solution.py:171
  40.6 1.1 %collective-permute-done.6.refs_3_ = bf16[4,152,128]{2,1,0:T(8,128)(2,1)S(1)} collective-permute-done((bf16[4,152,128]{2,1,0:T(8,128)(2,1)S(1)}, bf16[4,152,128]{2,1,0:T(8,128)(2,1)S(1)}, u32[]{:S(2)}, u32[]{:S(2)}) %collective-permute-start.6) | collective-permute-done | bytes 155680 | tf_op jit(solution)/shard_map/ppermute | solution.py:171
  41.6 1.3 %shard_map.43 = (bf16[4,152,128]{2,1,0:T(8,128)(2,1)S(1)}, bf16[4,152,128]{2,1,0:T(8,128)(2,1)S(1)}, bf16[4,152,128]{2,1,0:T(8,128)(2,1)S(1)}, bf16[4,152,128]{2,1,0:T(8,128)(2,1)S(1)}) custom-call(bf16[4,152,128]{2,1,0:T(8,128)(2,1)S(1)} %get-tuple-element.41.refs_4_.refs_0_, bf16[4,152,128]{2,1,0:T(8,128)(2,1)S(1)} %collective-permute-done.4.refs_1_, ...), custom_call_target="tpu_custom_call" | custom-call | flops 737280000 | bytes 2880000 | tf_op jit(solution)/shard_map/pallas_call | solution.py:48
  42.9 0.0 copy-start.2
  42.9 0.6 collective-permute-start.13
  43.5 0.5 collective-permute-start.14
  44.0 2.8 %collective-permute-start.16 = (bf16[4,152,128]{2,1,0:T(8,128)(2,1)S(1)}, bf16[4,152,128]{2,1,0:T(8,128)(2,1)S(1)}, u32[]{:S(2)}, u32[]{:S(2)}) collective-permute-start(bf16[4,152,128]{2,1,0:T(8,128)(2,1)S(1)} %get-tuple-element.55), channel_id=1, source_target_pairs={{0,5},{1,4},{2,7},{3,6},{4,1},{5,0},{6,3},{7,2},{8,13},{9,12},{10,... | collective-permute-start | bytes 466952 | tf_op jit(solution)/shard_map/ppermute | solution.py:171
  46.7 2.6 %collective-permute-start.20 = (bf16[4,152,128]{2,1,0:T(8,128)(2,1)S(1)}, bf16[4,152,128]{2,1,0:T(8,128)(2,1)S(1)}, u32[]{:S(2)}, u32[]{:S(2)}) collective-permute-start(bf16[4,152,128]{2,1,0:T(8,128)(2,1)S(1)} %get-tuple-element.59), channel_id=1, source_target_pairs={{0,16},{1,17},{2,18},{3,19},{4,20},{5,21},{6,22},{7,23},{8,24},{9,... | collective-permute-start | bytes 466952 | tf_op jit(solution)/shard_map/ppermute | solution.py:171
  49.3 0.1 collective-permute-done.13.refs_0_
  49.4 2.3 %collective-permute-start.21 = (bf16[4,152,128]{2,1,0:T(8,128)(2,1)S(1)}, bf16[4,152,128]{2,1,0:T(8,128)(2,1)S(1)}, u32[]{:S(2)}, u32[]{:S(2)}) collective-permute-start(bf16[4,152,128]{2,1,0:T(8,128)(2,1)S(1)} %get-tuple-element.60), channel_id=1, source_target_pairs={{0,24},{1,25},{2,26},{3,27},{4,28},{5,29},{6,30},{7,31},{8,16},{9,... | collective-permute-start | bytes 466952 | tf_op jit(solution)/shard_map/ppermute | solution.py:171
  51.7 0.9 %collective-permute-start.22 = (bf16[4,152,128]{2,1,0:T(8,128)(2,1)S(1)}, bf16[4,152,128]{2,1,0:T(8,128)(2,1)S(1)}, u32[]{:S(2)}, u32[]{:S(2)}) collective-permute-start(bf16[4,152,128]{2,1,0:T(8,128)(2,1)S(1)} %get-tuple-element.61), channel_id=1, source_target_pairs={{0,8},{1,9},{2,10},{3,11},{4,12},{5,13},{6,14},{7,15},{8,0},{9,1},... | collective-permute-start | bytes 466952 | tf_op jit(solution)/shard_map/ppermute | solution.py:171
  52.6 8.2 %collective-permute-done.20.refs_1_ = bf16[4,152,128]{2,1,0:T(8,128)(2,1)S(1)} collective-permute-done((bf16[4,152,128]{2,1,0:T(8,128)(2,1)S(1)}, bf16[4,152,128]{2,1,0:T(8,128)(2,1)S(1)}, u32[]{:S(2)}, u32[]{:S(2)}) %collective-permute-start.20) | collective-permute-done | bytes 155680 | tf_op jit(solution)/shard_map/ppermute | solution.py:171
  60.8 0.1 collective-permute-done.22.refs_3_
  60.9 0.1 collective-permute-start.23
  61.0 1.8 %collective-permute-start.24 = (bf16[4,152,128]{2,1,0:T(8,128)(2,1)S(1)}, bf16[4,152,128]{2,1,0:T(8,128)(2,1)S(1)}, u32[]{:S(2)}, u32[]{:S(2)}) collective-permute-start(bf16[4,152,128]{2,1,0:T(8,128)(2,1)S(1)} %get-tuple-element.65), channel_id=1, source_target_pairs={{0,6},{1,7},{2,4},{3,5},{4,2},{5,3},{6,0},{7,1},{8,14},{9,15},{10,... | collective-permute-start | bytes 466952 | tf_op jit(solution)/shard_map/ppermute | solution.py:171
  62.8 0.9 %collective-permute-start.25 = (bf16[4,152,128]{2,1,0:T(8,128)(2,1)S(1)}, bf16[4,152,128]{2,1,0:T(8,128)(2,1)S(1)}, u32[]{:S(2)}, u32[]{:S(2)}) collective-permute-start(bf16[4,152,128]{2,1,0:T(8,128)(2,1)S(1)} %get-tuple-element.66), channel_id=1, source_target_pairs={{0,7},{1,6},{2,5},{3,4},{4,3},{5,2},{6,1},{7,0},{8,15},{9,14},{10,... | collective-permute-start | bytes 466952 | tf_op jit(solution)/shard_map/ppermute | solution.py:171
  63.8 3.4 %collective-permute-start.17 = (bf16[4,152,128]{2,1,0:T(8,128)(2,1)S(1)}, bf16[4,152,128]{2,1,0:T(8,128)(2,1)S(1)}, u32[]{:S(2)}, u32[]{:S(2)}) collective-permute-start(bf16[4,152,128]{2,1,0:T(8,128)(2,1)S(1)} %get-tuple-element.56), channel_id=1, source_target_pairs={{0,16},{1,17},{2,18},{3,19},{4,20},{5,21},{6,22},{7,23},{8,24},{9,... | collective-permute-start | bytes 466952 | tf_op jit(solution)/shard_map/ppermute | solution.py:171
  67.2 1.5 %collective-permute-start.18 = (bf16[4,152,128]{2,1,0:T(8,128)(2,1)S(1)}, bf16[4,152,128]{2,1,0:T(8,128)(2,1)S(1)}, u32[]{:S(2)}, u32[]{:S(2)}) collective-permute-start(bf16[4,152,128]{2,1,0:T(8,128)(2,1)S(1)} %get-tuple-element.57), channel_id=1, source_target_pairs={{0,24},{1,25},{2,26},{3,27},{4,28},{5,29},{6,30},{7,31},{8,16},{9,... | collective-permute-start | bytes 466952 | tf_op jit(solution)/shard_map/ppermute | solution.py:171
  68.7 0.2 collective-permute-done.24.refs_4_
  68.9 2.3 %collective-permute-done.25.refs_5_ = bf16[4,152,128]{2,1,0:T(8,128)(2,1)S(1)} collective-permute-done((bf16[4,152,128]{2,1,0:T(8,128)(2,1)S(1)}, bf16[4,152,128]{2,1,0:T(8,128)(2,1)S(1)}, u32[]{:S(2)}, u32[]{:S(2)}) %collective-permute-start.25) | collective-permute-done | bytes 155680 | tf_op jit(solution)/shard_map/ppermute | solution.py:171
  71.1 1.0 %shard_map.46.refs_5_ = f32[32,256]{1,0:T(8,128)S(1)} custom-call(s32[1]{0:T(128)} %bitcast.refs_0_, bf16[32,1,32,1200]{3,2,1,0:T(8,128)(2,1)S(1)} %copy-done, bf16[4,152,128]{2,1,0:T(8,128)(2,1)S(1)} %get-tuple-element.63.refs_2_, bf16[4,152,128]{2,1,0:T(8,128)(2,1)S(1)} %collective-permute-done.23.refs_3_, ...), custom_call_target="tpu_custom_call" | custom-call | flops 12288000 | bytes 1536000 | tf_op jit(solution)/shard_map/pallas_call | solution.py:48
  72.1 6.6 %collective-permute-done.17.refs_2_ = bf16[4,152,128]{2,1,0:T(8,128)(2,1)S(1)} collective-permute-done((bf16[4,152,128]{2,1,0:T(8,128)(2,1)S(1)}, bf16[4,152,128]{2,1,0:T(8,128)(2,1)S(1)}, u32[]{:S(2)}, u32[]{:S(2)}) %collective-permute-start.17) | collective-permute-done | bytes 155680 | tf_op jit(solution)/shard_map/ppermute | solution.py:171
  78.8 1.0 %collective-permute-done.19.refs_4_ = bf16[4,152,128]{2,1,0:T(8,128)(2,1)S(1)} collective-permute-done((bf16[4,152,128]{2,1,0:T(8,128)(2,1)S(1)}, bf16[4,152,128]{2,1,0:T(8,128)(2,1)S(1)}, u32[]{:S(2)}, u32[]{:S(2)}) %collective-permute-start.19) | collective-permute-done | bytes 155680 | tf_op jit(solution)/shard_map/ppermute | solution.py:171
  79.8 1.2 %shard_map.47 = bf16[32,256]{1,0:T(8,128)(2,1)} custom-call(s32[1]{0:T(128)} %bitcast.refs_0_, bf16[32,1,32,1200]{3,2,1,0:T(8,128)(2,1)S(1)} %copy-done, bf16[4,152,128]{2,1,0:T(8,128)(2,1)S(1)} %collective-permute-done.17.refs_2_, bf16[4,152,128]{2,1,0:T(8,128)(2,1)S(1)} %collective-permute-done.18.refs_3_, ...), custom_call_target="tpu_custom_call" | custom-call | flops 7372800 | bytes 921600 | tf_op jit(solution)/shard_map/pallas_call | solution.py:48
  (21 shorter events, 0.2 us)
Async XLA Ops:
  0.0 1.8 %copy-start = (bf16[32,1,32,1200]{3,2,1,0:T(8,128)(2,1)S(1)}, bf16[32,1,32,1200]{3,2,1,0:T(8,128)(2,1)}, u32[]{:S(2)}) copy-start(bf16[32,1,32,1200]{3,2,1,0:T(8,128)(2,1)} %refs_1_.9) | copy-start | bytes 7372804
  1.8 29.7 %copy-start.1 = (bf16[1,1200,1200]{2,1,0:T(8,128)(2,1)S(1)}, bf16[1,1200,1200]{2,1,0:T(8,128)(2,1)}, u32[]{:S(2)}) copy-start(bf16[1,1200,1200]{2,1,0:T(8,128)(2,1)} %refs_4_.3) | copy-start | bytes 8640004
  2.0 7.8 %collective-permute-start.1 = (bf16[4,152,128]{2,1,0:T(8,128)(2,1)S(1)}, bf16[4,152,128]{2,1,0:T(8,128)(2,1)S(1)}, u32[]{:S(2)}, u32[]{:S(2)}) collective-permute-start(bf16[4,152,128]{2,1,0:T(8,128)(2,1)S(1)} %get-tuple-element.37), channel_id=1, source_target_pairs={{0,4},{1,5},{2,6},{3,7},{4,0},{5,1},{6,2},{7,3},{8,12},{9,13},{10,... | collective-permute-start | bytes 466952 | tf_op jit(solution)/shard_map/ppermute | solution.py:171
  5.0 6.4 %collective-permute-start.2 = (bf16[4,152,128]{2,1,0:T(8,128)(2,1)S(1)}, bf16[4,152,128]{2,1,0:T(8,128)(2,1)S(1)}, u32[]{:S(2)}, u32[]{:S(2)}) collective-permute-start(bf16[4,152,128]{2,1,0:T(8,128)(2,1)S(1)} %get-tuple-element.38), channel_id=1, source_target_pairs={{0,3},{1,2},{2,1},{3,0},{4,7},{5,6},{6,5},{7,4},{8,11},{9,10},{10,... | collective-permute-start | bytes 466952 | tf_op jit(solution)/shard_map/ppermute | solution.py:171
  5.7 11.2 %collective-permute-start.7 = (bf16[4,152,128]{2,1,0:T(8,128)(2,1)S(1)}, bf16[4,152,128]{2,1,0:T(8,128)(2,1)S(1)}, u32[]{:S(2)}, u32[]{:S(2)}) collective-permute-start(bf16[4,152,128]{2,1,0:T(8,128)(2,1)S(1)} %shard_map.37.refs_2_), channel_id=1, source_target_pairs={{0,16},{1,17},{2,18},{3,19},{4,20},{5,21},{6,22},{7,23},{8,24},{9,... | collective-permute-start | bytes 466952 | tf_op jit(solution)/shard_map/ppermute | solution.py:171
  8.3 6.6 %collective-permute-start.3 = (bf16[4,152,128]{2,1,0:T(8,128)(2,1)S(1)}, bf16[4,152,128]{2,1,0:T(8,128)(2,1)S(1)}, u32[]{:S(2)}, u32[]{:S(2)}) collective-permute-start(bf16[4,152,128]{2,1,0:T(8,128)(2,1)S(1)} %get-tuple-element.39), channel_id=1, source_target_pairs={{0,5},{1,4},{2,7},{3,6},{4,1},{5,0},{6,3},{7,2},{8,13},{9,12},{10,... | collective-permute-start | bytes 466952 | tf_op jit(solution)/shard_map/ppermute | solution.py:171
  9.1 5.9 %collective-permute-start = (bf16[4,152,128]{2,1,0:T(8,128)(2,1)S(1)}, bf16[4,152,128]{2,1,0:T(8,128)(2,1)S(1)}, u32[]{:S(2)}, u32[]{:S(2)}) collective-permute-start(bf16[4,152,128]{2,1,0:T(8,128)(2,1)S(1)} %get-tuple-element.36.refs_2_), channel_id=1, source_target_pairs={{0,2},{1,3},{2,0},{3,1},{4,6},{5,7},{6,4},{7,5},{8,10},{9,11},{10,... | collective-permute-start | bytes 466952 | tf_op jit(solution)/shard_map/ppermute | solution.py:171
  9.8 8.6 %collective-permute-start.9 = (bf16[4,152,128]{2,1,0:T(8,128)(2,1)S(1)}, bf16[4,152,128]{2,1,0:T(8,128)(2,1)S(1)}, u32[]{:S(2)}, u32[]{:S(2)}) collective-permute-start(bf16[4,152,128]{2,1,0:T(8,128)(2,1)S(1)} %get-tuple-element.46), channel_id=1, source_target_pairs={{0,8},{1,9},{2,10},{3,11},{4,12},{5,13},{6,14},{7,15},{8,0},{9,1},... | collective-permute-start | bytes 466952 | tf_op jit(solution)/shard_map/ppermute | solution.py:171
  11.4 9.9 %collective-permute-start.8 = (bf16[4,152,128]{2,1,0:T(8,128)(2,1)S(1)}, bf16[4,152,128]{2,1,0:T(8,128)(2,1)S(1)}, u32[]{:S(2)}, u32[]{:S(2)}) collective-permute-start(bf16[4,152,128]{2,1,0:T(8,128)(2,1)S(1)} %get-tuple-element.40.refs_4_), channel_id=1, source_target_pairs={{0,24},{1,25},{2,26},{3,27},{4,28},{5,29},{6,30},{7,31},{8,16},{9,... | collective-permute-start | bytes 466952 | tf_op jit(solution)/shard_map/ppermute | solution.py:171
  21.4 8.1 %collective-permute-start.10 = (bf16[4,152,128]{2,1,0:T(8,128)(2,1)S(1)}, bf16[4,152,128]{2,1,0:T(8,128)(2,1)S(1)}, u32[]{:S(2)}, u32[]{:S(2)}) collective-permute-start(bf16[4,152,128]{2,1,0:T(8,128)(2,1)S(1)} %get-tuple-element.48), channel_id=1, source_target_pairs={{0,1},{1,0},{2,3},{3,2},{4,5},{5,4},{6,7},{7,6},{8,9},{9,8},{10,11... | collective-permute-start | bytes 466952 | tf_op jit(solution)/shard_map/ppermute | solution.py:171
  21.4 8.1 %collective-permute-start.11 = (bf16[4,152,128]{2,1,0:T(8,128)(2,1)S(1)}, bf16[4,152,128]{2,1,0:T(8,128)(2,1)S(1)}, u32[]{:S(2)}, u32[]{:S(2)}) collective-permute-start(bf16[4,152,128]{2,1,0:T(8,128)(2,1)S(1)} %get-tuple-element.49), channel_id=1, source_target_pairs={{0,6},{1,7},{2,4},{3,5},{4,2},{5,3},{6,0},{7,1},{8,14},{9,15},{10,... | collective-permute-start | bytes 466952 | tf_op jit(solution)/shard_map/ppermute | solution.py:171
  23.4 8.1 %collective-permute-start.12 = (bf16[4,152,128]{2,1,0:T(8,128)(2,1)S(1)}, bf16[4,152,128]{2,1,0:T(8,128)(2,1)S(1)}, u32[]{:S(2)}, u32[]{:S(2)}) collective-permute-start(bf16[4,152,128]{2,1,0:T(8,128)(2,1)S(1)} %get-tuple-element.50), channel_id=1, source_target_pairs={{0,7},{1,6},{2,5},{3,4},{4,3},{5,2},{6,1},{7,0},{8,15},{9,14},{10,... | collective-permute-start | bytes 466952 | tf_op jit(solution)/shard_map/ppermute | solution.py:171
  24.2 16.4 %collective-permute-start.4 = (bf16[4,152,128]{2,1,0:T(8,128)(2,1)S(1)}, bf16[4,152,128]{2,1,0:T(8,128)(2,1)S(1)}, u32[]{:S(2)}, u32[]{:S(2)}) collective-permute-start(bf16[4,152,128]{2,1,0:T(8,128)(2,1)S(1)} %get-tuple-element.42), channel_id=1, source_target_pairs={{0,16},{1,17},{2,18},{3,19},{4,20},{5,21},{6,22},{7,23},{8,24},{9,... | collective-permute-start | bytes 466952 | tf_op jit(solution)/shard_map/ppermute | solution.py:171
  29.0 11.6 %collective-permute-start.5 = (bf16[4,152,128]{2,1,0:T(8,128)(2,1)S(1)}, bf16[4,152,128]{2,1,0:T(8,128)(2,1)S(1)}, u32[]{:S(2)}, u32[]{:S(2)}) collective-permute-start(bf16[4,152,128]{2,1,0:T(8,128)(2,1)S(1)} %get-tuple-element.43), channel_id=1, source_target_pairs={{0,24},{1,25},{2,26},{3,27},{4,28},{5,29},{6,30},{7,31},{8,16},{9,... | collective-permute-start | bytes 466952 | tf_op jit(solution)/shard_map/ppermute | solution.py:171
  29.4 12.2 %collective-permute-start.6 = (bf16[4,152,128]{2,1,0:T(8,128)(2,1)S(1)}, bf16[4,152,128]{2,1,0:T(8,128)(2,1)S(1)}, u32[]{:S(2)}, u32[]{:S(2)}) collective-permute-start(bf16[4,152,128]{2,1,0:T(8,128)(2,1)S(1)} %get-tuple-element.44), channel_id=1, source_target_pairs={{0,8},{1,9},{2,10},{3,11},{4,12},{5,13},{6,14},{7,15},{8,0},{9,1},... | collective-permute-start | bytes 466952 | tf_op jit(solution)/shard_map/ppermute | solution.py:171
  42.9 36.9 %copy-start.2 = (s32[32,1]{0,1:T(1,128)S(1)}, s32[32,1]{0,1:T(1,128)}, u32[]{:S(2)}) copy-start(s32[32,1]{0,1:T(1,128)} %param.5) | copy-start | bytes 388
  42.9 6.5 %collective-permute-start.13 = (bf16[4,152,128]{2,1,0:T(8,128)(2,1)S(1)}, bf16[4,152,128]{2,1,0:T(8,128)(2,1)S(1)}, u32[]{:S(2)}, u32[]{:S(2)}) collective-permute-start(bf16[4,152,128]{2,1,0:T(8,128)(2,1)S(1)} %get-tuple-element.52), channel_id=1, source_target_pairs={{0,2},{1,3},{2,0},{3,1},{4,6},{5,7},{6,4},{7,5},{8,10},{9,11},{10,... | collective-permute-start | bytes 466952 | tf_op jit(solution)/shard_map/ppermute | solution.py:171
  43.5 8.2 %collective-permute-start.14 = (bf16[4,152,128]{2,1,0:T(8,128)(2,1)S(1)}, bf16[4,152,128]{2,1,0:T(8,128)(2,1)S(1)}, u32[]{:S(2)}, u32[]{:S(2)}) collective-permute-start(bf16[4,152,128]{2,1,0:T(8,128)(2,1)S(1)} %get-tuple-element.53), channel_id=1, source_target_pairs={{0,4},{1,5},{2,6},{3,7},{4,0},{5,1},{6,2},{7,3},{8,12},{9,13},{10,... | collective-permute-start | bytes 466952 | tf_op jit(solution)/shard_map/ppermute | solution.py:171
  44.0 8.6 %collective-permute-start.15 = (bf16[4,152,128]{2,1,0:T(8,128)(2,1)S(1)}, bf16[4,152,128]{2,1,0:T(8,128)(2,1)S(1)}, u32[]{:S(2)}, u32[]{:S(2)}) collective-permute-start(bf16[4,152,128]{2,1,0:T(8,128)(2,1)S(1)} %get-tuple-element.54), channel_id=1, source_target_pairs={{0,3},{1,2},{2,1},{3,0},{4,7},{5,6},{6,5},{7,4},{8,11},{9,10},{10,... | collective-permute-start | bytes 466952 | tf_op jit(solution)/shard_map/ppermute | solution.py:171
  44.0 8.6 %collective-permute-start.16 = (bf16[4,152,128]{2,1,0:T(8,128)(2,1)S(1)}, bf16[4,152,128]{2,1,0:T(8,128)(2,1)S(1)}, u32[]{:S(2)}, u32[]{:S(2)}) collective-permute-start(bf16[4,152,128]{2,1,0:T(8,128)(2,1)S(1)} %get-tuple-element.55), channel_id=1, source_target_pairs={{0,5},{1,4},{2,7},{3,6},{4,1},{5,0},{6,3},{7,2},{8,13},{9,12},{10,... | collective-permute-start | bytes 466952 | tf_op jit(solution)/shard_map/ppermute | solution.py:171
  46.7 14.0 %collective-permute-start.20 = (bf16[4,152,128]{2,1,0:T(8,128)(2,1)S(1)}, bf16[4,152,128]{2,1,0:T(8,128)(2,1)S(1)}, u32[]{:S(2)}, u32[]{:S(2)}) collective-permute-start(bf16[4,152,128]{2,1,0:T(8,128)(2,1)S(1)} %get-tuple-element.59), channel_id=1, source_target_pairs={{0,16},{1,17},{2,18},{3,19},{4,20},{5,21},{6,22},{7,23},{8,24},{9,... | collective-permute-start | bytes 466952 | tf_op jit(solution)/shard_map/ppermute | solution.py:171
  49.4 11.4 %collective-permute-start.21 = (bf16[4,152,128]{2,1,0:T(8,128)(2,1)S(1)}, bf16[4,152,128]{2,1,0:T(8,128)(2,1)S(1)}, u32[]{:S(2)}, u32[]{:S(2)}) collective-permute-start(bf16[4,152,128]{2,1,0:T(8,128)(2,1)S(1)} %get-tuple-element.60), channel_id=1, source_target_pairs={{0,24},{1,25},{2,26},{3,27},{4,28},{5,29},{6,30},{7,31},{8,16},{9,... | collective-permute-start | bytes 466952 | tf_op jit(solution)/shard_map/ppermute | solution.py:171
  51.7 9.2 %collective-permute-start.22 = (bf16[4,152,128]{2,1,0:T(8,128)(2,1)S(1)}, bf16[4,152,128]{2,1,0:T(8,128)(2,1)S(1)}, u32[]{:S(2)}, u32[]{:S(2)}) collective-permute-start(bf16[4,152,128]{2,1,0:T(8,128)(2,1)S(1)} %get-tuple-element.61), channel_id=1, source_target_pairs={{0,8},{1,9},{2,10},{3,11},{4,12},{5,13},{6,14},{7,15},{8,0},{9,1},... | collective-permute-start | bytes 466952 | tf_op jit(solution)/shard_map/ppermute | solution.py:171
  60.9 7.7 %collective-permute-start.23 = (bf16[4,152,128]{2,1,0:T(8,128)(2,1)S(1)}, bf16[4,152,128]{2,1,0:T(8,128)(2,1)S(1)}, u32[]{:S(2)}, u32[]{:S(2)}) collective-permute-start(bf16[4,152,128]{2,1,0:T(8,128)(2,1)S(1)} %get-tuple-element.64), channel_id=1, source_target_pairs={{0,1},{1,0},{2,3},{3,2},{4,5},{5,4},{6,7},{7,6},{8,9},{9,8},{10,11... | collective-permute-start | bytes 466952 | tf_op jit(solution)/shard_map/ppermute | solution.py:171
  61.0 7.9 %collective-permute-start.24 = (bf16[4,152,128]{2,1,0:T(8,128)(2,1)S(1)}, bf16[4,152,128]{2,1,0:T(8,128)(2,1)S(1)}, u32[]{:S(2)}, u32[]{:S(2)}) collective-permute-start(bf16[4,152,128]{2,1,0:T(8,128)(2,1)S(1)} %get-tuple-element.65), channel_id=1, source_target_pairs={{0,6},{1,7},{2,4},{3,5},{4,2},{5,3},{6,0},{7,1},{8,14},{9,15},{10,... | collective-permute-start | bytes 466952 | tf_op jit(solution)/shard_map/ppermute | solution.py:171
  62.8 8.3 %collective-permute-start.25 = (bf16[4,152,128]{2,1,0:T(8,128)(2,1)S(1)}, bf16[4,152,128]{2,1,0:T(8,128)(2,1)S(1)}, u32[]{:S(2)}, u32[]{:S(2)}) collective-permute-start(bf16[4,152,128]{2,1,0:T(8,128)(2,1)S(1)} %get-tuple-element.66), channel_id=1, source_target_pairs={{0,7},{1,6},{2,5},{3,4},{4,3},{5,2},{6,1},{7,0},{8,15},{9,14},{10,... | collective-permute-start | bytes 466952 | tf_op jit(solution)/shard_map/ppermute | solution.py:171
  63.8 15.0 %collective-permute-start.17 = (bf16[4,152,128]{2,1,0:T(8,128)(2,1)S(1)}, bf16[4,152,128]{2,1,0:T(8,128)(2,1)S(1)}, u32[]{:S(2)}, u32[]{:S(2)}) collective-permute-start(bf16[4,152,128]{2,1,0:T(8,128)(2,1)S(1)} %get-tuple-element.56), channel_id=1, source_target_pairs={{0,16},{1,17},{2,18},{3,19},{4,20},{5,21},{6,22},{7,23},{8,24},{9,... | collective-permute-start | bytes 466952 | tf_op jit(solution)/shard_map/ppermute | solution.py:171
  67.2 11.6 %collective-permute-start.18 = (bf16[4,152,128]{2,1,0:T(8,128)(2,1)S(1)}, bf16[4,152,128]{2,1,0:T(8,128)(2,1)S(1)}, u32[]{:S(2)}, u32[]{:S(2)}) collective-permute-start(bf16[4,152,128]{2,1,0:T(8,128)(2,1)S(1)} %get-tuple-element.57), channel_id=1, source_target_pairs={{0,24},{1,25},{2,26},{3,27},{4,28},{5,29},{6,30},{7,31},{8,16},{9,... | collective-permute-start | bytes 466952 | tf_op jit(solution)/shard_map/ppermute | solution.py:171
  68.7 11.1 %collective-permute-start.19 = (bf16[4,152,128]{2,1,0:T(8,128)(2,1)S(1)}, bf16[4,152,128]{2,1,0:T(8,128)(2,1)S(1)}, u32[]{:S(2)}, u32[]{:S(2)}) collective-permute-start(bf16[4,152,128]{2,1,0:T(8,128)(2,1)S(1)} %get-tuple-element.58), channel_id=1, source_target_pairs={{0,8},{1,9},{2,10},{3,11},{4,12},{5,13},{6,14},{7,15},{8,0},{9,1},... | collective-permute-start | bytes 466952 | tf_op jit(solution)/shard_map/ppermute | solution.py:171
